TPU v7x, 32 devices: a whole 2x2x4 slice. The times are simulated.
32 devices in a mesh: dp: 8 (over z, y), tensor: 4 (over x, core).
Axes of the slice: x: 2, y: 2, z: 4, core: 2. Of those that a mesh axis runs over, the one named last changes fastest.
Arguments:
- tokens: bfloat16 [16384, 1536], P(('dp', 'tensor')), may hold values from -6 to 6
- segments: int32 [16384], P('dp'), may hold values from 0 to 3, as said below
- positions: int32 [16384], P('dp'), may hold values from 0 to 2044, as said below
- norm_attn: float32 [1536], replicated, may hold values from 0.1 to 1.9
- w_query: bfloat16 [1536, 1536], P(None, 'tensor'), may hold values from -0.15625 to 0.15625
- key_weight: bfloat16 [1536, 768], P(None, 'tensor'), may hold values from -0.15625 to 0.15625
- value_weight: bfloat16 [1536, 768], P(None, 'tensor'), may hold values from -0.15625 to 0.15625
- w_out: bfloat16 [1536, 1536], P('tensor'), may hold values from -1.5 to 1.5
- norm_mlp: float32 [1536], replicated, may hold values from 0.1 to 1.9
- w_gate: bfloat16 [1536, 4096], P(None, 'tensor'), may hold values from -0.15625 to 0.15625
- w_up: bfloat16 [1536, 4096], P(None, 'tensor'), may hold values from -0.15625 to 0.15625
- w_down: bfloat16 [4096, 1536], P('tensor'), may hold values from -0.09375 to 0.09375
- cotangent: bfloat16 [16384, 1536], P(('dp', 'tensor')), may hold values from -6 to 6
Outputs:
- output: bfloat16 [16384, 1536], P(('dp', 'tensor'))
- grad_tokens: float32 [16384, 1536], P(('dp', 'tensor'))
- grad_norm_attn: float32 [1536], replicated
- grad_w_query: float32 [1536, 1536], P(None, 'tensor')
- grad_w_key: float32 [1536, 768], P(None, 'tensor')
- grad_w_value: float32 [1536, 768], P(None, 'tensor')
- grad_w_out: float32 [1536, 1536], P('tensor')
- grad_norm_mlp: float32 [1536], replicated
- grad_w_gate: float32 [1536, 4096], P(None, 'tensor')
- grad_w_up: float32 [1536, 4096], P(None, 'tensor')
- grad_w_down: float32 [4096, 1536], P('tensor')
Inputs may be any that keep to these rules, and one draw needn't show every extreme that they name: `segments`: within each sequence of 2048 tokens the document numbers never fall, start at 0 and end at 3, each document one token or more. `positions`: each token's position within its document, 0 at the document's first token; the first sequence holds a document of 2045 tokens.
All inputs are finite; a program needn't handle non-finite values.
Results may differ from a plain program's by a relative error of at most 0.018.
Values may be sent and summed in bfloat16 or wider, within the bound.
A program may use at most 256 MiB of HBM per device.

v0:
```python
import math

import jax
import jax.numpy as jnp
from jax import lax
from jax.sharding import PartitionSpec as P

HEAD_SIZE = 96


epsilon = 1e-05
rope_base = 100000.0
masked_value = -1e30


def angle_tables(positions, width):
    middle = width // 2
    freq_steps = jnp.arange(middle, dtype=jnp.float32)
    inverse = jnp.exp(freq_steps * (-2.0 * math.log(rope_base) / width))
    angles = positions.astype(jnp.float32)[:, None] * inverse[None, :]
    return (jnp.cos(angles)[:, None, :], jnp.sin(angles)[:, None, :])


def apply_rotary(values, cosine_lookup, sine_lookup):
    middle = values.shape[-1] // 2
    front, second = (values[..., :middle], values[..., middle:])
    return jnp.concatenate(
        [
            front * cosine_lookup - second * sine_lookup,
            second * cosine_lookup + front * sine_lookup,
        ],
        axis=-1,
    )


def rotate_back(grads_in, cosine_lookup, sine_lookup):
    middle = grads_in.shape[-1] // 2
    front, second = (grads_in[..., :middle], grads_in[..., middle:])
    return jnp.concatenate(
        [
            front * cosine_lookup + second * sine_lookup,
            second * cosine_lookup - front * sine_lookup,
        ],
        axis=-1,
    )


def rms_inverse(values):
    return lax.rsqrt(jnp.mean(values * values, axis=-1, keepdims=True) + epsilon)


def norm_back(grad_normed, gain, unit_rows, inverse):
    scaled = grad_normed * gain
    return inverse * (scaled - unit_rows * jnp.mean(scaled * unit_rows, axis=-1, keepdims=True))


def contract_rows(left, right):
    return lax.dot_general(
        left, right, (((0,), (0,)), ((), ())), preferred_element_type=jnp.float32
    )


def contract_cols(left, right):
    return lax.dot_general(
        left, right, (((1,), (1,)), ((), ())), preferred_element_type=jnp.float32
    )


def block_scores(query_block, heads_of_key, allowed, score_scale):
    scores = (
        jnp.einsum("qgrd,kgd->grqk", query_block, heads_of_key, preferred_element_type=jnp.float32)
        * score_scale
    )
    return jnp.where(allowed[None, None], scores, masked_value)


def body(
    tokens,
    segments,
    positions,
    norm_attn,
    w_query,
    key_weight,
    value_weight,
    w_out,
    norm_mlp,
    w_gate,
    w_up,
    w_down,
    cotangent,
):
    sequence_length = segments.shape[0]
    q_heads = w_query.shape[1] // HEAD_SIZE
    kv_heads = key_weight.shape[1] // HEAD_SIZE
    head_repetitions = q_heads // kv_heads
    score_scale = 1.0 / math.sqrt(HEAD_SIZE)
    rows_per_block = min(512, sequence_length)
    block_total = sequence_length // rows_per_block
    cosine_lookup, sine_lookup = angle_tables(positions, HEAD_SIZE)
    indices = jnp.arange(sequence_length, dtype=jnp.int32)
    seg_blocks = segments.reshape(block_total, rows_per_block)
    index_blocks = indices.reshape(block_total, rows_per_block)
    inputs = tokens.astype(jnp.float32)
    inverse_one = rms_inverse(inputs)
    unit_one = inputs * inverse_one
    first_normalized = (unit_one * norm_attn).astype(jnp.bfloat16)
    attn_in = lax.all_gather(first_normalized, "tensor", axis=0, tiled=True)
    query_proj = jnp.dot(attn_in, w_query, preferred_element_type=jnp.float32).reshape(
        sequence_length, q_heads, HEAD_SIZE
    )
    key_proj = jnp.dot(attn_in, key_weight, preferred_element_type=jnp.float32).reshape(
        sequence_length, kv_heads, HEAD_SIZE
    )
    query_rows = apply_rotary(query_proj, cosine_lookup, sine_lookup).astype(jnp.bfloat16)
    heads_of_key = apply_rotary(key_proj, cosine_lookup, sine_lookup).astype(jnp.bfloat16)
    heads_of_value = (
        jnp.dot(attn_in, value_weight, preferred_element_type=jnp.float32)
        .astype(jnp.bfloat16)
        .reshape(sequence_length, kv_heads, HEAD_SIZE)
    )
    blocks_of_query = query_rows.reshape(
        block_total, rows_per_block, kv_heads, head_repetitions, HEAD_SIZE
    )

    def attend(member):
        query_block, rows_seg, rows_idx = member
        allowed = (rows_seg[:, None] == segments[None, :]) & (indices[None, :] <= rows_idx[:, None])
        scores = block_scores(query_block, heads_of_key, allowed, score_scale)
        row_peak = jnp.max(scores, axis=-1, keepdims=True)
        weights = jnp.exp(scores - row_peak)
        totals = jnp.sum(weights, axis=-1, keepdims=True)
        weights_low = (weights / totals).astype(jnp.bfloat16)
        mixed_heads = jnp.einsum(
            "grqk,kgd->qgrd", weights_low, heads_of_value, preferred_element_type=jnp.float32
        )
        return (mixed_heads.astype(jnp.bfloat16), row_peak[..., 0] + jnp.log(totals[..., 0]))

    attended, log_totals = lax.map(attend, (blocks_of_query, seg_blocks, index_blocks))
    attended = attended.reshape(sequence_length, q_heads * HEAD_SIZE)
    row_slice = attended
    attn_out = lax.psum_scatter(
        jnp.dot(row_slice, w_out, preferred_element_type=jnp.float32),
        "tensor",
        scatter_dimension=0,
        tiled=True,
    )
    hidden_one = inputs + attn_out
    inverse_two = rms_inverse(hidden_one)
    unit_two = hidden_one * inverse_two
    normed_two = (unit_two * norm_mlp).astype(jnp.bfloat16)
    mlp_in = lax.all_gather(normed_two, "tensor", axis=0, tiled=True)
    gate_proj = jnp.dot(mlp_in, w_gate, preferred_element_type=jnp.float32)
    up_proj = jnp.dot(mlp_in, w_up, preferred_element_type=jnp.float32)
    sigmoid_gate = jax.nn.sigmoid(gate_proj)
    activated = gate_proj * sigmoid_gate
    hidden = (activated * up_proj).astype(jnp.bfloat16)
    row_slice = hidden
    mlp_out = lax.psum_scatter(
        jnp.dot(row_slice, w_down, preferred_element_type=jnp.float32).astype(jnp.bfloat16),
        "tensor",
        scatter_dimension=0,
        tiled=True,
    ).astype(jnp.float32)
    output = (hidden_one + mlp_out).astype(jnp.bfloat16)
    grad_out = lax.all_gather(cotangent, "tensor", axis=0, tiled=True)
    grad_w_down = contract_rows(hidden, grad_out)
    grad_hidden = contract_cols(grad_out, w_down)
    grad_gate = (
        grad_hidden * up_proj * sigmoid_gate * (1.0 + gate_proj * (1.0 - sigmoid_gate))
    ).astype(jnp.bfloat16)
    grad_upper = (grad_hidden * activated).astype(jnp.bfloat16)
    grad_w_gate = contract_rows(mlp_in, grad_gate)
    grad_w_up = contract_rows(mlp_in, grad_upper)
    grad_normed_two = lax.psum_scatter(
        contract_cols(grad_gate, w_gate) + contract_cols(grad_upper, w_up),
        "tensor",
        scatter_dimension=0,
        tiled=True,
    )
    grad_norm_mlp = jnp.sum(grad_normed_two * unit_two, axis=0)
    grad_hidden_one = cotangent.astype(jnp.float32) + norm_back(
        grad_normed_two, norm_mlp, unit_two, inverse_two
    )
    grad_attn_rows = lax.all_gather(
        grad_hidden_one.astype(jnp.bfloat16), "tensor", axis=0, tiled=True
    )
    grad_w_out = contract_rows(attended, grad_attn_rows)
    grad_attended = contract_cols(grad_attn_rows, w_out).astype(jnp.bfloat16)
    grad_blocks = grad_attended.reshape(
        block_total, rows_per_block, kv_heads, head_repetitions, HEAD_SIZE
    )

    def attend_back(running, member):
        query_block, grad_block, rows_seg, rows_idx, log_block = member
        allowed = (rows_seg[:, None] == segments[None, :]) & (indices[None, :] <= rows_idx[:, None])
        scores = block_scores(query_block, heads_of_key, allowed, score_scale)
        weights = jnp.exp(scores - log_block[..., None])
        grad_weights = jnp.einsum(
            "qgrd,kgd->grqk", grad_block, heads_of_value, preferred_element_type=jnp.float32
        )
        inner_sum = jnp.sum(weights * grad_weights, axis=-1, keepdims=True)
        grad_scores = (weights * (grad_weights - inner_sum)).astype(jnp.bfloat16)
        grad_query = (
            jnp.einsum(
                "grqk,kgd->qgrd", grad_scores, heads_of_key, preferred_element_type=jnp.float32
            )
            * score_scale
        )
        grad_keys = (
            running[0]
            + jnp.einsum(
                "grqk,qgrd->kgd", grad_scores, query_block, preferred_element_type=jnp.float32
            )
            * score_scale
        )
        grad_values = running[1] + jnp.einsum(
            "grqk,qgrd->kgd",
            weights.astype(jnp.bfloat16),
            grad_block,
            preferred_element_type=jnp.float32,
        )
        return ((grad_keys, grad_values), grad_query)

    zero_state = jnp.zeros((sequence_length, kv_heads, HEAD_SIZE), jnp.float32)
    (grad_keys, grad_values), grad_queries = lax.scan(
        attend_back,
        (zero_state, zero_state),
        (blocks_of_query, grad_blocks, seg_blocks, index_blocks, log_totals),
    )
    grad_queries = grad_queries.reshape(sequence_length, q_heads, HEAD_SIZE)
    grad_q_proj = (
        rotate_back(grad_queries, cosine_lookup, sine_lookup)
        .reshape(sequence_length, q_heads * HEAD_SIZE)
        .astype(jnp.bfloat16)
    )
    grad_k_proj = (
        rotate_back(grad_keys, cosine_lookup, sine_lookup)
        .reshape(sequence_length, kv_heads * HEAD_SIZE)
        .astype(jnp.bfloat16)
    )
    grad_v_proj = grad_values.reshape(sequence_length, kv_heads * HEAD_SIZE).astype(jnp.bfloat16)
    grad_w_query = contract_rows(attn_in, grad_q_proj)
    grad_w_key = contract_rows(attn_in, grad_k_proj)
    grad_w_value = contract_rows(attn_in, grad_v_proj)
    grad_normed_one = lax.psum_scatter(
        (
            contract_cols(grad_q_proj, w_query)
            + contract_cols(grad_k_proj, key_weight)
            + contract_cols(grad_v_proj, value_weight)
        ).astype(jnp.bfloat16),
        "tensor",
        scatter_dimension=0,
        tiled=True,
    ).astype(jnp.float32)
    grad_norm_attn = jnp.sum(grad_normed_one * unit_one, axis=0)
    grad_tokens = grad_hidden_one + norm_back(grad_normed_one, norm_attn, unit_one, inverse_one)
    grad_norm_attn, grad_norm_mlp = lax.psum((grad_norm_attn, grad_norm_mlp), ("dp", "tensor"))
    grad_w_query, grad_w_key, grad_w_value, grad_w_out, grad_w_gate, grad_w_up, grad_w_down = (
        lax.psum(grad_w_query.astype(jnp.bfloat16), "dp").astype(jnp.float32),
        lax.psum(grad_w_key.astype(jnp.bfloat16), "dp").astype(jnp.float32),
        lax.psum(grad_w_value.astype(jnp.bfloat16), "dp").astype(jnp.float32),
        lax.psum(grad_w_out.astype(jnp.bfloat16), "dp").astype(jnp.float32),
        lax.psum(grad_w_gate.astype(jnp.bfloat16), "dp").astype(jnp.float32),
        lax.psum(grad_w_up.astype(jnp.bfloat16), "dp").astype(jnp.float32),
        lax.psum(grad_w_down.astype(jnp.bfloat16), "dp").astype(jnp.float32),
    )
    return (
        output,
        grad_tokens,
        grad_norm_attn,
        grad_w_query,
        grad_w_key,
        grad_w_value,
        grad_w_out,
        grad_norm_mlp,
        grad_w_gate,
        grad_w_up,
        grad_w_down,
    )


def solution(mesh):
    in_specs = (
        P(("dp", "tensor"), None),
        P("dp"),
        P("dp"),
        P(),
        P(None, "tensor"),
        P(None, "tensor"),
        P(None, "tensor"),
        P("tensor", None),
        P(),
        P(None, "tensor"),
        P(None, "tensor"),
        P("tensor", None),
        P(("dp", "tensor"), None),
    )
    out_specs = (
        P(("dp", "tensor"), None),
        P(("dp", "tensor"), None),
        P(),
        P(None, "tensor"),
        P(None, "tensor"),
        P(None, "tensor"),
        P("tensor", None),
        P(),
        P(None, "tensor"),
        P(None, "tensor"),
        P("tensor", None),
    )
    return jax.shard_map(body, mesh=mesh, in_specs=in_specs, out_specs=out_specs, check_vma=False)
```

profile of v0, /device:TPU:24, one launch (start us, length us, event | category | flops | bytes accessed | tf_op | source)
XLA Modules:
  0.0 1457.8 jit_solution(5925052065785356915)
XLA Ops:
  15.7 44.6 %all-gather.5.cloned.1.call-done = bf16[2048,1536]{1,0:T(8,128)(2,1)} async-done(((bf16[512,1536]{1,0:T(8,128)(2,1)}), bf16[2048,1536]{1,0:T(8,128)(2,1)}) %all-gather.5.cloned.1.call-update) | async-done | bytes 6291472 | tf_op jit(solution)/shard_map/all_gather | solution.py:107
  88.1 66.6 %while.28 = (s32[]{:T(128)}, bf16[4,512,2,2,96]{1,4,3,2,0:T(8,128)(2,1)}, f32[4,2,2,512]{3,2,1,0:T(2,128)}, s32[4,512]{1,0:T(4,128)S(1)}, s32[2048]{0:T(1024)S(1...) while((s32[]{:T(128)}, ...), condition=%wide.region_4.5_spmd.clone, body=%wide.region_1.4_spmd.clone.sunk | while | flops 1664284672 | bytes 60117144 | solution.py:138
  165.5 99.1 %reduce-scatter.5.cloned.1.call-done = f32[512,1536]{1,0:T(8,128)} async-done(((f32[2048,1536]{1,0:T(8,128)}), f32[512,1536]{1,0:T(8,128)}) %reduce-scatter.5.cloned.1.call-update) | async-done | bytes 3145744 | tf_op jit(solution)/shard_map/reduce_scatter | solution.py:141
  271.3 45.9 %all-gather.7.cloned.1.call-done = bf16[2048,1536]{1,0:T(8,128)(2,1)} async-done(((bf16[512,1536]{1,0:T(8,128)(2,1)}), bf16[2048,1536]{1,0:T(8,128)(2,1)}) %all-gather.7.cloned.1.call-update) | async-done | bytes 6291472 | tf_op jit(solution)/shard_map/all_gather | solution.py:151
  317.2 12.6 fusion.74
  338.7 26.4 %all-gather.9.cloned.1.call-done = bf16[2048,1536]{1,0:T(8,128)(2,1)} async-done(((bf16[512,1536]{1,0:T(8,128)(2,1)}), bf16[2048,1536]{1,0:T(8,128)(2,1)}) %all-gather.9.cloned.1.call-update) | async-done | bytes 6291472 | tf_op jit(solution)/shard_map/all_gather | solution.py:165
  365.0 18.8 %multiply_convert_fusion = (bf16[2048,1024]{1,0:T(8,128)(2,1)}, bf16[2048,1024]{1,0:T(8,128)(2,1)}, bf16[2048,1024]{1,0:T(8,128)(2,1)}) fusion(f32[2048,1024]{1,0:T(8,128)} %fusion.73, f32[2048,1024]{1,0:T(8,128)} %fusion.74, bf16[2048,1536]{1,0:T(8,128)(2,1)} %all-gather.9.cloned.1.call-done, bf16[1024,1536]{1,0:T(8,128)(2,1)S(1)} %copy-done), kind=kOutput, calls=%fused_computation.69 | convolution fusion | flops 6473908224 | bytes 38797312 | tf_op jit(solution)/shard_map/dot_general | solution.py:64
  395.5 12.9 convolution_add_fusion
  408.4 99.1 %reduce-scatter.9.cloned.1.call-done = f32[512,1536]{1,0:T(8,128)} async-done(((f32[2048,1536]{1,0:T(8,128)}), f32[512,1536]{1,0:T(8,128)}) %reduce-scatter.9.cloned.1.call-update) | async-done | bytes 3145744 | tf_op jit(solution)/shard_map/reduce_scatter | solution.py:174
  515.9 46.5 %all-gather.11.cloned.1.call-done = bf16[2048,1536]{1,0:T(8,128)(2,1)} async-done(((bf16[512,1536]{1,0:T(8,128)(2,1)}), bf16[2048,1536]{1,0:T(8,128)(2,1)}) %all-gather.11.cloned.1.call-update) | async-done | bytes 6291472 | tf_op jit(solution)/shard_map/all_gather | solution.py:184
  583.0 274.0 %while.29 = (s32[]{:T(128)}, f32[2048,2,96]{0,2,1:T(8,128)}, f32[2048,2,96]{0,2,1:T(8,128)}, f32[4,512,2,2,96]{1,0,4,3,2:T(4,128)}, bf16[4,512,2,2,96]{1,4,3,2,0...) while((s32[]{:T(128)}, f32[2048,2,96]{0,2,1:T(8,128)}, ...), condition=%wide.region_12.13_spmd.clone, body=%wide.region_10.12_spmd.clone.sunk | while | flops 4094752768 | bytes 214511840 | solution.py:225
  601.9 12.6 fusion.155
  614.5 12.2 fusion.156
  634.9 16.1 %dynamic_update_slice.22 = f32[4,512,2,2,96]{1,0,4,3,2:T(4,128)} dynamic-update-slice(f32[4,512,2,2,96]{1,0,4,3,2:T(4,128)} %get-tuple-element.503, f32[1,512,2,2,96]{1,0,4,3,2:T(1,128)} %copy.49, s32[]{:T(128)S(6)} %copy.66, s32[]{:T(128)} %constant.58.clone.1..sunk, s32[]{:T(128)} %constant.58.clone.1..sunk, s32[]{:T(128)} %constant.58.clone.1..sunk, s32[]{:T(128)} %constant.58.clone.1..sunk) | dynamic-update-slice | bytes 1572868 | tf_op jit(solution)/shard_map/while/body/jit(dynamic_update_index_in_dim)/dynamic_update_slice | solution.py:225
  670.0 12.6 fusion.155
  703.5 16.1 %dynamic_update_slice.22 = f32[4,512,2,2,96]{1,0,4,3,2:T(4,128)} dynamic-update-slice(f32[4,512,2,2,96]{1,0,4,3,2:T(4,128)} %get-tuple-element.503, f32[1,512,2,2,96]{1,0,4,3,2:T(1,128)} %copy.49, s32[]{:T(128)S(6)} %copy.66, s32[]{:T(128)} %constant.58.clone.1..sunk, s32[]{:T(128)} %constant.58.clone.1..sunk, s32[]{:T(128)} %constant.58.clone.1..sunk, s32[]{:T(128)} %constant.58.clone.1..sunk) | dynamic-update-slice | bytes 1572868 | tf_op jit(solution)/shard_map/while/body/jit(dynamic_update_index_in_dim)/dynamic_update_slice | solution.py:225
  738.6 12.6 fusion.155
  772.1 16.1 %dynamic_update_slice.22 = f32[4,512,2,2,96]{1,0,4,3,2:T(4,128)} dynamic-update-slice(f32[4,512,2,2,96]{1,0,4,3,2:T(4,128)} %get-tuple-element.503, f32[1,512,2,2,96]{1,0,4,3,2:T(1,128)} %copy.49, s32[]{:T(128)S(6)} %copy.66, s32[]{:T(128)} %constant.58.clone.1..sunk, s32[]{:T(128)} %constant.58.clone.1..sunk, s32[]{:T(128)} %constant.58.clone.1..sunk, s32[]{:T(128)} %constant.58.clone.1..sunk) | dynamic-update-slice | bytes 1572868 | tf_op jit(solution)/shard_map/while/body/jit(dynamic_update_index_in_dim)/dynamic_update_slice | solution.py:225
  807.2 12.6 fusion.155
  840.8 16.1 %dynamic_update_slice.22 = f32[4,512,2,2,96]{1,0,4,3,2:T(4,128)} dynamic-update-slice(f32[4,512,2,2,96]{1,0,4,3,2:T(4,128)} %get-tuple-element.503, f32[1,512,2,2,96]{1,0,4,3,2:T(1,128)} %copy.49, s32[]{:T(128)S(6)} %copy.66, s32[]{:T(128)} %constant.58.clone.1..sunk, s32[]{:T(128)} %constant.58.clone.1..sunk, s32[]{:T(128)} %constant.58.clone.1..sunk, s32[]{:T(128)} %constant.58.clone.1..sunk) | dynamic-update-slice | bytes 1572868 | tf_op jit(solution)/shard_map/while/body/jit(dynamic_update_index_in_dim)/dynamic_update_slice | solution.py:225
  881.3 12.8 add_convert_fusion
  955.6 39.0 %all-reduce = (f32[1536]{0:T(1024)}, f32[1536]{0:T(1024)}) all-reduce(f32[1536]{0:T(1024)S(1)} %get-tuple-element.234, f32[1536]{0:T(1024)S(1)} %copy-done.41), channel_id=1, replica_groups=mesh['dp'=8,'tensor'=4] {'dp','tensor'}, use_global_device_ids=true, to_apply=%region_16.17 | all-reduce | flops 3072 | bytes 24576 | tf_op jit(solution)/shard_map/psum | solution.py:257
  994.6 20.4 %reduce-scatter.7.cloned.1.call-done = bf16[512,1536]{1,0:T(8,128)(2,1)} async-done(((bf16[2048,1536]{1,0:T(8,128)(2,1)}), bf16[512,1536]{1,0:T(8,128)(2,1)}) %reduce-scatter.7.cloned.1.call-update) | async-done | bytes 1572880 | tf_op jit(solution)/shard_map/reduce_scatter | solution.py:158
  1022.0 411.3 %all-reduce.4.cloned.1.call-done = (bf16[1536,384]{1,0:T(8,128)(2,1)}, bf16[1536,192]{0,1:T(8,128)(2,1)}, bf16[1536,192]{0,1:T(8,128)(2,1)}, bf16[384,1536]{1,0:...) async-done(((bf16[1536,384]{1,0:T(8,128)(2,1)}, bf16[1536,192]{0,1:T(8,128)(2,1)}, bf16[1536,192]{0,1:T(8,128)(2,1)}, ...) | async-done | bytes 12976144 | tf_op jit(solution)/shard_map/psum | solution.py:259
  (284 shorter events, 425.3 us)
Async XLA Ops:
  7.2 357.9 %copy-start = (bf16[1024,1536]{1,0:T(8,128)(2,1)S(1)}, bf16[1024,1536]{1,0:T(8,128)(2,1)}, u32[]{:S(2)}) copy-start(bf16[1024,1536]{1,0:T(8,128)(2,1)} %param.28) | copy-start | bytes 9437188
  7.2 53.1 %all-gather.5.cloned.1.call-start = ((), (), s32[]{:S(2)}) async-start(), calls=%async_computation.4 | async-start | bytes 7864320 | tf_op jit(solution)/shard_map/all_gather | solution.py:107
  12.8 251.9 %reduce-scatter.5.cloned.1.call-start = ((), (), s32[]{:S(2)}) async-start(), calls=%async_computation.5 | async-start | bytes 15728640 | tf_op jit(solution)/shard_map/reduce_scatter | solution.py:141
  15.7 54.0 %copy-start.7 = (f32[2048,48]{0,1:T(8,128)}, f32[2048,48]{0,1:T(8,128)S(1)}, u32[]{:S(2)}) copy-start(f32[2048,48]{0,1:T(8,128)S(1)} %get-tuple-element.310) | copy-start | bytes 1179652
  165.5 103.7 %copy-start.35 = (f32[1536]{0:T(1024)S(1)}, f32[1536]{0:T(1024)}, u32[]{:S(2)}) copy-start(f32[1536]{0:T(1024)} %param.25) | copy-start | bytes 18436
  165.5 151.7 %all-gather.7.cloned.1.call-start = ((), (), s32[]{:S(2)}) async-start(), calls=%async_computation.6 | async-start | bytes 7864320 | tf_op jit(solution)/shard_map/all_gather | solution.py:151
  267.5 244.4 %copy-start.39 = (f32[512]{0:T(512)}, f32[512]{0:T(512)S(1)}, u32[]{:S(2)}) copy-start(f32[512]{0:T(512)S(1)} %add_rsqrt_fusion) | copy-start | bytes 6148
  270.7 94.4 %all-gather.9.cloned.1.call-start = ((), (), s32[]{:S(2)}) async-start(), calls=%async_computation.8 | async-start | bytes 7864320 | tf_op jit(solution)/shard_map/all_gather | solution.py:165
  271.2 236.3 %reduce-scatter.9.cloned.1.call-start = ((), (), s32[]{:S(2)}) async-start(), calls=%async_computation.9 | async-start | bytes 15728640 | tf_op jit(solution)/shard_map/reduce_scatter | solution.py:174
  317.2 12.6 copy-start.48
  317.2 12.6 copy-start.49
  365.0 18.8 %copy-start.50 = (bf16[1536,1024]{1,0:T(8,128)(2,1)S(1)}, bf16[1536,1024]{1,0:T(8,128)(2,1)}, u32[]{:S(2)}) copy-start(bf16[1536,1024]{1,0:T(8,128)(2,1)} %param.26) | copy-start | bytes 9437188
  408.4 154.0 %all-gather.11.cloned.1.call-start = ((), (), s32[]{:S(2)}) async-start(), calls=%async_computation.10 | async-start | bytes 7864320 | tf_op jit(solution)/shard_map/all_gather | solution.py:184
  515.8 436.8 %reduce-scatter.11.cloned.1.call-start = ((), (), s32[]{:S(2)}) async-start(), calls=%async_computation.11 | async-start | bytes 7864320 | tf_op jit(solution)/shard_map/reduce_scatter | solution.py:245
  614.5 12.2 copy-start.2
  682.6 12.2 copy-start.2
  866.7 14.7 %copy-start.20 = (bf16[2048,2,96]{0,2,1:T(8,128)(2,1)}, bf16[2048,2,96]{0,2,1:T(8,128)(2,1)S(1)}, u32[]{:S(2)}) copy-start(bf16[2048,2,96]{0,2,1:T(8,128)(2,1)S(1)} %convert_element_type.138) | copy-start | bytes 2359300
  894.1 120.9 %reduce-scatter.7.cloned.1.call-start = ((), (), s32[]{:S(2)}) async-start(), calls=%async_computation.7 | async-start | bytes 7864320 | tf_op jit(solution)/shard_map/reduce_scatter | solution.py:158
  905.2 528.1 %all-reduce.4.cloned.1.call-start = ((), (), s32[]{:S(2)}) async-start(), calls=%async_computation.12 | async-start | bytes 25952256 | tf_op jit(solution)/shard_map/psum | solution.py:259
  905.2 22.2 %slice-start.2 = ((s8[6291456]{0:T(1024)(128)(4,1)}), s8[4194304]{0:T(1024)(128)(4,1)S(1)}, s32[]{:S(2)}) async-start(s8[6291456]{0:T(1024)(128)(4,1)} %bitcast.262), calls=%async_computation.15 | async-start | bytes 8388608
  917.3 18.7 %slice-start = ((s8[6291456]{0:T(1024)(128)(4,1)}), s8[4194304]{0:T(1024)(128)(4,1)S(1)}, s32[]{:S(2)}) async-start(s8[6291456]{0:T(1024)(128)(4,1)} %bitcast.260), calls=%async_computation.13 | async-start | bytes 8388608
  948.8 66.2 %copy-start.36 = (f32[1536]{0:T(1024)S(1)}, f32[1536]{0:T(1024)}, u32[]{:S(2)}) copy-start(f32[1536]{0:T(1024)} %param.25) | copy-start | bytes 18436
  948.8 66.2 %copy-start.40 = (f32[512]{0:T(512)S(1)}, f32[512]{0:T(512)}, u32[]{:S(2)}) copy-start(f32[512]{0:T(512)} %copy-done.39) | copy-start | bytes 6148
  948.8 66.2 %copy-start.45 = (f32[512]{0:T(512)S(1)}, f32[512]{0:T(512)}, u32[]{:S(2)}) copy-start(f32[512]{0:T(512)} %copy-done.44) | copy-start | bytes 6148
  (55 other events, 293.0 us)
Sparse Core Ops, SparseCore 0:
  12.9 47.3 all-gather.4
  165.6 99.0 reduce-scatter.4
  270.8 46.3 all-gather.6
  318.6 46.3 all-gather.8
  408.5 99.0 reduce-scatter.8
  515.9 46.3 all-gather.10
  894.2 58.3 reduce-scatter.10
  955.9 59.0 reduce-scatter.6
  1021.8 411.3 all-reduce.3
where the time goes:
time: 1470 us; the launch traced here: 1460 us
  waiting for transfers between devices  798 us (54%)
  matrix products  337 us (23%)
  other arithmetic  136 us (9%)
  local copies, waits for them, and re-layouts  132 us (9%)
  blocking collectives  39 us (3%)
  between operations  14.9 us (1%)
    psum x1, waiting for transfers between devices, body(): lax.psum(grad_w_query.astype(jnp.bfloat16), 'dp').astype(jnp.float32)  411 us
    reduce_scatter x1, waiting for transfers between devices, body(): lax.psum_scatter(contract_cols(grad_gate, w_gate) + contract_cols(grad_up...  99.1 us
    reduce_scatter x1, waiting for transfers between devices, body(): lax.psum_scatter(jnp.dot(row_slice, w_out, preferred_element_type=jnp.flo...  99.1 us
    dot_general x7, matrix products, contract_cols(): lax.dot_general(left, right, (((1,), (1,)), ((), ())), preferred_element_...  76.6 us
    dynamic_update_slice x8, local copies, waits for them, and re-layouts, body(): lax.scan(attend_back, (zero_state, zero_state), (blocks_of_query, grad_bl...  71.2 us
    dot_general x4, matrix products, attend_back(): jnp.einsum('qgrd,kgd->grqk', grad_block, heads_of_value, preferred_elemen...  50.6 us
    convert_element_type x4, other arithmetic, attend_back(): grad_scores = (weights * (grad_weights - inner_sum)).astype(jnp.bfloat16)  48.7 us
    all_gather x1, waiting for transfers between devices, body(): lax.all_gather(grad_hidden_one.astype(jnp.bfloat16), 'tensor', axis=0, ti...  46.5 us
  transfers between devices with their start and end apart: 9, of which 9 were waited for; matrix products, arithmetic and copies ran while one was open for 6% of the time, Pallas kernels for 0%

commit v1 on v0

v1 whole, which is shorter than its diff:
```python
import functools
import math

import jax
import jax.numpy as jnp
from jax import lax
from jax.experimental import pallas as pl
from jax.experimental.pallas import tpu as pltpu
from jax.sharding import PartitionSpec as P

HEAD_SIZE = 96
HALF = HEAD_SIZE // 2
LANES = 128
epsilon = 1e-05
rope_base = 100000.0
masked_value = -1e30
score_scale = 1.0 / math.sqrt(HEAD_SIZE)
log2_e = math.log2(math.e)
bf16, f32 = jnp.bfloat16, jnp.float32
NN = (((1,), (0,)), ((), ()))
NT = (((1,), (1,)), ((), ()))
TN = (((0,), (0,)), ((), ()))
VMEM_LIMIT = 62 * 1024 * 1024
CHUNKS = 2


def dot(left, right, dims=NN):
    return lax.dot_general(left, right, dims, preferred_element_type=f32)


def params():
    return pltpu.CompilerParams(vmem_limit_bytes=VMEM_LIMIT)


def cost(flops, nbytes):
    return pl.CostEstimate(flops=int(flops), bytes_accessed=int(nbytes), transcendentals=0)


def whole(shape):
    return pl.BlockSpec(shape, lambda *_: (0,) * len(shape), pipeline_mode=pl.Buffered(1))


def swap(values, bits):
    size = lax.axis_size("tensor")
    return lax.ppermute(values, "tensor", [(i, i ^ bits) for i in range(size)])


def gather_four(own):
    side = swap(own, 1)
    across = swap(own, 2)
    return own, side, across, swap(across, 1)


def scatter_sum(part):
    from_side_2 = swap(part[3], 1)
    travelling = (part[2].astype(f32) + from_side_2.astype(f32)).astype(bf16)
    from_across = swap(travelling, 2)
    from_side_0 = swap(part[1], 1)
    return part[0], from_side_0, from_across


def dp_swap(values, bits):
    size = lax.axis_size("dp")
    return lax.ppermute(values, "dp", [(i, i ^ bits) for i in range(size)])


def dp_sum(values):
    size, index = lax.axis_size("dp"), lax.axis_index("dp")
    rows = values.shape[0]
    piece = values
    bit = 1
    while bit < size:
        half = piece.shape[0] // 2
        mine = (index // bit) % 2
        send = lax.dynamic_slice_in_dim(piece, (1 - mine) * half, half, 0)
        keep = lax.dynamic_slice_in_dim(piece, mine * half, half, 0)
        got = dp_swap(send, bit)
        piece = (keep.astype(f32) + got.astype(f32)).astype(bf16)
        bit *= 2
    while bit > 1:
        bit //= 2
        mine = (index // bit) % 2
        got = dp_swap(piece, bit)
        piece = jnp.where(mine == 0, jnp.concatenate([piece, got], 0), jnp.concatenate([got, piece], 0))
    return piece.astype(f32)


def all_sum(values):
    bit = 1
    while bit < lax.axis_size("tensor"):
        values = values + swap(values, bit)
        bit *= 2
    bit = 1
    while bit < lax.axis_size("dp"):
        values = values + dp_swap(values, bit)
        bit *= 2
    return values


def qkv_kernel(count, *refs):
    xs, (wq, wk, wv, cos_ref, sin_ref), rest = refs[:count], refs[count : count + 5], refs[count + 5 :]
    qkv_ref, stack_ref = rest[-2:]
    for k in range(count):

        @pl.when(pl.program_id(0) == k)
        def _():
            x = xs[k][...]
            cos, sin = cos_ref[0, 0], sin_ref[0, 0]
            stack_ref[0, 0] = x
            rows = x.shape[0]
            lane = lax.broadcasted_iota(jnp.int32, (rows, LANES), 1)
            for w, base, turn in ((wq, 0, True), (wk, 4, True), (wv, 6, False)):
                y = dot(x, w[...])
                for h in range(w.shape[1] // LANES):
                    v = y[:, h * LANES : (h + 1) * LANES]
                    if turn:
                        v = v * cos + pltpu.roll(v, LANES // 2, 1) * sin
                    else:
                        v = jnp.where(lane == HALF, 1.0, v)
                    at = (base + h) * LANES
                    qkv_ref[0, 0, :, at : at + LANES] = v.astype(bf16)


def qkv_call(first, piece, pieces, xs, wq, wk, wv, cos, sin, before):
    count = len(xs)
    rows, width = xs[0].shape
    spec = lambda cols: pl.BlockSpec((1, 1, rows, cols), lambda k: (first + k, piece, 0, 0))
    aliased = before is not None
    inputs = [*xs, wq, wk, wv, cos, sin]
    specs = [whole((rows, width))] * count + [whole(w.shape) for w in (wq, wk, wv)] + [spec(LANES)] * 2
    aliases = {}
    if aliased:
        aliases = {len(inputs): 0, len(inputs) + 1: 1}
        inputs += list(before)
        specs += [pl.BlockSpec(memory_space=pl.ANY)] * 2
    return pl.pallas_call(
        functools.partial(qkv_kernel, count),
        grid=(count,),
        in_specs=specs,
        out_specs=[spec(8 * LANES), spec(width)],
        out_shape=[
            jax.ShapeDtypeStruct((4, pieces, rows, 8 * LANES), bf16),
            jax.ShapeDtypeStruct((4, pieces, rows, width), bf16),
        ],
        input_output_aliases=aliases,
        compiler_params=params(),
        cost_estimate=cost(2 * count * rows * width * 8 * LANES, 2 * width * 8 * LANES + count * rows * width * 6),
        name="project_qkv",
    )(*inputs)


def attend_kernel(me_ref, q_ref, k_ref, v_ref, start_ref, o_ref, lse_ref, *, blocks, size):
    me = me_ref[0]
    for i in range(blocks):
        at = pl.multiple_of((i ^ me) * size, size)
        queries = [q_ref[pl.ds(at, size), r * LANES : (r + 1) * LANES] for r in range(2)]
        start = start_ref[:, pl.ds(at, size)]
        state = [None, None]
        for j in [i, *range(i)]:
            key_at = pl.multiple_of((j ^ me) * size, size)
            keys = k_ref[pl.ds(key_at, size), :]
            values = v_ref[pl.ds(key_at, size), :]
            key_rows = lax.broadcasted_iota(jnp.int32, (size, size), 0)
            allowed = key_rows >= start - j * size
            if j == i:
                allowed &= key_rows <= lax.broadcasted_iota(jnp.int32, (size, size), 1)
            for r in range(2):
                scores = jnp.where(allowed, dot(keys, queries[r], NT) * (score_scale * log2_e), masked_value)
                peak = jnp.max(scores, axis=0, keepdims=True)
                if state[r] is not None:
                    peak = jnp.maximum(state[r][0], peak)
                weights = jnp.exp2(scores - peak)
                mixed = dot(values, weights.astype(bf16), TN)
                if state[r] is not None:
                    mixed += state[r][1] * jnp.exp2(state[r][0] - peak)
                state[r] = (peak, mixed)
        for r, (peak, mixed) in enumerate(state):
            total = mixed[HALF : HALF + 1, :]
            o_ref[pl.ds(at, size), r * LANES : (r + 1) * LANES] = (mixed / total).T.astype(bf16)
            lse_ref[0, r : r + 1, pl.ds(at, size)] = peak + jnp.log2(total)


def attend(me, qkv, start, blocks):
    seq = qkv.shape[0]
    flops = 2 * 2 * 4 * LANES * seq * seq
    return pl.pallas_call(
        functools.partial(attend_kernel, blocks=blocks, size=seq // blocks),
        grid_spec=pltpu.PrefetchScalarGridSpec(
            num_scalar_prefetch=1,
            grid=(2,),
            in_specs=[
                pl.BlockSpec((seq, 2 * LANES), lambda g, _: (0, g)),
                pl.BlockSpec((seq, LANES), lambda g, _: (0, 4 + g)),
                pl.BlockSpec((seq, LANES), lambda g, _: (0, 6 + g)),
                pl.BlockSpec((1, seq), lambda g, _: (0, 0)),
            ],
            out_specs=[
                pl.BlockSpec((seq, 2 * LANES), lambda g, _: (0, g)),
                pl.BlockSpec((1, 2, seq), lambda g, _: (g, 0, 0)),
            ],
        ),
        out_shape=[jax.ShapeDtypeStruct((seq, 4 * LANES), bf16), jax.ShapeDtypeStruct((2, 2, seq), f32)],
        compiler_params=params(),
        cost_estimate=cost(flops, 6 * seq * 8 * LANES),
        name="attention",
    )(me, qkv, qkv, qkv, start)


def attend_back_kernel(
    me_ref, q_ref, k_ref, v_ref, o_ref, do_ref, lse_ref, start_ref, cos_ref, sin_ref,
    dq_ref, dk_ref, dv_ref, dq_sum, dk_sum, dv_sum, inner, *, blocks, size,
):
    me = me_ref[0]
    for c in range(blocks):
        rows = slice(c * size, (c + 1) * size)
        for r in range(2):
            cols = slice(r * LANES, (r + 1) * LANES)
            product = do_ref[rows, cols].astype(f32) * o_ref[rows, cols].astype(f32)
            inner[r : r + 1, rows] = jnp.sum(product.T, axis=0, keepdims=True)
    for i in reversed(range(blocks)):
        for j in [i, *range(i)]:
            at = pl.multiple_of((i ^ me) * size, size)
            key_at = pl.multiple_of((j ^ me) * size, size)
            keys = k_ref[pl.ds(key_at, size), :]
            values = v_ref[pl.ds(key_at, size), :]
            start = start_ref[:, pl.ds(at, size)]
            key_rows = lax.broadcasted_iota(jnp.int32, (size, size), 0)
            allowed = key_rows >= start - j * size
            if j == i:
                allowed &= key_rows <= lax.broadcasted_iota(jnp.int32, (size, size), 1)
            dk = dv = None
            for r in range(2):
                cols = slice(r * LANES, (r + 1) * LANES)
                queries = q_ref[pl.ds(at, size), cols]
                grads = do_ref[pl.ds(at, size), cols]
                scores = jnp.where(allowed, dot(keys, queries, NT) * (score_scale * log2_e), masked_value)
                weights = jnp.exp2(scores - lse_ref[0, r : r + 1, pl.ds(at, size)])
                grad_weights = dot(values, grads, NT)
                grad_scores = (weights * (grad_weights - inner[r : r + 1, pl.ds(at, size)])).astype(bf16)
                dv_term = dot(weights.astype(bf16), grads)
                dk_term = dot(grad_scores, queries)
                dv = dv_term if dv is None else dv + dv_term
                dk = dk_term if dk is None else dk + dk_term
                dq = dot(grad_scores, keys, TN)
                if j == i:
                    dq_sum[pl.ds(at, size), cols] = dq
                else:
                    dq_sum[pl.ds(at, size), cols] += dq
            if i == blocks - 1:
                dk_sum[pl.ds(key_at, size), :] = dk
                dv_sum[pl.ds(key_at, size), :] = dv
            else:
                dk_sum[pl.ds(key_at, size), :] += dk
                dv_sum[pl.ds(key_at, size), :] += dv
    for c in range(blocks):
        rows = slice(c * size, (c + 1) * size)
        cos, sin = cos_ref[rows, :], sin_ref[rows, :]

        def back(grads):
            return ((grads * cos - pltpu.roll(grads, LANES // 2, 1) * sin) * score_scale).astype(bf16)

        for r in range(2):
            cols = slice(r * LANES, (r + 1) * LANES)
            dq_ref[rows, cols] = back(dq_sum[rows, cols])
        dk_ref[rows, :] = back(dk_sum[rows, :])
        dv_ref[rows, :] = dv_sum[rows, :].astype(bf16)


def attend_back(me, qkv, attended, grads, lse, start, cos, sin, blocks):
    seq = qkv.shape[0]
    pair = pl.BlockSpec((seq, 2 * LANES), lambda g, _: (0, g))
    single = pl.BlockSpec((seq, LANES), lambda g, _: (0, g))
    table = pl.BlockSpec((seq, LANES), lambda g, _: (0, 0))
    return pl.pallas_call(
        functools.partial(attend_back_kernel, blocks=blocks, size=seq // blocks),
        grid_spec=pltpu.PrefetchScalarGridSpec(
            num_scalar_prefetch=1,
            grid=(2,),
            in_specs=[
                pair,
                pl.BlockSpec((seq, LANES), lambda g, _: (0, 4 + g)),
                pl.BlockSpec((seq, LANES), lambda g, _: (0, 6 + g)),
                pair,
                pair,
                pl.BlockSpec((1, 2, seq), lambda g, _: (g, 0, 0)),
                pl.BlockSpec((1, seq), lambda g, _: (0, 0)),
                table,
                table,
            ],
            out_specs=[pair, single, single],
            scratch_shapes=[
                pltpu.VMEM((seq, 2 * LANES), f32),
                pltpu.VMEM((seq, LANES), f32),
                pltpu.VMEM((seq, LANES), f32),
                pltpu.VMEM((2, seq), f32),
            ],
        ),
        out_shape=[
            jax.ShapeDtypeStruct((seq, 4 * LANES), bf16),
            jax.ShapeDtypeStruct((seq, 2 * LANES), bf16),
            jax.ShapeDtypeStruct((seq, 2 * LANES), bf16),
        ],
        compiler_params=params(),
        cost_estimate=cost(5 * 2 * 4 * LANES * seq * seq, 10 * seq * 8 * LANES),
        name="attention_back",
    )(me, qkv, qkv, qkv, attended, grads, lse, start, cos, sin)


def out_kernel(att_ref, w_ref, *outs):
    p = pl.program_id(0)
    for k in range(4):

        @pl.when(p == k)
        def _():
            outs[3 - k][...] = dot(att_ref[0, 0], w_ref[...]).astype(bf16)


def out_projection(attended, w_out, piece):
    _, pieces, rows, depth = attended.shape
    width = w_out.shape[1]
    out = jax.ShapeDtypeStruct((rows, width), bf16)
    terms = pl.pallas_call(
        out_kernel,
        grid=(4,),
        in_specs=[pl.BlockSpec((1, 1, rows, depth), lambda k: (k, piece, 0, 0)), whole(w_out.shape)],
        out_specs=[whole((rows, width))] * 4,
        out_shape=[out] * 4,
        compiler_params=params(),
        cost_estimate=cost(8 * rows * depth * width, 2 * (depth * width + 4 * rows * (depth + width))),
        name="out_projection",
    )(attended, w_out)
    return terms[::-1]


def norm_kernel(x_ref, a_ref, b_ref, c_ref, gain_ref, hidden_ref, normed_ref):
    hidden = x_ref[...].astype(f32) + (a_ref[...].astype(f32) + b_ref[...].astype(f32) + c_ref[...].astype(f32))
    hidden_ref[...] = hidden
    inverse = lax.rsqrt(jnp.mean(hidden * hidden, axis=-1, keepdims=True) + epsilon)
    normed_ref[...] = (hidden * inverse * gain_ref[...]).astype(bf16)


def add_norm(tokens, piece, terms, gain):
    rows, width = terms[0].shape
    step = min(rows, 128)
    block = pl.BlockSpec((step, width), lambda k: (k, 0))
    return pl.pallas_call(
        norm_kernel,
        grid=(rows // step,),
        in_specs=[pl.BlockSpec((step, width), lambda k: (piece * (rows // step) + k, 0)), block, block, block, whole((1, width))],
        out_specs=[block, block],
        out_shape=[jax.ShapeDtypeStruct((rows, width), f32), jax.ShapeDtypeStruct((rows, width), bf16)],
        compiler_params=params(),
        cost_estimate=cost(10 * rows * width, 14 * rows * width),
        name="add_norm",
    )(tokens, *terms, gain)


def mlp_kernel(count, *refs):
    xs, cots = refs[:count], refs[count : 2 * count]
    wg, wu, wd = refs[2 * count : 2 * count + 3]
    stack_x, stack_cot, hidden_ref, gate_ref, up_ref, *parts = refs[-(5 + 2 * count) :]
    for k in range(count):

        @pl.when(pl.program_id(0) == k)
        def _():
            x, cot = xs[k][...], cots[k][...]
            stack_x[0, 0], stack_cot[0, 0] = x, cot
            gate = dot(x, wg[...])
            up = dot(x, wu[...])
            grad_hidden = dot(cot, wd[...], NT)
            sig = jax.nn.sigmoid(gate)
            act = gate * sig
            hidden = (act * up).astype(bf16)
            grad_gate = (grad_hidden * up * sig * (1.0 + gate * (1.0 - sig))).astype(bf16)
            grad_up = (grad_hidden * act).astype(bf16)
            hidden_ref[0, 0], gate_ref[0, 0], up_ref[0, 0] = hidden, grad_gate, grad_up
            parts[k][...] = (dot(grad_gate, wg[...], NT) + dot(grad_up, wu[...], NT)).astype(bf16)
            parts[count + k][...] = dot(hidden, wd[...]).astype(bf16)


def mlp_call(first, piece, pieces, xs, cots, wg, wu, wd, before):
    count = len(xs)
    rows, width = xs[0].shape
    units = wg.shape[1]
    spec = lambda cols: pl.BlockSpec((1, 1, rows, cols), lambda k: (first + k, piece, 0, 0))
    inputs = [*xs, *cots, wg, wu, wd]
    specs = [whole((rows, width))] * (2 * count) + [whole(w.shape) for w in (wg, wu, wd)]
    aliases = {}
    if before is not None:
        aliases = {len(inputs) + k: k for k in range(5)}
        inputs += list(before)
        specs += [pl.BlockSpec(memory_space=pl.ANY)] * 5
    cols = (width, width, units, units, units)
    outs = pl.pallas_call(
        functools.partial(mlp_kernel, count),
        grid=(count,),
        in_specs=specs,
        out_specs=[spec(c) for c in cols] + [whole((rows, width))] * (2 * count),
        out_shape=[jax.ShapeDtypeStruct((4, pieces, rows, c), bf16) for c in cols]
        + [jax.ShapeDtypeStruct((rows, width), bf16)] * (2 * count),
        input_output_aliases=aliases,
        compiler_params=params(),
        cost_estimate=cost(12 * count * rows * width * units, 6 * width * units + 2 * count * rows * (6 * width + 3 * units)),
        name="mlp",
    )(*inputs)
    return outs[:5], outs[5 : 5 + count], outs[5 + count :]


def norm_back_kernel(hidden_ref, cot_ref, a_ref, b_ref, c_ref, gain_ref, grad_ref, low_ref, gain_grad_ref):
    hidden = hidden_ref[...]
    grad = a_ref[...].astype(f32) + b_ref[...].astype(f32) + c_ref[...].astype(f32)
    inverse = lax.rsqrt(jnp.mean(hidden * hidden, axis=-1, keepdims=True) + epsilon)
    unit = hidden * inverse
    scaled = grad * gain_ref[...]
    result = cot_ref[...].astype(f32) + inverse * (scaled - unit * jnp.mean(scaled * unit, axis=-1, keepdims=True))
    grad_ref[...] = result
    if low_ref is not None:
        low_ref[...] = result.astype(bf16)
    product = grad * unit
    sums = jnp.sum(product.reshape(-1, 8, product.shape[-1]), axis=0)

    @pl.when(pl.program_id(0) == 0)
    def _():
        gain_grad_ref[...] = sums

    @pl.when(pl.program_id(0) > 0)
    def _():
        gain_grad_ref[...] += sums


def norm_back(hidden, cot, piece, cot_piece, terms, gain, low):
    rows, width = terms[0].shape
    step = min(rows, 128)
    steps = rows // step
    block = pl.BlockSpec((step, width), lambda k: (k, 0))
    at = lambda base: pl.BlockSpec((step, width), lambda k: (base * steps + k, 0))
    outs = [block] + [block] * low + [whole((8, width))]
    shapes = [jax.ShapeDtypeStruct((rows, width), f32)] + [jax.ShapeDtypeStruct((rows, width), bf16)] * low
    shapes += [jax.ShapeDtypeStruct((8, width), f32)]

    def kernel(h, c, t0, t1, t2, gain_ref, *out_refs):
        grad_ref, *rest = out_refs
        if not low:
            rest = [None, *rest]
        cast = h
        norm_back_kernel(_Widened(cast), c, t0, t1, t2, gain_ref, grad_ref, *rest)

    return pl.pallas_call(
        kernel,
        grid=(steps,),
        in_specs=[at(piece), at(cot_piece), block, block, block, whole((1, width))],
        out_specs=outs,
        out_shape=shapes,
        compiler_params=params(),
        cost_estimate=cost(20 * rows * width, 20 * rows * width),
        name="norm_back",
    )(hidden, cot, *terms, gain)


class _Widened:
    def __init__(self, ref):
        self.ref = ref

    def __getitem__(self, index):
        return self.ref[index].astype(f32)


def grad_attended_kernel(*refs):
    xs, w, rest = refs[:4], refs[4], refs[5:]
    out_ref, stack_ref = rest[-2:]
    for k in range(4):

        @pl.when(pl.program_id(0) == k)
        def _():
            g = xs[k][...]
            stack_ref[0, 0] = g
            out_ref[0, 0] = dot(g, w[...], NT).astype(bf16)


def grad_attended_call(piece, pieces, xs, w_out, before):
    rows, width = xs[0].shape
    depth = w_out.shape[0]
    spec = lambda cols: pl.BlockSpec((1, 1, rows, cols), lambda k: (k, piece, 0, 0))
    inputs = [*xs, w_out]
    specs = [whole((rows, width))] * 4 + [whole(w_out.shape)]
    aliases = {}
    if before is not None:
        aliases = {5: 0, 6: 1}
        inputs += list(before)
        specs += [pl.BlockSpec(memory_space=pl.ANY)] * 2
    return pl.pallas_call(
        grad_attended_kernel,
        grid=(4,),
        in_specs=specs,
        out_specs=[spec(depth), spec(width)],
        out_shape=[jax.ShapeDtypeStruct((4, pieces, rows, c), bf16) for c in (depth, width)],
        input_output_aliases=aliases,
        compiler_params=params(),
        cost_estimate=cost(8 * rows * width * depth, 2 * (width * depth + 4 * rows * (2 * width + depth))),
        name="grad_attended",
    )(*inputs)


def grad_normed_kernel(dq_ref, dk_ref, dv_ref, wq, wk, wv, *outs):
    for k in range(4):

        @pl.when(pl.program_id(0) == k)
        def _():
            total = dot(dq_ref[...], wq[...], NT) + dot(dk_ref[...], wk[...], NT) + dot(dv_ref[...], wv[...], NT)
            outs[3 - k][...] = total.astype(bf16)


def grad_normed(dq, dk, dv, wq, wk, wv):
    rows, width = dq.shape[0] // 4, wq.shape[0]
    block = lambda cols: pl.BlockSpec((rows, cols), lambda k: (k, 0))
    terms = pl.pallas_call(
        grad_normed_kernel,
        grid=(4,),
        in_specs=[block(dq.shape[1]), block(dk.shape[1]), block(dv.shape[1])] + [whole(w.shape) for w in (wq, wk, wv)],
        out_specs=[whole((rows, width))] * 4,
        out_shape=[jax.ShapeDtypeStruct((rows, width), bf16)] * 4,
        compiler_params=params(),
        cost_estimate=cost(8 * rows * width * 8 * LANES, 2 * width * 8 * LANES + 8 * rows * (width + 8 * LANES)),
        name="grad_normed",
    )(dq, dk, dv, wq, wk, wv)
    return terms[::-1]


def spread(heads):
    col = lax.broadcasted_iota(jnp.int32, (heads * HEAD_SIZE, heads * LANES), 1)
    row = lax.broadcasted_iota(jnp.int32, (heads * HEAD_SIZE, heads * LANES), 0)
    half, feature = row // HALF, row % HALF
    return (col == half * (LANES // 2) + feature).astype(bf16)


def body(
    tokens, segments, positions, norm_attn, w_query, key_weight, value_weight, w_out,
    norm_mlp, w_gate, w_up, w_down, cotangent,
):
    seq = segments.shape[0]
    own, width = tokens.shape
    me = lax.axis_index("tensor")
    order = me ^ jnp.arange(4, dtype=jnp.int32)
    blocks = 4

    starts = jnp.zeros_like(segments)
    for document in (1, 2, 3):
        first = jnp.sum((segments < document).astype(jnp.int32))
        starts = jnp.where(segments >= document, first, starts)
    start = jnp.take(starts.reshape(4, own), order, axis=0).reshape(1, seq)
    places = jnp.take(positions.reshape(4, own), order, axis=0).reshape(seq)
    lane = jnp.arange(LANES // 2)
    inverse = jnp.exp(lane.astype(f32) * (-2.0 * math.log(rope_base) / HEAD_SIZE))
    angles = places.astype(f32)[:, None] * jnp.where(lane < HALF, inverse, 0.0)[None, :]
    cos, sin = jnp.cos(angles), jnp.sin(angles)
    cos = jnp.concatenate([cos, cos], 1)
    sin = jnp.concatenate([-sin, sin], 1)
    me_ref = me.astype(jnp.int32).reshape(1)

    spread_q, spread_k = spread(w_query.shape[1] // HEAD_SIZE), spread(key_weight.shape[1] // HEAD_SIZE)
    wq = dot(w_query, spread_q).astype(bf16)
    wk = dot(key_weight, spread_k).astype(bf16)
    wv = dot(value_weight, spread_k).astype(bf16)
    wo = dot(spread_q, w_out, TN).astype(bf16)
    gain_attn, gain_mlp = norm_attn.reshape(1, width), norm_mlp.reshape(1, width)

    inputs = tokens.astype(f32)
    inverse_one = lax.rsqrt(jnp.mean(inputs * inputs, axis=-1, keepdims=True) + epsilon)
    normed_one = (inputs * inverse_one * norm_attn).astype(bf16)

    pieces, rows = CHUNKS, own // CHUNKS
    table = lambda t: t.reshape(4, pieces, rows, LANES)
    split = lambda t: [t[k * rows : (k + 1) * rows] for k in range(pieces)]
    stacks = None
    gathered = [gather_four(x) for x in split(normed_one)]
    for first in (0, 2):
        for piece in range(pieces):
            stacks = qkv_call(first, piece, pieces, gathered[piece][first : first + 2], wq, wk, wv, table(cos), table(sin), stacks)
    qkv, attn_in = stacks[0].reshape(seq, 8 * LANES), stacks[1].reshape(seq, width)

    attended, lse = attend(me_ref, qkv, start, blocks)
    cots = [gather_four(x) for x in split(cotangent)]

    attended_pieces = attended.reshape(4, pieces, rows, 4 * LANES)
    hidden_one, grad_one, gain_two_grads = [], [], []
    stacks = grads = None
    outs = []
    for piece in range(pieces):
        terms = scatter_sum(out_projection(attended_pieces, wo, piece))
        hidden, normed = add_norm(tokens, piece, terms, gain_mlp)
        xs = gather_four(normed)
        stacks, grad_low, out_low = mlp_call(0, piece, pieces, xs[:2], cots[piece][:2], w_gate, w_up, w_down, stacks)
        stacks, grad_high, out_high = mlp_call(2, piece, pieces, xs[2:], cots[piece][2:], w_gate, w_up, w_down, stacks)
        terms = scatter_sum([*grad_low, *grad_high])
        grad, low, gain_grad = norm_back(hidden, cotangent, 0, piece, terms, gain_mlp, 1)
        grads = grad_attended_call(piece, pieces, gather_four(low), wo, grads)
        hidden_one.append(hidden)
        grad_one.append(grad)
        gain_two_grads.append(gain_grad)
        outs.append([*out_low, *out_high])
    mlp_in, grad_out, hidden, grad_gate, grad_up = [t.reshape(seq, -1) for t in stacks]
    grad_attended, grad_rows = [t.reshape(seq, -1) for t in grads]

    grad_w_down = dp_sum(dot(hidden, grad_out, TN).astype(bf16))
    grad_w_gate = dp_sum(dot(mlp_in, grad_gate, TN).astype(bf16))
    grad_w_up = dp_sum(dot(mlp_in, grad_up, TN).astype(bf16))
    grad_w_out = dp_sum(dot(dot(attended, spread_q, NT).astype(bf16), grad_rows, TN).astype(bf16))

    output = []
    for piece in range(pieces):
        a, b, c = scatter_sum(outs[piece])
        output.append((hidden_one[piece] + (a.astype(f32) + b.astype(f32) + c.astype(f32))).astype(bf16))
    output = jnp.concatenate(output, 0)

    dq, dk, dv = attend_back(me_ref, qkv, attended, grad_attended, lse, start, cos, sin, blocks)
    grad_w_query = dp_sum(dot(attn_in, dot(dq, spread_q, NT).astype(bf16), TN).astype(bf16))
    grad_w_key = dp_sum(dot(attn_in, dot(dk, spread_k, NT).astype(bf16), TN).astype(bf16))
    grad_w_value = dp_sum(dot(attn_in, dot(dv, spread_k, NT).astype(bf16), TN).astype(bf16))
    terms = scatter_sum(grad_normed(dq, dk, dv, wq, wk, wv))
    grad_tokens, gain_one_grad = norm_back(tokens, jnp.concatenate(grad_one, 0), 0, 0, terms, gain_attn, 0)

    gains = jnp.stack([jnp.sum(gain_one_grad, 0), jnp.sum(sum(gain_two_grads), 0)])
    gains = all_sum(gains)
    return (
        output, grad_tokens, gains[0], grad_w_query, grad_w_key, grad_w_value, grad_w_out,
        gains[1], grad_w_gate, grad_w_up, grad_w_down,
    )


def solution(mesh):
    rows, cols, both = P("tensor", None), P(None, "tensor"), P(("dp", "tensor"), None)
    in_specs = (both, P("dp"), P("dp"), P(), cols, cols, cols, rows, P(), cols, cols, rows, both)
    out_specs = (both, both, P(), cols, cols, cols, rows, P(), cols, cols, rows)
    return jax.shard_map(body, mesh=mesh, in_specs=in_specs, out_specs=out_specs, check_vma=False)
```

time: 1470 us -> 940 us (0.64)
  waiting for transfers between devices: 798 us -> 484 us
  matrix products: 337 us -> 59.8 us
  Pallas kernels: 0 us -> 218 us
  local copies, waits for them, and re-layouts: 132 us -> 16.4 us
  starting transfers between devices: 0.37 us -> 68.9 us
  other arithmetic: 136 us -> 79.4 us
  blocking collectives: 39 us -> 0 us
    ppermute x0 -> x92, waiting for transfers between devices: none -> 484 us  [the longest x45 351 us: dp_swap(): return lax.ppermute(values, 'dp', [(i, i ^ bits) for i in range(size)])]
    psum x1 -> x0, waiting for transfers between devices: 411 us -> none  [body(): lax.psum(grad_w_query.astype(jnp.bfloat16), 'dp').astype(jnp.float32)]
    dot_general x49 -> x11, matrix products: 337 us -> 59.8 us  [dot(): return lax.dot_general(left, right, dims, preferred_element_type=f32)]
    reduce_scatter x4 -> x0, waiting for transfers between devices: 223 us -> none  [the longest x1 99.1 us: body(): lax.psum_scatter(contract_cols(grad_gate, w_gate) + contract_cols(grad_up...]
    pallas_call x0 -> x20, Pallas kernels: none -> 218 us  [the longest x4 74.2 us: mlp_call(): pl.pallas_call(functools.partial(mlp_kernel, count), grid=(count,), in_sp...]
    all_gather x4 -> x0, waiting for transfers between devices: 163 us -> none  [the longest x1 46.5 us: body(): lax.all_gather(grad_hidden_one.astype(jnp.bfloat16), 'tensor', axis=0, ti...]
    dynamic_update_slice x8 -> x0, local copies, waits for them, and re-layouts: 71.2 us -> none  [body(): lax.scan(attend_back, (zero_state, zero_state), (blocks_of_query, grad_bl...]
    ppermute x0 -> x92, starting transfers between devices: none -> 68.9 us  [the longest x45 49.4 us: dp_swap(): return lax.ppermute(values, 'dp', [(i, i ^ bits) for i in range(size)])]
  transfers between devices with their start and end apart: 9 -> 92, of which waited for: 9 -> 36; matrix products, arithmetic and copies ran while one was open for 6% -> 16% of each run, Pallas kernels for 0% -> 20%
where the time goes in v1:
time: 940 us; the launch traced here: 929 us
  waiting for transfers between devices  484 us (51%)
  Pallas kernels  218 us (23%)
  other arithmetic  79.4 us (8%)
  starting transfers between devices  68.9 us (7%)
  matrix products  59.8 us (6%)
  local copies, waits for them, and re-layouts  16.4 us (2%)
    ppermute x45, waiting for transfers between devices, dp_swap(): return lax.ppermute(values, 'dp', [(i, i ^ bits) for i in range(size)])  351 us
    ppermute x47, waiting for transfers between devices, swap(): return lax.ppermute(values, 'tensor', [(i, i ^ bits) for i in range(size)])  133 us
    pallas_call x4, Pallas kernels, mlp_call(): pl.pallas_call(functools.partial(mlp_kernel, count), grid=(count,), in_sp...  74.2 us
    dot_general x11, matrix products, dot(): return lax.dot_general(left, right, dims, preferred_element_type=f32)  59.8 us
    ppermute x45, starting transfers between devices, dp_swap(): return lax.ppermute(values, 'dp', [(i, i ^ bits) for i in range(size)])  49.4 us
    pallas_call x1, Pallas kernels, attend_back(): pl.pallas_call(functools.partial(attend_back_kernel, blocks=blocks, size=...  39.2 us
    pallas_call x4, Pallas kernels, qkv_call(): pl.pallas_call(functools.partial(qkv_kernel, count), grid=(count,), in_sp...  23 us
    convert_element_type x7, other arithmetic, dp_sum(): return piece.astype(f32)  22.3 us
  transfers between devices with their start and end apart: 92, of which 36 were waited for; matrix products, arithmetic and copies ran while one was open for 16% of the time, Pallas kernels for 20%

profile of v1, /device:TPU:24, one launch (start us, length us, event | category | flops | bytes accessed | tf_op | source)
XLA Modules:
  0.0 929.0 jit_solution(1554507205535751639)
XLA Ops:
  18.1 22.2 %collective-permute-done.2.refs_0_ = bf16[256,1536]{1,0:T(8,128)(2,1)} collective-permute-done((bf16[256,1536]{1,0:T(8,128)(2,1)S(1)}, bf16[256,1536]{1,0:T(8,128)(2,1)}, u32[]{:S(2)}, u32[]{:S(2)}) %collective-permute-start.2) | collective-permute-done | bytes 786464 | tf_op jit(solution)/shard_map/ppermute | solution.py:45
  71.2 22.1 %attention.1 = (bf16[2048,512]{1,0:T(8,128)(2,1)}, f32[2,2,2048]{2,1,0:T(2,128)}) custom-call(s32[1]{0:T(128)} %bitcast.me_ref, bf16[2048,1024]{1,0:T(8,128)(2,1)} %bitcast.53, bf16[2048,1024]{1,0:T(8,128)(2,1)} %bitcast.54, bf16[2048,1024]{1,0:T(8,128)(2,1)} %bitcast.55, s32[1,2048]{1,0:T(1,128)} %bitcast.63), custom_call_target="tpu_custom_call" | custom-call | flops 8589934592 | bytes 12582912 | tf_op jit(solution)/shard_map/attention/pallas_call | solution.py:186
  115.8 13.8 %collective-permute-done.8.c_ref = bf16[256,1536]{1,0:T(8,128)(2,1)} collective-permute-done((bf16[256,1536]{1,0:T(8,128)(2,1)}, bf16[256,1536]{1,0:T(8,128)(2,1)}, u32[]{:S(2)}, u32[]{:S(2)}) %collective-permute-start.8) | collective-permute-done | bytes 786464 | tf_op jit(solution)/shard_map/ppermute | solution.py:45
  134.9 11.6 %collective-permute-done.20.c_ref = bf16[256,1536]{1,0:T(8,128)(2,1)} collective-permute-done((bf16[256,1536]{1,0:T(8,128)(2,1)}, bf16[256,1536]{1,0:T(8,128)(2,1)}, u32[]{:S(2)}, u32[]{:S(2)}) %collective-permute-start.20) | collective-permute-done | bytes 786464 | tf_op jit(solution)/shard_map/ppermute | solution.py:45
  155.3 24.9 %collective-permute-done.26.refs_2_ = bf16[256,1536]{1,0:T(8,128)(2,1)} collective-permute-done((bf16[256,1536]{1,0:T(8,128)(2,1)S(1)}, bf16[256,1536]{1,0:T(8,128)(2,1)}, u32[]{:S(2)}, u32[]{:S(2)}) %collective-permute-start.26) | collective-permute-done | bytes 786464 | tf_op jit(solution)/shard_map/ppermute | solution.py:45
  180.8 15.4 %collective-permute-done.12.refs_0_ = bf16[256,1536]{1,0:T(8,128)(2,1)} collective-permute-done((bf16[256,1536]{1,0:T(8,128)(2,1)}, bf16[256,1536]{1,0:T(8,128)(2,1)}, u32[]{:S(2)}, u32[]{:S(2)}) %collective-permute-start.12) | collective-permute-done | bytes 786464 | tf_op jit(solution)/shard_map/ppermute | solution.py:45
  197.6 18.5 %mlp.4 = (bf16[4,2,256,1536]{3,2,1,0:T(8,128)(2,1)}, bf16[4,2,256,1536]{3,2,1,0:T(8,128)(2,1)}, bf16[4,2,256,1024]{3,2,1,0:T(8,128)(2,1)}, bf16[4,2,256,1024]{3,...) custom-call(bf16[256,1536]{1,0:T(8,128)(2,1)} %get-tuple-element.102, ...), custom_call_target="tpu_custom_call" | custom-call | flops 9663676416 | bytes 22020096 | tf_op jit(solution)/shard_map/mlp/pallas_call | solution.py:394
  218.1 18.5 %mlp.5 = (bf16[4,2,256,1536]{3,2,1,0:T(8,128)(2,1)}, bf16[4,2,256,1536]{3,2,1,0:T(8,128)(2,1)}, bf16[4,2,256,1024]{3,2,1,0:T(8,128)(2,1)}, bf16[4,2,256,1024]{3,...) custom-call(bf16[256,1536]{1,0:T(8,128)(2,1)} %collective-permute-do, ...), custom_call_target="tpu_custom_call", output_to_operand_aliasing={{0}: (7, {}), {1}: (8, {}), {2}: (9, {}), {3}: (10, {}), {4... | custom-call | flops 9663676416 | bytes 22020096 | tf_op jit(solution)/shard_map/mlp/pallas_call | solution.py:394
  236.6 18.7 %mlp.6 = (bf16[4,2,256,1536]{3,2,1,0:T(8,128)(2,1)}, bf16[4,2,256,1536]{3,2,1,0:T(8,128)(2,1)}, bf16[4,2,256,1024]{3,2,1,0:T(8,128)(2,1)}, bf16[4,2,256,1024]{3,...) custom-call(bf16[256,1536]{1,0:T(8,128)(2,1)} %get-tuple-element.117, ...), custom_call_target="tpu_custom_call", output_to_operand_aliasing={{0}: (7, {}), {1}: (8, {}), {2}: (9, {}), {3}: (10, {}), {4... | custom-call | flops 9663676416 | bytes 22020096 | tf_op jit(solution)/shard_map/mlp/pallas_call | solution.py:394
  255.4 18.5 %mlp.7 = (bf16[4,2,256,1536]{3,2,1,0:T(8,128)(2,1)}, bf16[4,2,256,1536]{3,2,1,0:T(8,128)(2,1)}, bf16[4,2,256,1024]{3,2,1,0:T(8,128)(2,1)}, bf16[4,2,256,1024]{3,...) custom-call(bf16[256,1536]{1,0:T(8,128)(2,1)} %copy-done.35, ...), custom_call_target="tpu_custom_call", output_to_operand_aliasing={{0}: (7, {}), {1}: (8, {}), {2}: (9, {}), {3}: (10, {}), {4... | custom-call | flops 9663676416 | bytes 22020096 | tf_op jit(solution)/shard_map/mlp/pallas_call | solution.py:394
  307.4 30.1 %collective-permute-done.74 = bf16[768,1024]{1,0:T(8,128)(2,1)S(1)} collective-permute-done((bf16[768,1024]{1,0:T(8,128)(2,1)S(1)}, bf16[768,1024]{1,0:T(8,128)(2,1)S(1)}, u32[]{:S(2)}, u32[]{:S(2)}) %collective-permute-start.74) | collective-permute-done | bytes 1572896 | tf_op jit(solution)/shard_map/ppermute | solution.py:64
  339.3 31.9 %collective-permute-done.80 = bf16[768,1024]{1,0:T(8,128)(2,1)S(1)} collective-permute-done((bf16[768,1024]{1,0:T(8,128)(2,1)S(1)}, bf16[768,1024]{1,0:T(8,128)(2,1)S(1)}, u32[]{:S(2)}, u32[]{:S(2)}) %collective-permute-start.80) | collective-permute-done | bytes 1572896 | tf_op jit(solution)/shard_map/ppermute | solution.py:64
  373.6 30.4 %collective-permute-done.86 = bf16[512,1536]{1,0:T(8,128)(2,1)S(1)} collective-permute-done((bf16[512,1536]{1,0:T(8,128)(2,1)S(1)}, bf16[512,1536]{1,0:T(8,128)(2,1)S(1)}, u32[]{:S(2)}, u32[]{:S(2)}) %collective-permute-start.86) | collective-permute-done | bytes 1572896 | tf_op jit(solution)/shard_map/ppermute | solution.py:64
  407.5 17.0 %collective-permute-done.32.t2 = bf16[256,1536]{1,0:T(8,128)(2,1)S(1)} collective-permute-done((bf16[256,1536]{1,0:T(8,128)(2,1)S(1)}, bf16[256,1536]{1,0:T(8,128)(2,1)S(1)}, u32[]{:S(2)}, u32[]{:S(2)}) %collective-permute-start.32) | collective-permute-done | bytes 786464 | tf_op jit(solution)/shard_map/ppermute | solution.py:45
  446.3 12.0 %collective-permute-done.35.t2 = bf16[256,1536]{1,0:T(8,128)(2,1)} collective-permute-done((bf16[256,1536]{1,0:T(8,128)(2,1)}, bf16[256,1536]{1,0:T(8,128)(2,1)}, u32[]{:S(2)}, u32[]{:S(2)}) %collective-permute-start.35) | collective-permute-done | bytes 786464 | tf_op jit(solution)/shard_map/ppermute | solution.py:45
  470.2 13.1 %collective-permute-done.81 = bf16[384,1024]{1,0:T(8,128)(2,1)} collective-permute-done((bf16[384,1024]{1,0:T(8,128)(2,1)}, bf16[384,1024]{1,0:T(8,128)(2,1)}, u32[]{:S(2)}, u32[]{:S(2)}) %collective-permute-start.81) | collective-permute-done | bytes 786464 | tf_op jit(solution)/shard_map/ppermute | solution.py:64
  484.8 14.9 %collective-permute-done.87 = bf16[256,1536]{1,0:T(8,128)(2,1)} collective-permute-done((bf16[256,1536]{1,0:T(8,128)(2,1)}, bf16[256,1536]{1,0:T(8,128)(2,1)}, u32[]{:S(2)}, u32[]{:S(2)}) %collective-permute-start.87) | collective-permute-done | bytes 786464 | tf_op jit(solution)/shard_map/ppermute | solution.py:64
  504.1 12.8 %collective-permute-done.76 = bf16[192,1024]{1,0:T(8,128)(2,1)S(1)} collective-permute-done((bf16[192,1024]{1,0:T(8,128)(2,1)S(1)}, bf16[192,1024]{1,0:T(8,128)(2,1)S(1)}, u32[]{:S(2)}, u32[]{:S(2)}) %collective-permute-start.76) | collective-permute-done | bytes 393248 | tf_op jit(solution)/shard_map/ppermute | solution.py:64
  549.2 39.2 %attention_back.1 = (bf16[2048,512]{1,0:T(8,128)(2,1)}, bf16[2048,256]{1,0:T(8,128)(2,1)}, bf16[2048,256]{1,0:T(8,128)(2,1)}) custom-call(s32[1]{0:T(128)} %bitcast.me_ref, bf16[2048,1024]{1,0:T(8,128)(2,1)} %bitcast.56, bf16[2048,1024]{1,0:T(8,128)(2,1)} %bitcast.57, bf16[2048,1024]{1,0:T(8,128)(2,1)} %bitcast.58, ...), custom_call_target="tpu_custom_call" | custom-call | flops 21474836480 | bytes 20971520 | tf_op jit(solution)/shard_map/attention_back/pallas_call | solution.py:274
  603.0 12.8 %grad_normed.1 = (bf16[512,1536]{1,0:T(8,128)(2,1)}, bf16[512,1536]{1,0:T(8,128)(2,1)}, bf16[512,1536]{1,0:T(8,128)(2,1)}, bf16[512,1536]{1,0:T(8,128)(2,1)}) custom-call(bf16[2048,512]{1,0:T(8,128)(2,1)} %get-tuple-element.148.dq_ref, bf16[2048,256]{1,0:T(8,128)(2,1)} %get-tuple-element.149.dk_ref, bf16[2048,256]{1,0:T(8,128)(2,1)} %get-tuple-element.150.dv_ref, ...), custom_call_target="tpu_custom_call" | custom-call | flops 6442450944 | bytes 13631488 | tf_op jit(solution)/shard_map/grad_normed/pallas_call | solution.py:516
  649.6 28.1 %collective-permute-done.57 = bf16[384,192]{0,1:T(8,128)(2,1)S(1)} collective-permute-done((bf16[384,192]{0,1:T(8,128)(2,1)S(1)}, bf16[384,192]{0,1:T(8,128)(2,1)S(1)}, u32[]{:S(2)}, u32[]{:S(2)}) %collective-permute-start.57) | collective-permute-done | bytes 147488 | tf_op jit(solution)/shard_map/ppermute | solution.py:64
  715.2 10.6 %collective-permute-done.60 = bf16[384,192]{0,1:T(8,128)(2,1)S(1)} collective-permute-done((bf16[384,192]{0,1:T(8,128)(2,1)S(1)}, bf16[384,192]{0,1:T(8,128)(2,1)S(1)}, u32[]{:S(2)}, u32[]{:S(2)}) %collective-permute-start.60) | collective-permute-done | bytes 147488 | tf_op jit(solution)/shard_map/ppermute | solution.py:64
  810.8 16.5 %collective-permute-done.55 = bf16[768,384]{1,0:T(8,128)(2,1)S(1)} collective-permute-done((bf16[768,384]{1,0:T(8,128)(2,1)S(1)}, bf16[768,384]{1,0:T(8,128)(2,1)S(1)}, u32[]{:S(2)}, u32[]{:S(2)}) %collective-permute-start.55) | collective-permute-done | bytes 589856 | tf_op jit(solution)/shard_map/ppermute | solution.py:64
  829.0 77.4 %collective-permute-done.73 = bf16[192,1536]{1,0:T(8,128)(2,1)} collective-permute-done((bf16[192,1536]{1,0:T(8,128)(2,1)S(1)}, bf16[192,1536]{1,0:T(8,128)(2,1)}, u32[]{:S(2)}, u32[]{:S(2)}) %collective-permute-start.73) | collective-permute-done | bytes 589856 | tf_op jit(solution)/shard_map/ppermute | solution.py:64
  (444 shorter events, 395.6 us)
Async XLA Ops:
  113.0 67.2 %collective-permute-start.14 = (bf16[256,1536]{1,0:T(8,128)(2,1)}, bf16[256,1536]{1,0:T(8,128)(2,1)}, u32[]{:S(2)}, u32[]{:S(2)}) collective-permute-start(bf16[256,1536]{1,0:T(8,128)(2,1)} %get-tuple-element.171.refs_2_), channel_id=1, source_target_pairs={{0,2},{1,3},{2,0},{3,1},{4,6},{5,7},{6,4},{7,5},{8,10},{9,11},{10,... | collective-permute-start | bytes 2359304 | tf_op jit(solution)/shard_map/ppermute | solution.py:45
  115.7 65.0 %collective-permute-start.10 = (bf16[256,1536]{1,0:T(8,128)(2,1)}, bf16[256,1536]{1,0:T(8,128)(2,1)}, u32[]{:S(2)}, u32[]{:S(2)}) collective-permute-start(bf16[256,1536]{1,0:T(8,128)(2,1)} %get-tuple-element.171.refs_2_), channel_id=1, source_target_pairs={{0,1},{1,0},{2,3},{3,2},{4,5},{5,4},{6,7},{7,6},{8,9},{9,8},{10,11... | collective-permute-start | bytes 2359304 | tf_op jit(solution)/shard_map/ppermute | solution.py:45
  134.3 61.9 %collective-permute-start.12 = (bf16[256,1536]{1,0:T(8,128)(2,1)}, bf16[256,1536]{1,0:T(8,128)(2,1)}, u32[]{:S(2)}, u32[]{:S(2)}) collective-permute-start(bf16[256,1536]{1,0:T(8,128)(2,1)} %get-tuple-element.102.refs_0_), channel_id=1, source_target_pairs={{0,2},{1,3},{2,0},{3,1},{4,6},{5,7},{6,4},{7,5},{8,10},{9,11},{10,... | collective-permute-start | bytes 2359304 | tf_op jit(solution)/shard_map/ppermute | solution.py:45
  180.2 75.2 %collective-permute-start.27 = (bf16[256,1536]{1,0:T(8,128)(2,1)}, bf16[256,1536]{1,0:T(8,128)(2,1)}, u32[]{:S(2)}, u32[]{:S(2)}) collective-permute-start(bf16[256,1536]{1,0:T(8,128)(2,1)} %collective-permute-done.26.refs_2_), channel_id=1, source_target_pairs={{0,1},{1,0},{2,3},{3,2},{4,5},{5,4},{6,7},{7,6},{8,9},{9,8},{10,11... | collective-permute-start | bytes 2359304 | tf_op jit(solution)/shard_map/ppermute | solution.py:45
  217.6 212.4 %collective-permute-start.11 = (bf16[256,1536]{1,0:T(8,128)(2,1)}, bf16[256,1536]{1,0:T(8,128)(2,1)S(1)}, u32[]{:S(2)}, u32[]{:S(2)}) collective-permute-start(bf16[256,1536]{1,0:T(8,128)(2,1)} %get-tuple-element.104), channel_id=1, source_target_pairs={{0,1},{1,0},{2,3},{3,2},{4,5},{5,4},{6,7},{7,6},{8,9},{9,8},{10,11... | collective-permute-start | bytes 2359304 | tf_op jit(solution)/shard_map/ppermute | solution.py:45
  302.8 68.4 %collective-permute-start.80 = (bf16[768,1024]{1,0:T(8,128)(2,1)S(1)}, bf16[768,1024]{1,0:T(8,128)(2,1)S(1)}, u32[]{:S(2)}, u32[]{:S(2)}) collective-permute-start(bf16[768,1024]{1,0:T(8,128)(2,1)S(1)} %constant_dynamic-slice_fusion.5), channel_id=1, source_target_pairs={{0,4},{4,0},{8,12},{12,8},{16,20},{20,16},{24,28},{28,24},{1,5},{5... | collective-permute-start | bytes 4718600 | tf_op jit(solution)/shard_map/ppermute | solution.py:64
  304.9 99.1 %collective-permute-start.86 = (bf16[512,1536]{1,0:T(8,128)(2,1)S(1)}, bf16[512,1536]{1,0:T(8,128)(2,1)S(1)}, u32[]{:S(2)}, u32[]{:S(2)}) collective-permute-start(bf16[512,1536]{1,0:T(8,128)(2,1)S(1)} %constant_dynamic-slice_fusion.2), channel_id=1, source_target_pairs={{0,4},{4,0},{8,12},{12,8},{16,20},{20,16},{24,28},{28,24},{1,5},{5... | collective-permute-start | bytes 4718600 | tf_op jit(solution)/shard_map/ppermute | solution.py:64
  307.1 97.8 %collective-permute-start.30 = (bf16[256,1536]{1,0:T(8,128)(2,1)S(1)}, bf16[256,1536]{1,0:T(8,128)(2,1)S(1)}, u32[]{:S(2)}, u32[]{:S(2)}) collective-permute-start(bf16[256,1536]{1,0:T(8,128)(2,1)S(1)} %copy-done.63), channel_id=1, source_target_pairs={{0,1},{1,0},{2,3},{3,2},{4,5},{5,4},{6,7},{7,6},{8,9},{9,8},{10,11... | collective-permute-start | bytes 2359304 | tf_op jit(solution)/shard_map/ppermute | solution.py:45
  337.5 96.8 %collective-permute-start.23 = (bf16[256,1536]{1,0:T(8,128)(2,1)}, bf16[256,1536]{1,0:T(8,128)(2,1)}, u32[]{:S(2)}, u32[]{:S(2)}) collective-permute-start(bf16[256,1536]{1,0:T(8,128)(2,1)} %get-tuple-element.124), channel_id=1, source_target_pairs={{0,1},{1,0},{2,3},{3,2},{4,5},{5,4},{6,7},{7,6},{8,9},{9,8},{10,11... | collective-permute-start | bytes 2359304 | tf_op jit(solution)/shard_map/ppermute | solution.py:45
  430.6 103.1 %collective-permute-start.39 = (bf16[256,1536]{1,0:T(8,128)(2,1)}, bf16[256,1536]{1,0:T(8,128)(2,1)}, u32[]{:S(2)}, u32[]{:S(2)}) collective-permute-start(bf16[256,1536]{1,0:T(8,128)(2,1)} %get-tuple-element.143.refs_0_), channel_id=1, source_target_pairs={{0,1},{1,0},{2,3},{3,2},{4,5},{5,4},{6,7},{7,6},{8,9},{9,8},{10,11... | collective-permute-start | bytes 2359304 | tf_op jit(solution)/shard_map/ppermute | solution.py:45
  434.2 66.9 %collective-permute-start.40 = (bf16[256,1536]{1,0:T(8,128)(2,1)}, bf16[256,1536]{1,0:T(8,128)(2,1)}, u32[]{:S(2)}, u32[]{:S(2)}) collective-permute-start(bf16[256,1536]{1,0:T(8,128)(2,1)} %get-tuple-element.143.refs_0_), channel_id=1, source_target_pairs={{0,2},{1,3},{2,0},{3,1},{4,6},{5,7},{6,4},{7,5},{8,10},{9,11},{10,... | collective-permute-start | bytes 2359304 | tf_op jit(solution)/shard_map/ppermute | solution.py:45
  533.6 99.7 %collective-permute-start.77 = (bf16[192,1024]{1,0:T(8,128)(2,1)S(1)}, bf16[192,1024]{1,0:T(8,128)(2,1)}, u32[]{:S(2)}, u32[]{:S(2)}) collective-permute-start(bf16[192,1024]{1,0:T(8,128)(2,1)S(1)} %add_convert_fusion.19), channel_id=1, source_target_pairs={{0,16},{4,20},{8,24},{12,28},{16,0},{20,4},{24,8},{28,12},{1,17},{... | collective-permute-start | bytes 1179656 | tf_op jit(solution)/shard_map/ppermute | solution.py:64
  533.7 103.4 %collective-permute-start.83 = (bf16[192,1024]{1,0:T(8,128)(2,1)S(1)}, bf16[192,1024]{1,0:T(8,128)(2,1)}, u32[]{:S(2)}, u32[]{:S(2)}) collective-permute-start(bf16[192,1024]{1,0:T(8,128)(2,1)S(1)} %add_convert_fusion.18), channel_id=1, source_target_pairs={{0,16},{4,20},{8,24},{12,28},{16,0},{20,4},{24,8},{28,12},{1,17},{... | collective-permute-start | bytes 1179656 | tf_op jit(solution)/shard_map/ppermute | solution.py:64
  536.7 102.5 %collective-permute-start.89 = (bf16[128,1536]{1,0:T(8,128)(2,1)S(1)}, bf16[128,1536]{1,0:T(8,128)(2,1)}, u32[]{:S(2)}, u32[]{:S(2)}) collective-permute-start(bf16[128,1536]{1,0:T(8,128)(2,1)S(1)} %add_convert_fusion.17), channel_id=1, source_target_pairs={{0,16},{4,20},{8,24},{12,28},{16,0},{20,4},{24,8},{28,12},{1,17},{... | collective-permute-start | bytes 1179656 | tf_op jit(solution)/shard_map/ppermute | solution.py:64
  617.7 95.8 %collective-permute-start.50 = (bf16[768,384]{1,0:T(8,128)(2,1)}, bf16[768,384]{1,0:T(8,128)(2,1)}, u32[]{:S(2)}, u32[]{:S(2)}) collective-permute-start(bf16[768,384]{1,0:T(8,128)(2,1)} %constant_dynamic-slice_fusion.20), channel_id=1, source_target_pairs={{0,4},{4,0},{8,12},{12,8},{16,20},{20,16},{24,28},{28,24},{1,5},{5... | collective-permute-start | bytes 1769480 | tf_op jit(solution)/shard_map/ppermute | solution.py:64
  637.1 74.2 %collective-permute-start.68 = (bf16[192,1536]{1,0:T(8,128)(2,1)S(1)}, bf16[192,1536]{1,0:T(8,128)(2,1)S(1)}, u32[]{:S(2)}, u32[]{:S(2)}) collective-permute-start(bf16[192,1536]{1,0:T(8,128)(2,1)S(1)} %constant_dynamic-slice_fusion.11), channel_id=1, source_target_pairs={{0,4},{4,0},{8,12},{12,8},{16,20},{20,16},{24,28},{28,24},{1,5},{5... | collective-permute-start | bytes 1769480 | tf_op jit(solution)/shard_map/ppermute | solution.py:64
  639.2 88.3 %collective-permute-start.78 = (bf16[384,1024]{1,0:T(8,128)(2,1)S(1)}, bf16[384,1024]{1,0:T(8,128)(2,1)S(1)}, u32[]{:S(2)}, u32[]{:S(2)}) collective-permute-start(bf16[384,1024]{1,0:T(8,128)(2,1)S(1)} %maximum_select_fusion.8), channel_id=1, source_target_pairs={{0,8},{4,12},{8,0},{12,4},{16,24},{20,28},{24,16},{28,20},{1,9},{5... | collective-permute-start | bytes 2359304 | tf_op jit(solution)/shard_map/ppermute | solution.py:64
  643.3 86.4 %collective-permute-start.84 = (bf16[384,1024]{1,0:T(8,128)(2,1)S(1)}, bf16[384,1024]{1,0:T(8,128)(2,1)S(1)}, u32[]{:S(2)}, u32[]{:S(2)}) collective-permute-start(bf16[384,1024]{1,0:T(8,128)(2,1)S(1)} %maximum_select_fusion.9), channel_id=1, source_target_pairs={{0,8},{4,12},{8,0},{12,4},{16,24},{20,28},{24,16},{28,20},{1,9},{5... | collective-permute-start | bytes 2359304 | tf_op jit(solution)/shard_map/ppermute | solution.py:64
  725.8 63.2 %collective-permute-start.42 = (bf16[512,1536]{1,0:T(8,128)(2,1)S(1)}, bf16[512,1536]{1,0:T(8,128)(2,1)S(1)}, u32[]{:S(2)}, u32[]{:S(2)}) collective-permute-start(bf16[512,1536]{1,0:T(8,128)(2,1)S(1)} %copy-done.60), channel_id=1, source_target_pairs={{0,1},{1,0},{2,3},{3,2},{4,5},{5,4},{6,7},{7,6},{8,9},{9,8},{10,11... | collective-permute-start | bytes 4718600 | tf_op jit(solution)/shard_map/ppermute | solution.py:45
  777.2 133.0 %collective-permute-start.79 = (bf16[768,1024]{1,0:T(8,128)(2,1)}, bf16[768,1024]{1,0:T(8,128)(2,1)}, u32[]{:S(2)}, u32[]{:S(2)}) collective-permute-start(bf16[768,1024]{1,0:T(8,128)(2,1)} %maximum_select_fusion.3), channel_id=1, source_target_pairs={{0,4},{4,0},{8,12},{12,8},{16,20},{20,16},{24,28},{28,24},{1,5},{5... | collective-permute-start | bytes 4718600 | tf_op jit(solution)/shard_map/ppermute | solution.py:64
  788.8 126.6 %collective-permute-start.85 = (bf16[768,1024]{1,0:T(8,128)(2,1)}, bf16[768,1024]{1,0:T(8,128)(2,1)}, u32[]{:S(2)}, u32[]{:S(2)}) collective-permute-start(bf16[768,1024]{1,0:T(8,128)(2,1)} %maximum_select_fusion.4), channel_id=1, source_target_pairs={{0,4},{4,0},{8,12},{12,8},{16,20},{20,16},{24,28},{28,24},{1,5},{5... | collective-permute-start | bytes 4718600 | tf_op jit(solution)/shard_map/ppermute | solution.py:64
  789.0 134.2 %collective-permute-start.91 = (bf16[512,1536]{1,0:T(8,128)(2,1)}, bf16[512,1536]{1,0:T(8,128)(2,1)}, u32[]{:S(2)}, u32[]{:S(2)}) collective-permute-start(bf16[512,1536]{1,0:T(8,128)(2,1)} %maximum_select_fusion.5), channel_id=1, source_target_pairs={{0,4},{4,0},{8,12},{12,8},{16,20},{20,16},{24,28},{28,24},{1,5},{5... | collective-permute-start | bytes 4718600 | tf_op jit(solution)/shard_map/ppermute | solution.py:64
  801.8 104.7 %collective-permute-start.73 = (bf16[192,1536]{1,0:T(8,128)(2,1)S(1)}, bf16[192,1536]{1,0:T(8,128)(2,1)}, u32[]{:S(2)}, u32[]{:S(2)}) collective-permute-start(bf16[192,1536]{1,0:T(8,128)(2,1)S(1)} %maximum_select_fusion.14), channel_id=1, source_target_pairs={{0,4},{4,0},{8,12},{12,8},{16,20},{20,16},{24,28},{28,24},{1,5},{5... | collective-permute-start | bytes 1769480 | tf_op jit(solution)/shard_map/ppermute | solution.py:64
  829.0 80.5 %collective-permute-start.46 = (f32[2,1536]{1,0:T(2,128)S(1)}, f32[2,1536]{1,0:T(2,128)S(1)}, u32[]{:S(2)}, u32[]{:S(2)}) collective-permute-start(f32[2,1536]{1,0:T(2,128)S(1)} %fusion.25), channel_id=1, source_target_pairs={{0,2},{1,3},{2,0},{3,1},{4,6},{5,7},{6,4},{7,5},{8,10},{9,11},{10,... | collective-permute-start | bytes 36872 | tf_op jit(solution)/shard_map/ppermute | solution.py:45
  (136 other events, 2442.5 us)

commit v2 on v1

v2 whole, which is shorter than its diff:
```python
import functools
import math

import jax
import jax.numpy as jnp
from jax import lax
from jax.experimental import pallas as pl
from jax.experimental.pallas import tpu as pltpu
from jax.sharding import PartitionSpec as P

HEAD_SIZE = 96
HALF = HEAD_SIZE // 2
LANES = 128
epsilon = 1e-05
rope_base = 100000.0
masked_value = -1e30
score_scale = 1.0 / math.sqrt(HEAD_SIZE)
log2_e = math.log2(math.e)
bf16, f32 = jnp.bfloat16, jnp.float32
NN = (((1,), (0,)), ((), ()))
NT = (((1,), (1,)), ((), ()))
TN = (((0,), (0,)), ((), ()))
VMEM_LIMIT = 67043328
CHUNKS = 4


def dot(left, right, dims=NN):
    return lax.dot_general(left, right, dims, preferred_element_type=f32)


def params():
    return pltpu.CompilerParams(vmem_limit_bytes=VMEM_LIMIT)


def cost(flops, nbytes):
    return pl.CostEstimate(flops=int(flops), bytes_accessed=int(nbytes), transcendentals=0)


def whole(shape):
    return pl.BlockSpec(shape, lambda *_: (0,) * len(shape), pipeline_mode=pl.Buffered(1))


def swap(values, bits):
    size = lax.axis_size("tensor")
    return lax.ppermute(values, "tensor", [(i, i ^ bits) for i in range(size)])


def dp_swap(values, bits):
    size = lax.axis_size("dp")
    return lax.ppermute(values, "dp", [(i, i ^ bits) for i in range(size)])


def dp_sum(values):
    size, index = lax.axis_size("dp"), lax.axis_index("dp")
    rows = values.shape[0]
    piece = values
    bit = 1
    while bit < size:
        half = piece.shape[0] // 2
        mine = (index // bit) % 2
        send = lax.dynamic_slice_in_dim(piece, (1 - mine) * half, half, 0)
        keep = lax.dynamic_slice_in_dim(piece, mine * half, half, 0)
        got = dp_swap(send, bit)
        piece = (keep.astype(f32) + got.astype(f32)).astype(bf16)
        bit *= 2
    while bit > 1:
        bit //= 2
        mine = (index // bit) % 2
        got = dp_swap(piece, bit)
        piece = jnp.where(mine == 0, jnp.concatenate([piece, got], 0), jnp.concatenate([got, piece], 0))
    return piece.astype(f32)


def all_sum(values):
    bit = 1
    while bit < lax.axis_size("tensor"):
        values = values + swap(values, bit)
        bit *= 2
    bit = 1
    while bit < lax.axis_size("dp"):
        values = values + dp_swap(values, bit)
        bit *= 2
    return values


ANY = pl.BlockSpec(memory_space=pl.ANY)
VMEM = pl.BlockSpec(memory_space=pltpu.VMEM)


def peer(bits):
    me = lax.axis_index("tensor")
    low, high = lax.rem(me, 2), lax.div(me, 2)
    if bits % 2:
        low = 1 - low
    if bits // 2:
        high = 1 - high
    return 2 * high + low


def partner(bits):
    return {"tensor": peer(bits)}


def send(source, target, sems, at, bits):
    return pltpu.make_async_remote_copy(
        src_ref=source,
        dst_ref=target,
        send_sem=sems[0].at[at],
        recv_sem=sems[1].at[at],
        device_id=partner(bits),
        device_id_type=pl.DeviceIdType.MESH,
    )


def meet():
    barrier = pltpu.get_barrier_semaphore()
    for bits in (1, 2):
        pl.semaphore_signal(barrier, inc=1, device_id=partner(bits), device_id_type=pl.DeviceIdType.MESH)
    pl.semaphore_wait(barrier, 2)


def comm_params(number):
    return pltpu.CompilerParams(vmem_limit_bytes=VMEM_LIMIT, collective_id=number, has_side_effects=True)


def dma_sems(*shape):
    return [pltpu.SemaphoreType.DMA(shape)] * 2


def qkv_kernel(x_ref, wq, wk, wv, cos_ref, sin_ref, qkv_ref, stack_ref, land, send_sem, recv_sem, out_sem):
    sems = (send_sem, recv_sem)
    own = x_ref.shape[0]
    rows = own // CHUNKS
    lane = lax.broadcasted_iota(jnp.int32, (rows, LANES), 1)

    def project(ref, base):
        x = ref[...]
        cos, sin = cos_ref[pl.ds(base, rows), :], sin_ref[pl.ds(base, rows), :]
        for w, first, turn in ((wq, 0, True), (wk, 4, True), (wv, 6, False)):
            y = dot(x, w[...])
            for h in range(w.shape[1] // LANES):
                v = y[:, h * LANES : (h + 1) * LANES]
                if turn:
                    v = v * cos + pltpu.roll(v, LANES // 2, 1) * sin
                else:
                    v = jnp.where(lane == HALF, 1.0, v)
                at = (first + h) * LANES
                qkv_ref[pl.ds(base, rows), at : at + LANES] = v.astype(bf16)

    def piece(k):
        return pl.ds(pl.multiple_of(k * rows, rows), rows)

    side = send(x_ref, land.at[0], sems, 2 * CHUNKS, 1)
    across = lambda k: send(x_ref.at[piece(k)], land.at[1, piece(k)], sems, k, 2)
    onward = lambda k: send(land.at[1, piece(k)], land.at[2, piece(k)], sems, CHUNKS + k, 1)
    store = lambda p: pltpu.make_async_copy(x_ref if p == 0 else land.at[p - 1], stack_ref.at[p], out_sem.at[p])

    meet()
    side.start()
    for k in range(CHUNKS):
        across(k).start()
    store(0).start()

    @pl.loop(0, CHUNKS)
    def _(k):
        project(x_ref.at[piece(k)], pl.multiple_of(k * rows, rows))

    side.wait_recv()
    store(1).start()

    @pl.loop(0, CHUNKS)
    def _(k):
        project(land.at[0, piece(k)], pl.multiple_of(own + k * rows, rows))

    @pl.loop(0, CHUNKS)
    def _(k):
        across(k).wait_recv()
        onward(k).start()
        project(land.at[1, piece(k)], pl.multiple_of(2 * own + k * rows, rows))
        onward(k).wait_recv()
        project(land.at[2, piece(k)], pl.multiple_of(3 * own + k * rows, rows))

    store(2).start()
    store(3).start()
    side.wait_send()
    for k in range(CHUNKS):
        across(k).wait_send()
        onward(k).wait_send()
    for p in range(4):
        store(p).wait()


def project_qkv(x, wq, wk, wv, cos, sin):
    own, width = x.shape
    return pl.pallas_call(
        qkv_kernel,
        in_specs=[VMEM] * 6,
        out_specs=[VMEM, ANY],
        out_shape=[jax.ShapeDtypeStruct((4 * own, 8 * LANES), bf16), jax.ShapeDtypeStruct((4, own, width), bf16)],
        scratch_shapes=[pltpu.VMEM((3, own, width), bf16), *dma_sems(2 * CHUNKS + 1), pltpu.SemaphoreType.DMA((4,))],
        compiler_params=comm_params(1),
        cost_estimate=cost(40e-6 * 1e15, 20e6),
        name="gather_project_qkv",
    )(x, wq, wk, wv, cos, sin)


def attend_kernel(
    q_ref, k_ref, v_ref, start_ref, cot_ref, o_ref, lse_ref, cots_ref, send_sem, recv_sem, *, blocks, size
):
    sems = (send_sem, recv_sem)
    side = send(cot_ref, cots_ref.at[0], sems, 2 * CHUNKS, 1)
    across = lambda k: send(cot_ref.at[k], cots_ref.at[1, k], sems, k, 2)
    onward = lambda k: send(cots_ref.at[1, k], cots_ref.at[2, k], sems, CHUNKS + k, 1)

    @pl.when(pl.program_id(0) == 0)
    def _():
        meet()
        side.start()
        for k in range(CHUNKS):
            across(k).start()

    for i in range(blocks):
        at = pl.multiple_of(peer(i) * size, size)
        queries = [q_ref[pl.ds(at, size), r * LANES : (r + 1) * LANES] for r in range(2)]
        start = start_ref[:, pl.ds(at, size)]
        state = [None, None]
        for j in [i, *range(i)]:
            key_at = pl.multiple_of(peer(j) * size, size)
            keys = k_ref[pl.ds(key_at, size), :]
            values = v_ref[pl.ds(key_at, size), :]
            key_rows = lax.broadcasted_iota(jnp.int32, (size, size), 0)
            allowed = key_rows >= start - j * size
            if j == i:
                allowed &= key_rows <= lax.broadcasted_iota(jnp.int32, (size, size), 1)
            for r in range(2):
                scores = jnp.where(allowed, dot(keys, queries[r], NT) * (score_scale * log2_e), masked_value)
                peak = jnp.max(scores, axis=0, keepdims=True)
                if state[r] is not None:
                    peak = jnp.maximum(state[r][0], peak)
                weights = jnp.exp2(scores - peak)
                mixed = dot(values, weights.astype(bf16), TN)
                if state[r] is not None:
                    mixed += state[r][1] * jnp.exp2(state[r][0] - peak)
                state[r] = (peak, mixed)
        for r, (peak, mixed) in enumerate(state):
            total = mixed[HALF : HALF + 1, :]
            o_ref[pl.ds(at, size), r * LANES : (r + 1) * LANES] = (mixed / total).T.astype(bf16)
            lse_ref[0, r : r + 1, pl.ds(at, size)] = peak + jnp.log2(total)

    @pl.when(pl.program_id(0) == 1)
    def _():
        for k in range(CHUNKS):
            across(k).wait_recv()
            onward(k).start()
        side.wait()
        for k in range(CHUNKS):
            across(k).wait_send()
            onward(k).wait()


def attend(qkv, start, cot, blocks):
    seq = qkv.shape[0]
    own, width = cot.shape
    pieces = (CHUNKS, own // CHUNKS, width)
    flops = 2 * 2 * 4 * LANES * seq * seq
    return pl.pallas_call(
        functools.partial(attend_kernel, blocks=blocks, size=seq // blocks),
        grid=(2,),
        in_specs=[
            pl.BlockSpec((seq, 2 * LANES), lambda g: (0, g)),
            pl.BlockSpec((seq, LANES), lambda g: (0, 4 + g)),
            pl.BlockSpec((seq, LANES), lambda g: (0, 6 + g)),
            pl.BlockSpec((1, seq), lambda g: (0, 0)),
            ANY,
        ],
        out_specs=[
            pl.BlockSpec((seq, 2 * LANES), lambda g: (0, g)),
            pl.BlockSpec((1, 2, seq), lambda g: (g, 0, 0)),
            ANY,
        ],
        scratch_shapes=dma_sems(2 * CHUNKS + 1),
        out_shape=[
            jax.ShapeDtypeStruct((seq, 4 * LANES), bf16),
            jax.ShapeDtypeStruct((2, 2, seq), f32),
            jax.ShapeDtypeStruct((3, *pieces), bf16),
        ],
        compiler_params=comm_params(4),
        cost_estimate=cost(flops, 6 * seq * 8 * LANES),
        name="attention",
    )(qkv, qkv, qkv, start, cot.reshape(pieces))


def attend_back_kernel(
    q_ref, k_ref, v_ref, o_ref, do_ref, lse_ref, start_ref, cos_ref, sin_ref, parts, hid1,
    dq_ref, dk_ref, dv_ref, out_ref, dq_sum, dk_sum, dv_sum, inner, mine, side, across, send_sem, recv_sem, load_sem,
    *, blocks, size,
):
    pieces = parts.shape[0]
    sems = (send_sem, recv_sem)
    from_side = [send(parts.at[:, 3 - 2 * k], side.at[k], sems, k, 1) for k in range(2)]
    from_across = send(mine.at[0], across, sems, 2, 2)
    load = [pltpu.make_async_copy(parts.at[:, 2 - 2 * k], mine.at[k], load_sem.at[k]) for k in range(2)]

    @pl.when(pl.program_id(0) == 0)
    def _():
        load[0].start()
        load[1].start()
        meet()
        from_side[0].start()
        from_side[1].start()

    for c in range(blocks):
        rows = slice(c * size, (c + 1) * size)
        for r in range(2):
            cols = slice(r * LANES, (r + 1) * LANES)
            product = do_ref[rows, cols].astype(f32) * o_ref[rows, cols].astype(f32)
            inner[r : r + 1, rows] = jnp.sum(product.T, axis=0, keepdims=True)
    for i in reversed(range(blocks)):
        if i == blocks - 2:

            @pl.when(pl.program_id(0) == 0)
            def _():
                load[0].wait()
                from_side[0].wait_recv()
                for k in range(pieces):
                    mine[0, k] = (mine[0, k].astype(f32) + side[0, k].astype(f32)).astype(bf16)
                from_across.start()

        for j in [i, *range(i)]:
            at = pl.multiple_of(peer(i) * size, size)
            key_at = pl.multiple_of(peer(j) * size, size)
            keys = k_ref[pl.ds(key_at, size), :]
            values = v_ref[pl.ds(key_at, size), :]
            start = start_ref[:, pl.ds(at, size)]
            key_rows = lax.broadcasted_iota(jnp.int32, (size, size), 0)
            allowed = key_rows >= start - j * size
            if j == i:
                allowed &= key_rows <= lax.broadcasted_iota(jnp.int32, (size, size), 1)
            dk = dv = None
            for r in range(2):
                cols = slice(r * LANES, (r + 1) * LANES)
                queries = q_ref[pl.ds(at, size), cols]
                grads = do_ref[pl.ds(at, size), cols]
                scores = jnp.where(allowed, dot(keys, queries, NT) * (score_scale * log2_e), masked_value)
                weights = jnp.exp2(scores - lse_ref[0, r : r + 1, pl.ds(at, size)])
                grad_weights = dot(values, grads, NT)
                grad_scores = (weights * (grad_weights - inner[r : r + 1, pl.ds(at, size)])).astype(bf16)
                dv_term = dot(weights.astype(bf16), grads)
                dk_term = dot(grad_scores, queries)
                dv = dv_term if dv is None else dv + dv_term
                dk = dk_term if dk is None else dk + dk_term
                dq = dot(grad_scores, keys, TN)
                if j == i:
                    dq_sum[pl.ds(at, size), cols] = dq
                else:
                    dq_sum[pl.ds(at, size), cols] += dq
            if i == blocks - 1:
                dk_sum[pl.ds(key_at, size), :] = dk
                dv_sum[pl.ds(key_at, size), :] = dv
            else:
                dk_sum[pl.ds(key_at, size), :] += dk
                dv_sum[pl.ds(key_at, size), :] += dv
    for c in range(blocks):
        rows = slice(c * size, (c + 1) * size)
        cos, sin = cos_ref[rows, :], sin_ref[rows, :]

        def back(grads):
            return ((grads * cos - pltpu.roll(grads, LANES // 2, 1) * sin) * score_scale).astype(bf16)

        for r in range(2):
            cols = slice(r * LANES, (r + 1) * LANES)
            dq_ref[rows, cols] = back(dq_sum[rows, cols])
        dk_ref[rows, :] = back(dk_sum[rows, :])
        dv_ref[rows, :] = dv_sum[rows, :].astype(bf16)

    @pl.when(pl.program_id(0) == 1)
    def _():
        load[1].wait()
        from_side[1].wait_recv()
        from_across.wait()
        from_side[0].wait_send()
        from_side[1].wait_send()
        for k in range(pieces):
            term = mine[1, k].astype(f32) + side[1, k].astype(f32) + across[k].astype(f32)
            out_ref[k] = (hid1[k] + term).astype(bf16)


def attend_back(qkv, attended, grads, lse, start, cos, sin, parts, hid1, blocks):
    seq = qkv.shape[0]
    own = hid1.shape
    pair = pl.BlockSpec((seq, 2 * LANES), lambda g: (0, g))
    single = pl.BlockSpec((seq, LANES), lambda g: (0, g))
    table = pl.BlockSpec((seq, LANES), lambda g: (0, 0))
    return pl.pallas_call(
        functools.partial(attend_back_kernel, blocks=blocks, size=seq // blocks),
        grid=(2,),
        in_specs=[
            pair,
            pl.BlockSpec((seq, LANES), lambda g: (0, 4 + g)),
            pl.BlockSpec((seq, LANES), lambda g: (0, 6 + g)),
            pair,
            pair,
            pl.BlockSpec((1, 2, seq), lambda g: (g, 0, 0)),
            pl.BlockSpec((1, seq), lambda g: (0, 0)),
            table,
            table,
            ANY,
            whole(own),
        ],
        out_specs=[pair, single, single, whole(own)],
        scratch_shapes=[
            pltpu.VMEM((seq, 2 * LANES), f32),
            pltpu.VMEM((seq, LANES), f32),
            pltpu.VMEM((seq, LANES), f32),
            pltpu.VMEM((2, seq), f32),
            pltpu.VMEM((2, *own), bf16),
            pltpu.VMEM((2, *own), bf16),
            pltpu.VMEM(own, bf16),
            *dma_sems(3),
            pltpu.SemaphoreType.DMA((2,)),
        ],
        out_shape=[
            jax.ShapeDtypeStruct((seq, 4 * LANES), bf16),
            jax.ShapeDtypeStruct((seq, 2 * LANES), bf16),
            jax.ShapeDtypeStruct((seq, 2 * LANES), bf16),
            jax.ShapeDtypeStruct(own, bf16),
        ],
        compiler_params=comm_params(5),
        cost_estimate=cost(5 * 2 * 4 * LANES * seq * seq, 10 * seq * 8 * LANES),
        name="attention_back",
    )(qkv, qkv, qkv, attended, grads, lse, start, cos, sin, parts, hid1)


RS1_C0, RS1_C1, RS1_X, AG2_X, AG2_C, AG2_F, RS3_C0, RS3_C1, RS3_X, AG3_X, AG3_C, AG3_F = range(12)


def middle_kernel(
    att, wo, tokens, gain, cot_own, cots, wg, wu, wd,
    hid1, datt_out, parts_out, grad_one_out, dwd_out, dwg_out, dwu_out, dwo_out, gain_grad,
    xs, cot, hid, gg, gu, g, cr, xr, part_stage, grad_stage, datt_stage, tile_stage,
    send_sem, recv_sem, cot_sem, part_sem, grad_sem, datt_sem, tile_sem, free_sem,
):
    pieces, _, n, width = xs.shape
    units = wg.shape[1]
    heads = wo.shape[0]
    sems = (send_sem, recv_sem)
    two = (2 * n, width)

    def copy(kind, k):
        source, target, bits = {
            RS1_C0: (g.at[k, 3], cr.at[k, 0], 1),
            RS1_C1: (g.at[k, 1], cr.at[k, 1], 1),
            RS1_X: (g.at[k, 2], xr.at[k], 2),
            AG2_X: (xs.at[k, 0], xs.at[k, 2], 2),
            AG2_C: (xs.at[k, 0], xs.at[k, 1], 1),
            AG2_F: (xs.at[k, 2], xs.at[k, 3], 1),
            RS3_C0: (g.at[k, 3], cr.at[k, 0], 1),
            RS3_C1: (g.at[k, 1], cr.at[k, 1], 1),
            RS3_X: (g.at[k, 2], xr.at[k], 2),
            AG3_X: (g.at[k, 0], g.at[k, 2], 2),
            AG3_C: (g.at[k, 0], g.at[k, 1], 1),
            AG3_F: (g.at[k, 2], g.at[k, 3], 1),
        }[kind]
        return send(source, target, sems, (kind, k), bits)

    def credit(k, bits):
        pl.semaphore_signal(
            free_sem.at[bits - 1, k], inc=1, device_id=partner(bits), device_id_type=pl.DeviceIdType.MESH
        )

    def cot_copy(p):
        source = cot_own if p == 0 else cots.at[p - 1]
        return pltpu.make_async_copy(source, cot.at[:, p], cot_sem.at[p])

    def part_copy(k, low):
        return pltpu.make_async_copy(part_stage.at[k], parts_out.at[k, pl.ds(low, 2)], part_sem.at[k])

    for p in range(4):
        cot_copy(p).start()
    meet()

    @pl.loop(0, pieces)
    def _(k):
        for p, kind in ((3, RS1_C0), (1, RS1_C1)):
            g[k, p] = dot(att[p, k], wo[...]).astype(bf16)
            copy(kind, k).start()

    @pl.loop(0, pieces)
    def _(k):
        term = dot(att[2, k], wo[...])
        copy(RS1_C0, k).wait_recv()
        g[k, 2] = (term + cr[k, 0].astype(f32)).astype(bf16)
        copy(RS1_X, k).start()

    def feed_forward(k, low):
        x = xs[k, pl.ds(low, 2)].reshape(two)
        gate = dot(x, wg[...])
        up = dot(x, wu[...])
        grad_hidden = dot(cot[k, pl.ds(low, 2)].reshape(two), wd[...], NT)
        sig = jax.nn.sigmoid(gate)
        act = gate * sig
        hidden = (act * up).astype(bf16)
        grad_gate = (grad_hidden * up * sig * (1.0 + gate * (1.0 - sig))).astype(bf16)
        grad_up = (grad_hidden * act).astype(bf16)
        hid[k, pl.ds(low, 2)] = hidden.reshape(2, n, units)
        gg[k, pl.ds(low, 2)] = grad_gate.reshape(2, n, units)
        gu[k, pl.ds(low, 2)] = grad_up.reshape(2, n, units)
        back = dot(grad_gate, wg[...], NT) + dot(grad_up, wu[...], NT)
        g[k, pl.ds(low, 2)] = back.astype(bf16).reshape(2, n, width)
        return hidden

    def out_part(k, low, hidden):
        part_stage[k] = dot(hidden, wd[...]).astype(bf16).reshape(2, n, width)
        part_copy(k, low).start()

    for p in range(4):
        cot_copy(p).wait()

    @pl.loop(0, pieces)
    def _(k):
        term = dot(att[0, k], wo[...])
        copy(RS1_C1, k).wait_recv()
        copy(RS1_X, k).wait_recv()
        hidden = tokens[k].astype(f32) + (term + cr[k, 1].astype(f32) + xr[k].astype(f32))
        hid1[k] = hidden
        inverse = lax.rsqrt(jnp.mean(hidden * hidden, axis=-1, keepdims=True) + epsilon)
        xs[k, 0] = (hidden * inverse * gain[...]).astype(bf16)
        copy(AG2_X, k).start()
        copy(AG2_C, k).start()
        copy(AG2_C, k).wait_recv()
        copy(RS1_C1, k).wait_send()
        out_part(k, 0, feed_forward(k, 0))

    @pl.loop(0, pieces)
    def _(k):
        copy(AG2_X, k).wait_recv()
        copy(AG2_F, k).start()
        part_copy(k, 0).wait()
        copy(AG2_F, k).wait_recv()
        copy(RS1_C0, k).wait_send()
        copy(RS1_X, k).wait_send()
        hidden = feed_forward(k, 2)
        copy(RS3_C0, k).start()
        copy(RS3_C1, k).start()
        out_part(k, 2, hidden)
        copy(RS3_C0, k).wait_recv()
        g[k, 2] = (g[k, 2].astype(f32) + cr[k, 0].astype(f32)).astype(bf16)
        copy(RS3_X, k).start()

    tokens_all = 4 * pieces * n

    def tile(slot, left, right, cols, out, at):
        height = out.shape[1]
        target = out.at[pl.ds(pl.multiple_of(at * 256, 256), 256)]
        move = pltpu.make_async_copy(tile_stage.at[slot, :, pl.ds(0, height)], target, tile_sem.at[slot])
        part = left[:, :, :, pl.ds(pl.multiple_of(at * 256, 256), 256)].reshape(tokens_all, 256)
        tile_stage[slot, :, pl.ds(0, height)] = dot(part, right[...].reshape(tokens_all, cols), TN).astype(bf16)
        return move

    @pl.loop(0, 4)
    def _(k):
        down = tile(0, hid, cot, width, dwd_out, k)
        down.start()
        copy(RS3_C1, k).wait_recv()
        copy(RS3_X, k).wait_recv()
        copy(RS3_C0, k).wait_send()
        copy(RS3_C1, k).wait_send()
        credit(k, 1)
        copy(RS3_X, k).wait_send()
        credit(k, 2)
        grad = g[k, 0].astype(f32) + cr[k, 1].astype(f32) + xr[k].astype(f32)
        hidden = hid1[k]
        inverse = lax.rsqrt(jnp.mean(hidden * hidden, axis=-1, keepdims=True) + epsilon)
        unit = hidden * inverse
        scaled = grad * gain[...]
        result = cot[k, 0].astype(f32) + inverse * (scaled - unit * jnp.mean(scaled * unit, axis=-1, keepdims=True))
        g[k, 0] = result.astype(bf16)
        pl.semaphore_wait(free_sem.at[0, k], 1)
        pl.semaphore_wait(free_sem.at[1, k], 1)
        copy(AG3_X, k).start()
        copy(AG3_C, k).start()
        grad_stage[...] = result
        stored = pltpu.make_async_copy(grad_stage, grad_one_out.at[k], grad_sem.at[0])
        stored.start()
        sums = jnp.sum((grad * unit).reshape(-1, 8, width), axis=0)

        @pl.when(k == 0)
        def _():
            gain_grad[...] = sums

        @pl.when(k > 0)
        def _():
            gain_grad[...] += sums

        down.wait()
        gate = tile(0, xs, gg, units, dwg_out, k)
        gate.start()
        up = tile(1, xs, gu, units, dwu_out, k)
        up.start()
        gate.wait()
        up.wait()
        stored.wait()

    @pl.loop(0, pieces)
    def _(k):
        copy(AG3_X, k).wait_recv()
        copy(AG3_F, k).start()

        @pl.when(k < 2)
        def _():
            gate = tile(0, xs, gg, units, dwg_out, 4 + k)
            gate.start()
            up = tile(1, xs, gu, units, dwu_out, 4 + k)
            up.start()
            gate.wait()
            up.wait()

        copy(AG3_C, k).wait_recv()
        copy(AG3_F, k).wait_recv()
        datt_stage[...] = dot(g[k].reshape(4 * n, width), wo[...], NT).astype(bf16).reshape(4, n, heads)
        moved = pltpu.make_async_copy(datt_stage, datt_out.at[:, k], datt_sem.at[0])
        moved.start()
        moved.wait()

    for u in range(heads // 256):
        total = None
        for p in range(4):
            left = att[p, :, :, u * 256 : (u + 1) * 256].reshape(pieces * n, 256)
            term = dot(left, g[:, p].reshape(pieces * n, width), TN)
            total = term if total is None else total + term
        tile_stage[u] = total.astype(bf16)
        pltpu.make_async_copy(tile_stage.at[u], dwo_out.at[pl.ds(u * 256, 256)], tile_sem.at[u]).start()
    for u in range(heads // 256):
        pltpu.make_async_copy(tile_stage.at[u], dwo_out.at[pl.ds(u * 256, 256)], tile_sem.at[u]).wait()

    @pl.loop(0, pieces)
    def _(k):
        part_copy(k, 2).wait()
        for kind in (AG2_X, AG2_C, AG2_F, AG3_X, AG3_C, AG3_F):
            copy(kind, k).wait_send()


def middle(attended, wo, tokens, gain, cot_own, cots, wg, wu, wd):
    width, units, heads = wg.shape[0], wg.shape[1], wo.shape[0]
    pieces = CHUNKS
    n = tokens.shape[0] // pieces
    sds = jax.ShapeDtypeStruct
    own = (pieces, n, width)
    all_rows = (pieces, 4, n, width)
    all_units = (pieces, 4, n, units)
    return pl.pallas_call(
        middle_kernel,
        in_specs=[VMEM] * 4 + [ANY] * 2 + [VMEM] * 3,
        out_specs=[VMEM] + [ANY] * 7 + [VMEM],
        out_shape=[
            sds(own, f32),
            sds((4, pieces, n, heads), bf16),
            sds(all_rows, bf16),
            sds(own, f32),
            sds((units, width), bf16),
            sds((width, units), bf16),
            sds((width, units), bf16),
            sds((heads, width), bf16),
            sds((8, width), f32),
        ],
        scratch_shapes=[
            pltpu.VMEM(all_rows, bf16),
            pltpu.VMEM(all_rows, bf16),
            pltpu.VMEM(all_units, bf16),
            pltpu.VMEM(all_units, bf16),
            pltpu.VMEM(all_units, bf16),
            pltpu.VMEM(all_rows, bf16),
            pltpu.VMEM((pieces, 2, n, width), bf16),
            pltpu.VMEM(own, bf16),
            pltpu.VMEM((pieces, 2, n, width), bf16),
            pltpu.VMEM((n, width), f32),
            pltpu.VMEM((4, n, heads), bf16),
            pltpu.VMEM((2, 256, width), bf16),
            *dma_sems(12, pieces),
            pltpu.SemaphoreType.DMA((4,)),
            pltpu.SemaphoreType.DMA((pieces,)),
            pltpu.SemaphoreType.DMA((1,)),
            pltpu.SemaphoreType.DMA((1,)),
            pltpu.SemaphoreType.DMA((2,)),
            pltpu.SemaphoreType.REGULAR((2, pieces)),
        ],
        compiler_params=comm_params(2),
        cost_estimate=cost(150e-6 * 1e15, 80e6),
        name="middle",
    )(
        attended.reshape(4, pieces, n, heads), wo, tokens.reshape(own), gain,
        cot_own.reshape(own), cots, wg, wu, wd,
    )


def end_kernel(
    dq, dk, dv, wq, wk, wv, tokens, grad_one, gain, grad_ref, gain_grad, parts, cr, xr, send_sem, recv_sem
):
    own, width = tokens.shape
    rows = own // CHUNKS
    sems = (send_sem, recv_sem)

    def at(base, k):
        return pl.ds(pl.multiple_of(base + k * rows, rows), rows)

    def term(p, k):
        here = at(p * own, k)
        return dot(dq[here], wq[...], NT) + dot(dk[here], wk[...], NT) + dot(dv[here], wv[...], NT)

    side0 = lambda k: send(parts.at[at(0, k)], cr.at[0, at(0, k)], sems, (0, k), 1)
    side1 = lambda k: send(parts.at[at(own, k)], cr.at[1, at(0, k)], sems, (1, k), 1)
    across = lambda k: send(parts.at[at(2 * own, k)], xr.at[at(0, k)], sems, (2, k), 2)

    meet()

    @pl.loop(0, CHUNKS)
    def _(k):
        parts[at(0, k)] = term(3, k).astype(bf16)
        side0(k).start()
        mine = term(2, k)
        side0(k).wait_recv()
        parts[at(2 * own, k)] = (mine + cr[0, at(0, k)].astype(f32)).astype(bf16)
        across(k).start()

    @pl.loop(0, CHUNKS)
    def _(k):
        parts[at(own, k)] = term(1, k).astype(bf16)
        side1(k).start()
        grad_ref[at(0, k)] = term(0, k)

    @pl.loop(0, CHUNKS)
    def _(k):
        side1(k).wait_recv()
        across(k).wait_recv()
        here = at(0, k)
        grad = grad_ref[here] + cr[1, here].astype(f32) + xr[here].astype(f32)
        inputs = tokens[here].astype(f32)
        inverse = lax.rsqrt(jnp.mean(inputs * inputs, axis=-1, keepdims=True) + epsilon)
        unit = inputs * inverse
        scaled = grad * gain[...]
        grad_ref[here] = grad_one[here] + inverse * (scaled - unit * jnp.mean(scaled * unit, axis=-1, keepdims=True))
        sums = jnp.sum((grad * unit).reshape(-1, 8, width), axis=0)

        @pl.when(k == 0)
        def _():
            gain_grad[...] = sums

        @pl.when(k > 0)
        def _():
            gain_grad[...] += sums

    @pl.loop(0, CHUNKS)
    def _(k):
        side0(k).wait_send()
        side1(k).wait_send()
        across(k).wait_send()


def end(dq, dk, dv, wq, wk, wv, tokens, grad_one, gain):
    own, width = tokens.shape
    return pl.pallas_call(
        end_kernel,
        in_specs=[VMEM] * 9,
        out_specs=[VMEM] * 2,
        out_shape=[jax.ShapeDtypeStruct((own, width), f32), jax.ShapeDtypeStruct((8, width), f32)],
        scratch_shapes=[
            pltpu.VMEM((3 * own, width), bf16),
            pltpu.VMEM((2, own, width), bf16),
            pltpu.VMEM((own, width), bf16),
            *dma_sems(3, CHUNKS),
        ],
        compiler_params=comm_params(3),
        cost_estimate=cost(50e-6 * 1e15, 30e6),
        name="end",
    )(dq, dk, dv, wq, wk, wv, tokens, grad_one, gain)


def spread(heads):
    col = lax.broadcasted_iota(jnp.int32, (heads * HEAD_SIZE, heads * LANES), 1)
    row = lax.broadcasted_iota(jnp.int32, (heads * HEAD_SIZE, heads * LANES), 0)
    half, feature = row // HALF, row % HALF
    return (col == half * (LANES // 2) + feature).astype(bf16)


def body(
    tokens, segments, positions, norm_attn, w_query, key_weight, value_weight, w_out,
    norm_mlp, w_gate, w_up, w_down, cotangent,
):
    seq = segments.shape[0]
    own, width = tokens.shape
    me = lax.axis_index("tensor")
    order = me ^ jnp.arange(4, dtype=jnp.int32)
    blocks = 4

    starts = jnp.zeros_like(segments)
    for document in (1, 2, 3):
        first = jnp.sum((segments < document).astype(jnp.int32))
        starts = jnp.where(segments >= document, first, starts)
    start = jnp.take(starts.reshape(4, own), order, axis=0).reshape(1, seq)
    places = jnp.take(positions.reshape(4, own), order, axis=0).reshape(seq)
    lane = jnp.arange(LANES // 2)
    inverse = jnp.exp(lane.astype(f32) * (-2.0 * math.log(rope_base) / HEAD_SIZE))
    angles = places.astype(f32)[:, None] * jnp.where(lane < HALF, inverse, 0.0)[None, :]
    cos, sin = jnp.cos(angles), jnp.sin(angles)
    cos = jnp.concatenate([cos, cos], 1)
    sin = jnp.concatenate([-sin, sin], 1)

    spread_q, spread_k = spread(w_query.shape[1] // HEAD_SIZE), spread(key_weight.shape[1] // HEAD_SIZE)
    wq = dot(w_query, spread_q).astype(bf16)
    wk = dot(key_weight, spread_k).astype(bf16)
    wv = dot(value_weight, spread_k).astype(bf16)
    wo = dot(spread_q, w_out, TN).astype(bf16)
    gain_attn, gain_mlp = norm_attn.reshape(1, width), norm_mlp.reshape(1, width)

    inputs = tokens.astype(f32)
    inverse_one = lax.rsqrt(jnp.mean(inputs * inputs, axis=-1, keepdims=True) + epsilon)
    normed_one = (inputs * inverse_one * norm_attn).astype(bf16)

    qkv, attn_in = project_qkv(normed_one, wq, wk, wv, cos, sin)
    attended, lse, cots = attend(qkv, start, cotangent, blocks)
    hid1, grad_attended, parts, grad_one, dwd, dwg, dwu, dwo, gain_two_grad = middle(
        attended, wo, tokens, gain_mlp, cotangent, cots, w_gate, w_up, w_down
    )
    grad_attended = grad_attended.reshape(seq, -1)
    dq, dk, dv, output = attend_back(
        qkv, attended, grad_attended, lse, start, cos, sin, parts, hid1, blocks
    )
    output = output.reshape(own, width)
    attn_in = attn_in.reshape(seq, width)
    grad_w_down, grad_w_gate, grad_w_up = dp_sum(dwd), dp_sum(dwg), dp_sum(dwu)
    grad_w_out = dp_sum(dot(spread_q, dwo).astype(bf16))
    grad_w_query = dp_sum(dot(attn_in, dot(dq, spread_q, NT).astype(bf16), TN).astype(bf16))
    grad_w_key = dp_sum(dot(attn_in, dot(dk, spread_k, NT).astype(bf16), TN).astype(bf16))
    grad_w_value = dp_sum(dot(attn_in, dot(dv, spread_k, NT).astype(bf16), TN).astype(bf16))
    grad_tokens, gain_one_grad = end(dq, dk, dv, wq, wk, wv, tokens, grad_one.reshape(own, width), gain_attn)

    gains = jnp.stack([jnp.sum(gain_one_grad, 0), jnp.sum(gain_two_grad, 0)])
    gains = all_sum(gains)
    return (
        output, grad_tokens, gains[0], grad_w_query, grad_w_key, grad_w_value, grad_w_out,
        gains[1], grad_w_gate, grad_w_up, grad_w_down,
    )


def solution(mesh):
    rows, cols, both = P("tensor", None), P(None, "tensor"), P(("dp", "tensor"), None)
    in_specs = (both, P("dp"), P("dp"), P(), cols, cols, cols, rows, P(), cols, cols, rows, both)
    out_specs = (both, both, P(), cols, cols, cols, rows, P(), cols, cols, rows)
    return jax.shard_map(body, mesh=mesh, in_specs=in_specs, out_specs=out_specs, check_vma=False)
```

time: 940 us -> 830 us (0.88)
  waiting for transfers between devices: 484 us -> 343 us
  Pallas kernels: 218 us -> 354 us
  other arithmetic: 79.4 us -> 42 us
  starting transfers between devices: 68.9 us -> 33 us
  matrix products: 59.8 us -> 30.4 us
    ppermute x47 -> x2, waiting for transfers between devices: 133 us -> 0.36 us  [swap(): return lax.ppermute(values, 'tensor', [(i, i ^ bits) for i in range(size)])]
    pallas_call x18 -> x3, Pallas kernels: 157 us -> 260 us  [the longest x1 169 us: middle(): pl.pallas_call(middle_kernel, in_specs=[VMEM] * 4 + [ANY] * 2 + [VMEM] *...]
    dot_general x11 -> x8, matrix products: 59.8 us -> 30.4 us  [dot(): return lax.dot_general(left, right, dims, preferred_element_type=f32)]
    pallas_call x1, Pallas kernels: 22.1 us -> 42.1 us  [attend(): pl.pallas_call(functools.partial(attend_kernel, blocks=blocks, size=seq /...]
    ppermute x47 -> x2, starting transfers between devices: 19.6 us -> 1.05 us  [swap(): return lax.ppermute(values, 'tensor', [(i, i ^ bits) for i in range(size)])]
    ppermute x45, starting transfers between devices: 49.4 us -> 31.9 us  [dp_swap(): return lax.ppermute(values, 'dp', [(i, i ^ bits) for i in range(size)])]
    pallas_call x1, Pallas kernels: 39.2 us -> 52.1 us  [attend_back(): pl.pallas_call(functools.partial(attend_back_kernel, blocks=blocks, size=...]
    convert_element_type x9 -> x0, other arithmetic: 11.5 us -> none  [the longest x7 7.21 us: scatter_sum(): travelling = (part[2].astype(f32) + from_side_2.astype(f32)).astype(bf16)]
  transfers between devices with their start and end apart: 92 -> 47, of which waited for: 36 -> 32; matrix products, arithmetic and copies ran while one was open for 16% -> 7% of each run, Pallas kernels for 20% -> 0%
where the time goes in v2:
time: 830 us; the launch traced here: 823 us
  Pallas kernels  354 us (43%)
  waiting for transfers between devices  343 us (41%)
  other arithmetic  42 us (5%)
  starting transfers between devices  33 us (4%)
  matrix products  30.4 us (4%)
  local copies, waits for them, and re-layouts  18.5 us (2%)
    ppermute x45, waiting for transfers between devices, dp_swap(): return lax.ppermute(values, 'dp', [(i, i ^ bits) for i in range(size)])  343 us
    pallas_call x1, Pallas kernels, middle(): pl.pallas_call(middle_kernel, in_specs=[VMEM] * 4 + [ANY] * 2 + [VMEM] *...  169 us
    pallas_call x1, Pallas kernels, attend_back(): pl.pallas_call(functools.partial(attend_back_kernel, blocks=blocks, size=...  52.1 us
    pallas_call x1, Pallas kernels, end(): pl.pallas_call(end_kernel, in_specs=[VMEM] * 9, out_specs=[VMEM] * 2, out...  46.6 us
    pallas_call x1, Pallas kernels, project_qkv(): pl.pallas_call(qkv_kernel, in_specs=[VMEM] * 6, out_specs=[VMEM, ANY], ou...  44.1 us
    pallas_call x1, Pallas kernels, attend(): pl.pallas_call(functools.partial(attend_kernel, blocks=blocks, size=seq /...  42.1 us
    ppermute x45, starting transfers between devices, dp_swap(): return lax.ppermute(values, 'dp', [(i, i ^ bits) for i in range(size)])  31.9 us
    dot_general x8, matrix products, dot(): return lax.dot_general(left, right, dims, preferred_element_type=f32)  30.4 us
  transfers between devices with their start and end apart: 47, of which 32 were waited for; matrix products, arithmetic and copies ran while one was open for 7% of the time, Pallas kernels for 0%

profile of v2, /device:TPU:24, one launch (start us, length us, event | category | flops | bytes accessed | tf_op | source)
XLA Modules:
  0.0 822.8 jit_solution(97821536631764355)
XLA Ops:
  23.7 44.1 %gather_project_qkv.1 = (bf16[2048,1024]{1,0:T(8,128)(2,1)}, bf16[4,512,1536]{2,1,0:T(8,128)(2,1)}) custom-call(bf16[512,1536]{1,0:T(8,128)(2,1)} %fusion.2.x_ref, bf16[1536,512]{1,0:T(8,128)(2,1)} %fusion.6.wq, bf16[1536,256]{1,0:T(8,128)(2,1)} %fusion.7.wk, bf16[1536,256]{1,0:T(8,128)(2,1)} %fusion.8.wv, f32[2048,128]{1,0:T(8,128)} %get-tuple-element.74.cos_ref, ...), custom_call_target="tpu_custom_call" | custom-call | flops 40000000000 | bytes 20000000 | tf_op jit(solution)/shard_map/gather_project_qkv/pallas_call | solution.py:195
  67.8 42.1 %attention.1 = (bf16[2048,512]{1,0:T(8,128)(2,1)}, f32[2,2,2048]{2,1,0:T(2,128)}, bf16[3,4,128,1536]{3,2,1,0:T(8,128)(2,1)}) custom-call(bf16[2048,1024]{1,0:T(8,128)(2,1)} %get-tuple-element.32.q_ref.k_ref.v_ref, bf16[2048,1024]{1,0:T(8,128)(2,1)} %get-tuple-element.32.q_ref.k_ref.v_ref, bf16[2048,1024]{1,0:T(8,128)(2,1)} %get-tuple-element.32.q_ref.k_ref.v_ref, ...), custom_call_target="tpu_custom_call" | custom-call | flops 8589934592 | bytes 12582912 | tf_op jit(solution)/shard_map/attention/pallas_call | solution.py:266
  109.9 168.9 %middle.1 = (f32[4,128,1536]{2,1,0:T(8,128)}, bf16[4,4,128,512]{3,2,1,0:T(8,128)(2,1)}, bf16[4,4,128,1536]{3,2,1,0:T(8,128)(2,1)}, f32[4,128,1536]{2,1,0:T(8,128...) custom-call(bf16[4,4,128,512]{3,2,1,0:T(8,128)(2,1)} %bitcast.42, ...), custom_call_target="tpu_custom_call" | custom-call | flops 149999992832 | bytes 80000000 | tf_op jit(solution)/shard_map/middle/pallas_call | solution.py:651
  280.2 52.1 %attention_back.1 = (bf16[2048,512]{1,0:T(8,128)(2,1)}, bf16[2048,256]{1,0:T(8,128)(2,1)}, bf16[2048,256]{1,0:T(8,128)(2,1)}, bf16[4,128,1536]{2,1,0:T(8,128)(2,1)}) custom-call(bf16[2048,1024]{1,0:T(8,128)(2,1)} %get-tuple-element.32.q_ref.k_ref.v_ref, bf16[2048,1024]{1,0:T(8,128)(2,1)} %get-tuple-element.32.q_ref.k_ref.v_ref, ...), custom_call_target="tpu_custom_call" | custom-call | flops 21474836480 | bytes 20971520 | tf_op jit(solution)/shard_map/attention_back/pallas_call | solution.py:394
  332.4 46.6 %end.1 = (f32[512,1536]{1,0:T(8,128)}, f32[8,1536]{1,0:T(8,128)}) custom-call(bf16[2048,512]{1,0:T(8,128)(2,1)} %get-tuple-element.40.dq, bf16[2048,256]{1,0:T(8,128)(2,1)} %get-tuple-element.41.dk, bf16[2048,256]{1,0:T(8,128)(2,1)} %get-tuple-element.42.dv, bf16[1536,512]{1,0:T(8,128)(2,1)} %fusion.6.wq, bf16[1536,256]{1,0:T(8,128)(2,1)} %fusion.7.wk, ...), custom_call_target="tpu_custom_call" | custom-call | flops 49999998976 | bytes 30000000 | tf_op jit(solution)/shard_map/end/pallas_call | solution.py:761
  380.7 8.3 %convolution_convert_fusion.3 = bf16[1536,384]{1,0:T(8,128)(2,1)S(1)} fusion(bf16[2048,1536]{1,0:T(8,128)(2,1)} %bitcast.38, bf16[2048,512]{1,0:T(8,128)(2,1)} %get-tuple-element.40.dq, s32[384]{0:T(512)} %copy-done.35, s32[384]{0:T(512)} %copy-done.37, s32[384]{0:T(512)} %copy-done.33, s32[384]{0:T(512)} %copy-done.39, pred[384]{0:T(512)(128)(4,1)} %copy-done.45, ...), kind=kOutput, calls=%fused_computation.19 | convolution fusion | flops 3223584768 | bytes 9575168 | tf_op jit(solution)/shard_map/dot_general | solution.py:28
  415.9 15.6 %collective-permute-done.2 = f32[2,1536]{1,0:T(2,128)S(1)} collective-permute-done((f32[2,1536]{1,0:T(2,128)S(1)}, f32[2,1536]{1,0:T(2,128)S(1)}, u32[]{:S(2)}, u32[]{:S(2)}) %collective-permute-start.2) | collective-permute-done | bytes 12320 | tf_op jit(solution)/shard_map/ppermute | solution.py:50
  499.3 11.0 %collective-permute-done.7 = bf16[192,384]{1,0:T(8,128)(2,1)S(1)} collective-permute-done((bf16[192,384]{1,0:T(8,128)(2,1)S(1)}, bf16[192,384]{1,0:T(8,128)(2,1)S(1)}, u32[]{:S(2)}, u32[]{:S(2)}) %collective-permute-start.7) | collective-permute-done | bytes 147488 | tf_op jit(solution)/shard_map/ppermute | solution.py:50
  510.4 7.2 collective-permute-done.25
  523.3 21.1 %collective-permute-done.41 = bf16[512,1536]{1,0:T(8,128)(2,1)S(1)} collective-permute-done((bf16[512,1536]{1,0:T(8,128)(2,1)S(1)}, bf16[512,1536]{1,0:T(8,128)(2,1)S(1)}, u32[]{:S(2)}, u32[]{:S(2)}) %collective-permute-start.41) | collective-permute-done | bytes 1572896 | tf_op jit(solution)/shard_map/ppermute | solution.py:50
  548.0 21.2 %collective-permute-done.36 = bf16[384,1024]{1,0:T(8,128)(2,1)S(1)} collective-permute-done((bf16[384,1024]{1,0:T(8,128)(2,1)S(1)}, bf16[384,1024]{1,0:T(8,128)(2,1)S(1)}, u32[]{:S(2)}, u32[]{:S(2)}) %collective-permute-start.36) | collective-permute-done | bytes 786464 | tf_op jit(solution)/shard_map/ppermute | solution.py:50
  569.5 19.3 %collective-permute-done.42 = bf16[256,1536]{1,0:T(8,128)(2,1)S(1)} collective-permute-done((bf16[256,1536]{1,0:T(8,128)(2,1)S(1)}, bf16[256,1536]{1,0:T(8,128)(2,1)S(1)}, u32[]{:S(2)}, u32[]{:S(2)}) %collective-permute-start.42) | collective-permute-done | bytes 786464 | tf_op jit(solution)/shard_map/ppermute | solution.py:50
  589.2 21.6 %collective-permute-done.31 = bf16[192,1024]{1,0:T(8,128)(2,1)S(1)} collective-permute-done((bf16[192,1024]{1,0:T(8,128)(2,1)S(1)}, bf16[192,1024]{1,0:T(8,128)(2,1)S(1)}, u32[]{:S(2)}, u32[]{:S(2)}) %collective-permute-start.31) | collective-permute-done | bytes 393248 | tf_op jit(solution)/shard_map/ppermute | solution.py:50
  611.0 16.7 %collective-permute-done.37 = bf16[192,1024]{1,0:T(8,128)(2,1)S(1)} collective-permute-done((bf16[192,1024]{1,0:T(8,128)(2,1)S(1)}, bf16[192,1024]{1,0:T(8,128)(2,1)S(1)}, u32[]{:S(2)}, u32[]{:S(2)}) %collective-permute-start.37) | collective-permute-done | bytes 393248 | tf_op jit(solution)/shard_map/ppermute | solution.py:50
  627.9 16.7 %collective-permute-done.43 = bf16[128,1536]{1,0:T(8,128)(2,1)S(1)} collective-permute-done((bf16[128,1536]{1,0:T(8,128)(2,1)S(1)}, bf16[128,1536]{1,0:T(8,128)(2,1)S(1)}, u32[]{:S(2)}, u32[]{:S(2)}) %collective-permute-start.43) | collective-permute-done | bytes 393248 | tf_op jit(solution)/shard_map/ppermute | solution.py:50
  644.7 12.6 %collective-permute-done.32 = bf16[192,1024]{1,0:T(8,128)(2,1)S(1)} collective-permute-done((bf16[192,1024]{1,0:T(8,128)(2,1)S(1)}, bf16[192,1024]{1,0:T(8,128)(2,1)S(1)}, u32[]{:S(2)}, u32[]{:S(2)}) %collective-permute-start.32) | collective-permute-done | bytes 393248 | tf_op jit(solution)/shard_map/ppermute | solution.py:50
  657.8 8.0 collective-permute-done.38
  673.8 13.5 %collective-permute-done.33 = bf16[384,1024]{1,0:T(8,128)(2,1)S(1)} collective-permute-done((bf16[384,1024]{1,0:T(8,128)(2,1)S(1)}, bf16[384,1024]{1,0:T(8,128)(2,1)S(1)}, u32[]{:S(2)}, u32[]{:S(2)}) %collective-permute-start.33) | collective-permute-done | bytes 786464 | tf_op jit(solution)/shard_map/ppermute | solution.py:50
  695.1 15.3 %collective-permute-done.39 = bf16[384,1024]{1,0:T(8,128)(2,1)S(1)} collective-permute-done((bf16[384,1024]{1,0:T(8,128)(2,1)S(1)}, bf16[384,1024]{1,0:T(8,128)(2,1)S(1)}, u32[]{:S(2)}, u32[]{:S(2)}) %collective-permute-start.39) | collective-permute-done | bytes 786464 | tf_op jit(solution)/shard_map/ppermute | solution.py:50
  712.6 10.9 %collective-permute-done.45 = bf16[256,1536]{1,0:T(8,128)(2,1)S(1)} collective-permute-done((bf16[256,1536]{1,0:T(8,128)(2,1)S(1)}, bf16[256,1536]{1,0:T(8,128)(2,1)S(1)}, u32[]{:S(2)}, u32[]{:S(2)}) %collective-permute-start.45) | collective-permute-done | bytes 786464 | tf_op jit(solution)/shard_map/ppermute | solution.py:50
  727.7 15.9 %collective-permute-done.10 = bf16[768,384]{1,0:T(8,128)(2,1)S(1)} collective-permute-done((bf16[768,384]{1,0:T(8,128)(2,1)S(1)}, bf16[768,384]{1,0:T(8,128)(2,1)S(1)}, u32[]{:S(2)}, u32[]{:S(2)}) %collective-permute-start.10) | collective-permute-done | bytes 589856 | tf_op jit(solution)/shard_map/ppermute | solution.py:50
  745.2 11.0 %collective-permute-done.28 = bf16[192,1536]{1,0:T(8,128)(2,1)S(1)} collective-permute-done((bf16[192,1536]{1,0:T(8,128)(2,1)S(1)}, bf16[192,1536]{1,0:T(8,128)(2,1)S(1)}, u32[]{:S(2)}, u32[]{:S(2)}) %collective-permute-start.28) | collective-permute-done | bytes 589856 | tf_op jit(solution)/shard_map/ppermute | solution.py:50
  761.4 28.5 %collective-permute-done.40 = bf16[768,1024]{1,0:T(8,128)(2,1)S(1)} collective-permute-done((bf16[768,1024]{1,0:T(8,128)(2,1)S(1)}, bf16[768,1024]{1,0:T(8,128)(2,1)S(1)}, u32[]{:S(2)}, u32[]{:S(2)}) %collective-permute-start.40) | collective-permute-done | bytes 1572896 | tf_op jit(solution)/shard_map/ppermute | solution.py:50
  793.3 21.8 %collective-permute-done.46 = bf16[512,1536]{1,0:T(8,128)(2,1)S(1)} collective-permute-done((bf16[512,1536]{1,0:T(8,128)(2,1)S(1)}, bf16[512,1536]{1,0:T(8,128)(2,1)S(1)}, u32[]{:S(2)}, u32[]{:S(2)}) %collective-permute-start.46) | collective-permute-done | bytes 1572896 | tf_op jit(solution)/shard_map/ppermute | solution.py:50
  (281 shorter events, 170.6 us)
Async XLA Ops:
  390.0 92.4 %collective-permute-start.5 = (bf16[768,384]{1,0:T(8,128)(2,1)}, bf16[768,384]{1,0:T(8,128)(2,1)}, u32[]{:S(2)}, u32[]{:S(2)}) collective-permute-start(bf16[768,384]{1,0:T(8,128)(2,1)} %constant_dynamic-slice_fusion.20), channel_id=1, source_target_pairs={{0,4},{4,0},{8,12},{12,8},{16,20},{20,16},{24,28},{28,24},{1,5},{5... | collective-permute-start | bytes 1769480 | tf_op jit(solution)/shard_map/ppermute | solution.py:50
  397.7 44.4 %collective-permute-start.11 = (bf16[768,192]{0,1:T(8,128)(2,1)}, bf16[768,192]{0,1:T(8,128)(2,1)S(1)}, u32[]{:S(2)}, u32[]{:S(2)}) collective-permute-start(bf16[768,192]{0,1:T(8,128)(2,1)} %constant_dynamic-slice_fusion.17), channel_id=1, source_target_pairs={{0,4},{4,0},{8,12},{12,8},{16,20},{20,16},{24,28},{28,24},{1,5},{5... | collective-permute-start | bytes 884744 | tf_op jit(solution)/shard_map/ppermute | solution.py:50
  404.2 39.5 %collective-permute-start.17 = (bf16[768,192]{0,1:T(8,128)(2,1)}, bf16[768,192]{0,1:T(8,128)(2,1)}, u32[]{:S(2)}, u32[]{:S(2)}) collective-permute-start(bf16[768,192]{0,1:T(8,128)(2,1)} %constant_dynamic-slice_fusion.14), channel_id=1, source_target_pairs={{0,4},{4,0},{8,12},{12,8},{16,20},{20,16},{24,28},{28,24},{1,5},{5... | collective-permute-start | bytes 884744 | tf_op jit(solution)/shard_map/ppermute | solution.py:50
  412.5 73.2 %collective-permute-start.23 = (bf16[192,1536]{1,0:T(8,128)(2,1)}, bf16[192,1536]{1,0:T(8,128)(2,1)}, u32[]{:S(2)}, u32[]{:S(2)}) collective-permute-start(bf16[192,1536]{1,0:T(8,128)(2,1)} %constant_dynamic-slice_fusion.11), channel_id=1, source_target_pairs={{0,4},{4,0},{8,12},{12,8},{16,20},{20,16},{24,28},{28,24},{1,5},{5... | collective-permute-start | bytes 1769480 | tf_op jit(solution)/shard_map/ppermute | solution.py:50
  439.9 78.2 %collective-permute-start.29 = (bf16[768,1024]{1,0:T(8,128)(2,1)}, bf16[768,1024]{1,0:T(8,128)(2,1)S(1)}, u32[]{:S(2)}, u32[]{:S(2)}) collective-permute-start(bf16[768,1024]{1,0:T(8,128)(2,1)} %constant_dynamic-slice_fusion.8), channel_id=1, source_target_pairs={{0,4},{4,0},{8,12},{12,8},{16,20},{20,16},{24,28},{28,24},{1,5},{5... | collective-permute-start | bytes 4718600 | tf_op jit(solution)/shard_map/ppermute | solution.py:50
  442.0 79.4 %collective-permute-start.35 = (bf16[768,1024]{1,0:T(8,128)(2,1)}, bf16[768,1024]{1,0:T(8,128)(2,1)S(1)}, u32[]{:S(2)}, u32[]{:S(2)}) collective-permute-start(bf16[768,1024]{1,0:T(8,128)(2,1)} %constant_dynamic-slice_fusion.5), channel_id=1, source_target_pairs={{0,4},{4,0},{8,12},{12,8},{16,20},{20,16},{24,28},{28,24},{1,5},{5... | collective-permute-start | bytes 4718600 | tf_op jit(solution)/shard_map/ppermute | solution.py:50
  488.1 56.4 %collective-permute-start.41 = (bf16[512,1536]{1,0:T(8,128)(2,1)S(1)}, bf16[512,1536]{1,0:T(8,128)(2,1)S(1)}, u32[]{:S(2)}, u32[]{:S(2)}) collective-permute-start(bf16[512,1536]{1,0:T(8,128)(2,1)S(1)} %copy-done.8), channel_id=1, source_target_pairs={{0,4},{4,0},{8,12},{12,8},{16,20},{20,16},{24,28},{28,24},{1,5},{5... | collective-permute-start | bytes 4718600 | tf_op jit(solution)/shard_map/ppermute | solution.py:50
  494.4 176.1 %collective-permute-start.16 = (bf16[768,192]{0,1:T(8,128)(2,1)S(1)}, bf16[768,192]{0,1:T(8,128)(2,1)S(1)}, u32[]{:S(2)}, u32[]{:S(2)}) collective-permute-start(bf16[768,192]{0,1:T(8,128)(2,1)S(1)} %maximum_select_fusion.16), channel_id=1, source_target_pairs={{0,4},{4,0},{8,12},{12,8},{16,20},{20,16},{24,28},{28,24},{1,5},{5... | collective-permute-start | bytes 884744 | tf_op jit(solution)/shard_map/ppermute | solution.py:50
  518.1 139.5 %collective-permute-start.26 = (bf16[48,1536]{1,0:T(8,128)(2,1)S(1)}, bf16[48,1536]{1,0:T(8,128)(2,1)S(1)}, u32[]{:S(2)}, u32[]{:S(2)}) collective-permute-start(bf16[48,1536]{1,0:T(8,128)(2,1)S(1)} %add_convert_fusion.15), channel_id=1, source_target_pairs={{0,16},{4,20},{8,24},{12,28},{16,0},{20,4},{24,8},{28,12},{1,17},{... | collective-permute-start | bytes 442376 | tf_op jit(solution)/shard_map/ppermute | solution.py:50
  545.4 43.5 %collective-permute-start.42 = (bf16[256,1536]{1,0:T(8,128)(2,1)S(1)}, bf16[256,1536]{1,0:T(8,128)(2,1)S(1)}, u32[]{:S(2)}, u32[]{:S(2)}) collective-permute-start(bf16[256,1536]{1,0:T(8,128)(2,1)S(1)} %constant_dynamic-slice_fusion.1), channel_id=1, source_target_pairs={{0,8},{4,12},{8,0},{12,4},{16,24},{20,28},{24,16},{28,20},{1,9},{5... | collective-permute-start | bytes 2359304 | tf_op jit(solution)/shard_map/ppermute | solution.py:50
  547.1 142.3 %collective-permute-start.9 = (bf16[384,384]{1,0:T(8,128)(2,1)S(1)}, bf16[384,384]{1,0:T(8,128)(2,1)S(1)}, u32[]{:S(2)}, u32[]{:S(2)}) collective-permute-start(bf16[384,384]{1,0:T(8,128)(2,1)S(1)} %maximum_select_fusion.15), channel_id=1, source_target_pairs={{0,8},{4,12},{8,0},{12,4},{16,24},{20,28},{24,16},{28,20},{1,9},{5... | collective-permute-start | bytes 884744 | tf_op jit(solution)/shard_map/ppermute | solution.py:50
  569.2 41.7 %collective-permute-start.31 = (bf16[192,1024]{1,0:T(8,128)(2,1)S(1)}, bf16[192,1024]{1,0:T(8,128)(2,1)S(1)}, u32[]{:S(2)}, u32[]{:S(2)}) collective-permute-start(bf16[192,1024]{1,0:T(8,128)(2,1)S(1)} %constant_dynamic-slice_fusion.6), channel_id=1, source_target_pairs={{0,16},{4,20},{8,24},{12,28},{16,0},{20,4},{24,8},{28,12},{1,17},{... | collective-permute-start | bytes 1179656 | tf_op jit(solution)/shard_map/ppermute | solution.py:50
  588.8 38.9 %collective-permute-start.37 = (bf16[192,1024]{1,0:T(8,128)(2,1)S(1)}, bf16[192,1024]{1,0:T(8,128)(2,1)S(1)}, u32[]{:S(2)}, u32[]{:S(2)}) collective-permute-start(bf16[192,1024]{1,0:T(8,128)(2,1)S(1)} %constant_dynamic-slice_fusion.3), channel_id=1, source_target_pairs={{0,16},{4,20},{8,24},{12,28},{16,0},{20,4},{24,8},{28,12},{1,17},{... | collective-permute-start | bytes 1179656 | tf_op jit(solution)/shard_map/ppermute | solution.py:50
  610.9 33.7 %collective-permute-start.43 = (bf16[128,1536]{1,0:T(8,128)(2,1)S(1)}, bf16[128,1536]{1,0:T(8,128)(2,1)S(1)}, u32[]{:S(2)}, u32[]{:S(2)}) collective-permute-start(bf16[128,1536]{1,0:T(8,128)(2,1)S(1)} %constant_dynamic-slice_fusion), channel_id=1, source_target_pairs={{0,16},{4,20},{8,24},{12,28},{16,0},{20,4},{24,8},{28,12},{1,17},{... | collective-permute-start | bytes 1179656 | tf_op jit(solution)/shard_map/ppermute | solution.py:50
  627.7 29.6 %collective-permute-start.32 = (bf16[192,1024]{1,0:T(8,128)(2,1)S(1)}, bf16[192,1024]{1,0:T(8,128)(2,1)S(1)}, u32[]{:S(2)}, u32[]{:S(2)}) collective-permute-start(bf16[192,1024]{1,0:T(8,128)(2,1)S(1)} %add_convert_fusion.10), channel_id=1, source_target_pairs={{0,16},{4,20},{8,24},{12,28},{16,0},{20,4},{24,8},{28,12},{1,17},{... | collective-permute-start | bytes 1179656 | tf_op jit(solution)/shard_map/ppermute | solution.py:50
  657.6 29.6 %collective-permute-start.33 = (bf16[384,1024]{1,0:T(8,128)(2,1)S(1)}, bf16[384,1024]{1,0:T(8,128)(2,1)S(1)}, u32[]{:S(2)}, u32[]{:S(2)}) collective-permute-start(bf16[384,1024]{1,0:T(8,128)(2,1)S(1)} %maximum_select_fusion.8), channel_id=1, source_target_pairs={{0,8},{4,12},{8,0},{12,4},{16,24},{20,28},{24,16},{28,20},{1,9},{5... | collective-permute-start | bytes 2359304 | tf_op jit(solution)/shard_map/ppermute | solution.py:50
  670.3 40.1 %collective-permute-start.39 = (bf16[384,1024]{1,0:T(8,128)(2,1)S(1)}, bf16[384,1024]{1,0:T(8,128)(2,1)S(1)}, u32[]{:S(2)}, u32[]{:S(2)}) collective-permute-start(bf16[384,1024]{1,0:T(8,128)(2,1)S(1)} %maximum_select_fusion.9), channel_id=1, source_target_pairs={{0,8},{4,12},{8,0},{12,4},{16,24},{20,28},{24,16},{28,20},{1,9},{5... | collective-permute-start | bytes 2359304 | tf_op jit(solution)/shard_map/ppermute | solution.py:50
  670.5 53.0 %collective-permute-start.45 = (bf16[256,1536]{1,0:T(8,128)(2,1)S(1)}, bf16[256,1536]{1,0:T(8,128)(2,1)S(1)}, u32[]{:S(2)}, u32[]{:S(2)}) collective-permute-start(bf16[256,1536]{1,0:T(8,128)(2,1)S(1)} %maximum_select_fusion.10), channel_id=1, source_target_pairs={{0,8},{4,12},{8,0},{12,4},{16,24},{20,28},{24,16},{28,20},{1,9},{5... | collective-permute-start | bytes 2359304 | tf_op jit(solution)/shard_map/ppermute | solution.py:50
  687.2 38.6 %collective-permute-start.22 = (bf16[768,192]{0,1:T(8,128)(2,1)S(1)}, bf16[768,192]{0,1:T(8,128)(2,1)S(1)}, u32[]{:S(2)}, u32[]{:S(2)}) collective-permute-start(bf16[768,192]{0,1:T(8,128)(2,1)S(1)} %maximum_select_fusion.17), channel_id=1, source_target_pairs={{0,4},{4,0},{8,12},{12,8},{16,20},{20,16},{24,28},{28,24},{1,5},{5... | collective-permute-start | bytes 884744 | tf_op jit(solution)/shard_map/ppermute | solution.py:50
  689.4 68.5 %collective-permute-start.34 = (bf16[768,1024]{1,0:T(8,128)(2,1)S(1)}, bf16[768,1024]{1,0:T(8,128)(2,1)S(1)}, u32[]{:S(2)}, u32[]{:S(2)}) collective-permute-start(bf16[768,1024]{1,0:T(8,128)(2,1)S(1)} %maximum_select_fusion.3), channel_id=1, source_target_pairs={{0,4},{4,0},{8,12},{12,8},{16,20},{20,16},{24,28},{28,24},{1,5},{5... | collective-permute-start | bytes 4718600 | tf_op jit(solution)/shard_map/ppermute | solution.py:50
  693.5 50.0 %collective-permute-start.10 = (bf16[768,384]{1,0:T(8,128)(2,1)S(1)}, bf16[768,384]{1,0:T(8,128)(2,1)S(1)}, u32[]{:S(2)}, u32[]{:S(2)}) collective-permute-start(bf16[768,384]{1,0:T(8,128)(2,1)S(1)} %maximum_select_fusion.11), channel_id=1, source_target_pairs={{0,4},{4,0},{8,12},{12,8},{16,20},{20,16},{24,28},{28,24},{1,5},{5... | collective-permute-start | bytes 1769480 | tf_op jit(solution)/shard_map/ppermute | solution.py:50
  710.4 45.8 %collective-permute-start.28 = (bf16[192,1536]{1,0:T(8,128)(2,1)S(1)}, bf16[192,1536]{1,0:T(8,128)(2,1)S(1)}, u32[]{:S(2)}, u32[]{:S(2)}) collective-permute-start(bf16[192,1536]{1,0:T(8,128)(2,1)S(1)} %maximum_select_fusion.14), channel_id=1, source_target_pairs={{0,4},{4,0},{8,12},{12,8},{16,20},{20,16},{24,28},{28,24},{1,5},{5... | collective-permute-start | bytes 1769480 | tf_op jit(solution)/shard_map/ppermute | solution.py:50
  723.5 66.4 %collective-permute-start.40 = (bf16[768,1024]{1,0:T(8,128)(2,1)S(1)}, bf16[768,1024]{1,0:T(8,128)(2,1)S(1)}, u32[]{:S(2)}, u32[]{:S(2)}) collective-permute-start(bf16[768,1024]{1,0:T(8,128)(2,1)S(1)} %maximum_select_fusion.4), channel_id=1, source_target_pairs={{0,4},{4,0},{8,12},{12,8},{16,20},{20,16},{24,28},{28,24},{1,5},{5... | collective-permute-start | bytes 4718600 | tf_op jit(solution)/shard_map/ppermute | solution.py:50
  725.9 89.3 %collective-permute-start.46 = (bf16[512,1536]{1,0:T(8,128)(2,1)S(1)}, bf16[512,1536]{1,0:T(8,128)(2,1)S(1)}, u32[]{:S(2)}, u32[]{:S(2)}) collective-permute-start(bf16[512,1536]{1,0:T(8,128)(2,1)S(1)} %maximum_select_fusion.5), channel_id=1, source_target_pairs={{0,4},{4,0},{8,12},{12,8},{16,20},{20,16},{24,28},{28,24},{1,5},{5... | collective-permute-start | bytes 4718600 | tf_op jit(solution)/shard_map/ppermute | solution.py:50
  (71 other events, 726.6 us)

commit v3 on v2

--- a/solution.py
+++ b/solution.py
@@ -40,49 +40,6 @@
     return pl.BlockSpec(shape, lambda *_: (0,) * len(shape), pipeline_mode=pl.Buffered(1))
 
 
-def swap(values, bits):
-    size = lax.axis_size("tensor")
-    return lax.ppermute(values, "tensor", [(i, i ^ bits) for i in range(size)])
-
-
-def dp_swap(values, bits):
-    size = lax.axis_size("dp")
-    return lax.ppermute(values, "dp", [(i, i ^ bits) for i in range(size)])
-
-
-def dp_sum(values):
-    size, index = lax.axis_size("dp"), lax.axis_index("dp")
-    rows = values.shape[0]
-    piece = values
-    bit = 1
-    while bit < size:
-        half = piece.shape[0] // 2
-        mine = (index // bit) % 2
-        send = lax.dynamic_slice_in_dim(piece, (1 - mine) * half, half, 0)
-        keep = lax.dynamic_slice_in_dim(piece, mine * half, half, 0)
-        got = dp_swap(send, bit)
-        piece = (keep.astype(f32) + got.astype(f32)).astype(bf16)
-        bit *= 2
-    while bit > 1:
-        bit //= 2
-        mine = (index // bit) % 2
-        got = dp_swap(piece, bit)
-        piece = jnp.where(mine == 0, jnp.concatenate([piece, got], 0), jnp.concatenate([got, piece], 0))
-    return piece.astype(f32)
-
-
-def all_sum(values):
-    bit = 1
-    while bit < lax.axis_size("tensor"):
-        values = values + swap(values, bit)
-        bit *= 2
-    bit = 1
-    while bit < lax.axis_size("dp"):
-        values = values + dp_swap(values, bit)
-        bit *= 2
-    return values
-
-
 ANY = pl.BlockSpec(memory_space=pl.ANY)
 VMEM = pl.BlockSpec(memory_space=pltpu.VMEM)
 
@@ -112,11 +69,141 @@
     )
 
 
-def meet():
+def meet(*others):
     barrier = pltpu.get_barrier_semaphore()
-    for bits in (1, 2):
-        pl.semaphore_signal(barrier, inc=1, device_id=partner(bits), device_id_type=pl.DeviceIdType.MESH)
-    pl.semaphore_wait(barrier, 2)
+    for other in others:
+        pl.semaphore_signal(barrier, inc=1, device_id=other, device_id_type=pl.DeviceIdType.MESH)
+    pl.semaphore_wait(barrier, len(others))
+
+
+RING = 8
+EARLY = 4
+
+
+def ring_place():
+    index = lax.axis_index("dp")
+    deep, wide = lax.div(index, 2), lax.rem(index, 2)
+    return deep + wide * (RING - 1 - 2 * deep)
+
+
+def ring_peer(way):
+    place = lax.rem(ring_place() + (1, RING - 1)[way], RING)
+    wide = lax.div(place, RING // 2)
+    return {"dp": 2 * (place + wide * (RING - 1 - 2 * place)) + wide}
+
+
+def ring_chunk(way, step):
+    return lax.rem(ring_place() + (2 * RING - step if way == 0 else step), RING)
+
+
+def ring_send(source, target, sems, at, way):
+    return pltpu.make_async_remote_copy(
+        src_ref=source,
+        dst_ref=target,
+        send_sem=sems[0].at[at],
+        recv_sem=sems[1].at[at],
+        device_id=ring_peer(way),
+        device_id_type=pl.DeviceIdType.MESH,
+    )
+
+
+class Reduce:
+    def __init__(self, parts, state, land, mine, first, last, send_sem, recv_sem, load_sem):
+        self.parts, self.state, self.land, self.mine = parts, state, land, mine
+        self.first, self.last, self.sems, self.load_sem = first, last, (send_sem, recv_sem), load_sem
+
+    def begin(self, way):
+        source = self.parts.at[way, ring_chunk(way, 0)] if self.state is None else self.state.at[way]
+        return ring_send(source, self.land.at[way, 0], self.sems, (way, 0), way)
+
+    def copy(self, way, k):
+        return ring_send(self.land.at[way, k - 1], self.land.at[way, k], self.sems, (way, k), way)
+
+    def load(self, way, k):
+        source = self.parts.at[way, ring_chunk(way, self.first + k + 1)]
+        return pltpu.make_async_copy(source, self.mine.at[way, k], self.load_sem.at[way, k])
+
+    def start(self):
+        for way in range(2):
+            self.begin(way).start()
+
+    def prefetch(self):
+        for k in range(self.last - self.first):
+            for way in range(2):
+                self.load(way, k).start()
+
+    def step(self, k):
+        for way in range(2):
+            self.landed(way, k)
+            if self.mine is None:
+                own = self.parts[way, ring_chunk(way, self.first + k + 1)]
+            else:
+                self.load(way, k).wait()
+                own = self.mine[way, k]
+            self.land[way, k] = (self.land[way, k].astype(f32) + own.astype(f32)).astype(bf16)
+            if isinstance(k, int):
+                if k + 1 < self.last - self.first:
+                    self.copy(way, k + 1).start()
+            else:
+
+                @pl.when(k + 1 < self.last - self.first)
+                def _():
+                    self.copy(way, k + 1).start()
+
+    def landed(self, way, k):
+        ring_send(self.land.at[way, k], self.land.at[way, k], self.sems, (way, k), way).wait_recv()
+
+    def finish(self):
+        for way in range(2):
+            self.begin(way).wait_send()
+            for k in range(1, self.last - self.first):
+                self.copy(way, k).wait_send()
+
+
+class Spread:
+    def __init__(self, reduced, full, send_sem, recv_sem, own_sem):
+        self.reduced, self.full, self.sems, self.own_sem = reduced, full, (send_sem, recv_sem), own_sem
+
+    def slot(self, way, step):
+        return self.full.at[way, ring_chunk(way, step + RING - 1)]
+
+    def begin(self, way):
+        last = self.reduced.last - self.reduced.first - 1
+        return ring_send(self.reduced.land.at[way, last], self.slot(way, 0), self.sems, (way, 0), way)
+
+    def keep(self, way):
+        last = self.reduced.last - self.reduced.first - 1
+        return pltpu.make_async_copy(self.reduced.land.at[way, last], self.slot(way, 0), self.own_sem.at[way])
+
+    def start(self):
+        for way in range(2):
+            self.begin(way).start()
+            self.keep(way).start()
+
+    def copy(self, way, k):
+        return ring_send(self.slot(way, k), self.slot(way, k), self.sems, (way, k), way)
+
+    def step(self, k):
+        for way in range(2):
+            ring_send(self.slot(way, k + 1), self.slot(way, k + 1), self.sems, (way, k), way).wait_recv()
+
+            @pl.when(k < RING - 2)
+            def _():
+                self.copy(way, k + 1).start()
+
+    def finish(self):
+        for way in range(2):
+            self.begin(way).wait_send()
+            self.keep(way).wait()
+            for k in range(1, RING - 1):
+                self.copy(way, k).wait_send()
+
+
+def ring_scratch(shape, steps, loads):
+    rows, cols = shape[2:]
+    land = pltpu.VMEM((2, steps, rows, cols), bf16)
+    sems = [pltpu.SemaphoreType.DMA((2, steps))] * (3 if loads else 2)
+    return [land] * (2 if loads else 1) + sems
 
 
 def comm_params(number):
@@ -155,7 +242,7 @@
     onward = lambda k: send(land.at[1, piece(k)], land.at[2, piece(k)], sems, CHUNKS + k, 1)
     store = lambda p: pltpu.make_async_copy(x_ref if p == 0 else land.at[p - 1], stack_ref.at[p], out_sem.at[p])
 
-    meet()
+    meet(partner(1), partner(2))
     side.start()
     for k in range(CHUNKS):
         across(k).start()
@@ -214,7 +301,7 @@
 
     @pl.when(pl.program_id(0) == 0)
     def _():
-        meet()
+        meet(partner(1), partner(2))
         side.start()
         for k in range(CHUNKS):
             across(k).start()
@@ -290,24 +377,47 @@
     )(qkv, qkv, qkv, start, cot.reshape(pieces))
 
 
-def attend_back_kernel(
-    q_ref, k_ref, v_ref, o_ref, do_ref, lse_ref, start_ref, cos_ref, sin_ref, parts, hid1,
-    dq_ref, dk_ref, dv_ref, out_ref, dq_sum, dk_sum, dv_sum, inner, mine, side, across, send_sem, recv_sem, load_sem,
-    *, blocks, size,
-):
-    pieces = parts.shape[0]
-    sems = (send_sem, recv_sem)
-    from_side = [send(parts.at[:, 3 - 2 * k], side.at[k], sems, k, 1) for k in range(2)]
-    from_across = send(mine.at[0], across, sems, 2, 2)
-    load = [pltpu.make_async_copy(parts.at[:, 2 - 2 * k], mine.at[k], load_sem.at[k]) for k in range(2)]
-
-    @pl.when(pl.program_id(0) == 0)
-    def _():
-        load[0].start()
-        load[1].start()
-        meet()
-        from_side[0].start()
-        from_side[1].start()
+def attend_back_kernel(count, *refs, blocks, size):
+    q_ref, k_ref, v_ref, o_ref, do_ref, lse_ref, start_ref, cos_ref, sin_ref, *rest = refs
+    parts, rest = rest[:count], rest[count:]
+    dq_ref, dk_ref, dv_ref, *rest = rest
+    states, rest = rest[:count], rest[count:]
+    dq_sum, dk_sum, dv_sum, inner, *rest = rest
+    rings = [Reduce(p, None, *rest[5 * a : 5 * a + 2], 0, EARLY, *rest[5 * a + 2 : 5 * a + 5]) for a, p in enumerate(parts)]
+    keep_sem = rest[-1] if count else None
+
+    def keep(a, way):
+        return pltpu.make_async_copy(rings[a].land.at[way, EARLY - 1], states[a].at[way], keep_sem.at[a, way])
+
+    if count:
+
+        @pl.when(pl.program_id(0) == 0)
+        def _():
+            meet(ring_peer(0), ring_peer(1))
+            for ring in rings:
+                ring.start()
+            for ring in rings:
+                ring.prefetch()
+
+    pairs = blocks * (blocks + 1) // 2
+    hooks = {}
+    for number in range(count * EARLY):
+        hooks[min(round((number + 1) * 2.2) + 1, 2 * pairs - 1)] = hooks.get(min(round((number + 1) * 2.2) + 1, 2 * pairs - 1), []) + [
+            (number % count, number // count)
+        ]
+
+    def hook(pair):
+        for half in range(2):
+            todo = hooks.get(half * pairs + pair, [])
+            if todo:
+
+                @pl.when(pl.program_id(0) == half)
+                def _():
+                    for a, k in todo:
+                        rings[a].step(k)
+                        if k == EARLY - 1:
+                            keep(a, 0).start()
+                            keep(a, 1).start()
 
     for c in range(blocks):
         rows = slice(c * size, (c + 1) * size)
@@ -316,16 +426,6 @@
             product = do_ref[rows, cols].astype(f32) * o_ref[rows, cols].astype(f32)
             inner[r : r + 1, rows] = jnp.sum(product.T, axis=0, keepdims=True)
     for i in reversed(range(blocks)):
-        if i == blocks - 2:
-
-            @pl.when(pl.program_id(0) == 0)
-            def _():
-                load[0].wait()
-                from_side[0].wait_recv()
-                for k in range(pieces):
-                    mine[0, k] = (mine[0, k].astype(f32) + side[0, k].astype(f32)).astype(bf16)
-                from_across.start()
-
         for j in [i, *range(i)]:
             at = pl.multiple_of(peer(i) * size, size)
             key_at = pl.multiple_of(peer(j) * size, size)
@@ -360,6 +460,7 @@
             else:
                 dk_sum[pl.ds(key_at, size), :] += dk
                 dv_sum[pl.ds(key_at, size), :] += dv
+            hook(sum(range(blocks, i + 1, -1)) + (0 if j == i else j + 1))
     for c in range(blocks):
         rows = slice(c * size, (c + 1) * size)
         cos, sin = cos_ref[rows, :], sin_ref[rows, :]
@@ -373,26 +474,24 @@
         dk_ref[rows, :] = back(dk_sum[rows, :])
         dv_ref[rows, :] = dv_sum[rows, :].astype(bf16)
 
-    @pl.when(pl.program_id(0) == 1)
-    def _():
-        load[1].wait()
-        from_side[1].wait_recv()
-        from_across.wait()
-        from_side[0].wait_send()
-        from_side[1].wait_send()
-        for k in range(pieces):
-            term = mine[1, k].astype(f32) + side[1, k].astype(f32) + across[k].astype(f32)
-            out_ref[k] = (hid1[k] + term).astype(bf16)
-
-
-def attend_back(qkv, attended, grads, lse, start, cos, sin, parts, hid1, blocks):
+    if count:
+
+        @pl.when(pl.program_id(0) == 1)
+        def _():
+            for a, ring in enumerate(rings):
+                ring.finish()
+                keep(a, 0).wait()
+                keep(a, 1).wait()
+
+
+def attend_back(qkv, attended, grads, lse, start, cos, sin, parts, blocks):
     seq = qkv.shape[0]
-    own = hid1.shape
     pair = pl.BlockSpec((seq, 2 * LANES), lambda g: (0, g))
     single = pl.BlockSpec((seq, LANES), lambda g: (0, g))
     table = pl.BlockSpec((seq, LANES), lambda g: (0, 0))
-    return pl.pallas_call(
-        functools.partial(attend_back_kernel, blocks=blocks, size=seq // blocks),
+    count = len(parts)
+    outs = pl.pallas_call(
+        functools.partial(attend_back_kernel, count, blocks=blocks, size=seq // blocks),
         grid=(2,),
         in_specs=[
             pair,
@@ -404,31 +503,28 @@
             pl.BlockSpec((1, seq), lambda g: (0, 0)),
             table,
             table,
-            ANY,
-            whole(own),
+            *[ANY] * count,
         ],
-        out_specs=[pair, single, single, whole(own)],
+        out_specs=[pair, single, single, *[ANY] * count],
         scratch_shapes=[
             pltpu.VMEM((seq, 2 * LANES), f32),
             pltpu.VMEM((seq, LANES), f32),
             pltpu.VMEM((seq, LANES), f32),
             pltpu.VMEM((2, seq), f32),
-            pltpu.VMEM((2, *own), bf16),
-            pltpu.VMEM((2, *own), bf16),
-            pltpu.VMEM(own, bf16),
-            *dma_sems(3),
-            pltpu.SemaphoreType.DMA((2,)),
+            *[x for p in parts for x in ring_scratch(p.shape, EARLY, True)],
+            *[pltpu.SemaphoreType.DMA((count, 2))] * bool(count),
         ],
         out_shape=[
             jax.ShapeDtypeStruct((seq, 4 * LANES), bf16),
             jax.ShapeDtypeStruct((seq, 2 * LANES), bf16),
             jax.ShapeDtypeStruct((seq, 2 * LANES), bf16),
-            jax.ShapeDtypeStruct(own, bf16),
+            *[jax.ShapeDtypeStruct((2, *p.shape[2:]), bf16) for p in parts],
         ],
-        compiler_params=comm_params(5),
+        compiler_params=comm_params(5) if count else params(),
         cost_estimate=cost(5 * 2 * 4 * LANES * seq * seq, 10 * seq * 8 * LANES),
         name="attention_back",
-    )(qkv, qkv, qkv, attended, grads, lse, start, cos, sin, parts, hid1)
+    )(qkv, qkv, qkv, attended, grads, lse, start, cos, sin, *parts)
+    return outs[:3], outs[3:]
 
 
 RS1_C0, RS1_C1, RS1_X, AG2_X, AG2_C, AG2_F, RS3_C0, RS3_C1, RS3_X, AG3_X, AG3_C, AG3_F = range(12)
@@ -477,7 +573,7 @@
 
     for p in range(4):
         cot_copy(p).start()
-    meet()
+    meet(partner(1), partner(2))
 
     @pl.loop(0, pieces)
     def _(k):
@@ -693,12 +789,28 @@
     )
 
 
-def end_kernel(
-    dq, dk, dv, wq, wk, wv, tokens, grad_one, gain, grad_ref, gain_grad, parts, cr, xr, send_sem, recv_sem
-):
+def rows_back(grad, inputs, gain):
+    inverse = lax.rsqrt(jnp.mean(inputs * inputs, axis=-1, keepdims=True) + epsilon)
+    unit = inputs * inverse
+    scaled = grad * gain
+    back = inverse * (scaled - unit * jnp.mean(scaled * unit, axis=-1, keepdims=True))
+    return back, jnp.sum((grad * unit).reshape(-1, 8, grad.shape[-1]), axis=0)
+
+
+def end_kernel(count, *refs):
+    refs = list(refs)
+    take = lambda n: [refs.pop(0) for _ in range(n)]
+    dq, dk, dv, wq, wk, wv, tokens, grad_one, gain, attn_in, merge, gain_two, hid1, parts_in = take(14)
+    parts, states, dwo = take(count), take(count), take(1 if count else 0)
+    grad_ref, gains_ref, out_ref = take(3)
+    fulls = take(count + 2 if count else 0)
+    dwqkv_out = take(0 if count else 1)
+    terms, cr, xr, out_mine, out_side, out_across, gain_sum, gain_land, dwqkv = take(9)
+    send_sem, recv_sem, load_sem, gain_send, gain_recv = take(5)
     own, width = tokens.shape
     rows = own // CHUNKS
     sems = (send_sem, recv_sem)
+    gain_sems = (gain_send, gain_recv)
 
     def at(base, k):
         return pl.ds(pl.multiple_of(base + k * rows, rows), rows)
@@ -707,26 +819,96 @@
         here = at(p * own, k)
         return dot(dq[here], wq[...], NT) + dot(dk[here], wk[...], NT) + dot(dv[here], wv[...], NT)
 
-    side0 = lambda k: send(parts.at[at(0, k)], cr.at[0, at(0, k)], sems, (0, k), 1)
-    side1 = lambda k: send(parts.at[at(own, k)], cr.at[1, at(0, k)], sems, (1, k), 1)
-    across = lambda k: send(parts.at[at(2 * own, k)], xr.at[at(0, k)], sems, (2, k), 2)
-
-    meet()
+    side0 = lambda k: send(terms.at[at(0, k)], cr.at[0, at(0, k)], sems, (0, k), 1)
+    side1 = lambda k: send(terms.at[at(own, k)], cr.at[1, at(0, k)], sems, (1, k), 1)
+    across = lambda k: send(terms.at[at(2 * own, k)], xr.at[at(0, k)], sems, (2, k), 2)
+    out_load = [pltpu.make_async_copy(parts_in.at[:, 2 - 2 * k], out_mine.at[k], load_sem.at[k]) for k in range(2)]
+    out_from_side = [send(parts_in.at[:, 3 - 2 * k], out_side.at[k], sems, (3, k), 1) for k in range(2)]
+    out_from_across = send(out_mine.at[0], out_across, sems, (3, 2), 2)
+
+    if count:
+        reduces, rest = [], take(5 * count)
+        for a in range(count):
+            land, mine, *own_sems = rest[5 * a : 5 * a + 5]
+            reduces.append(Reduce(parts[a], states[a], land, mine, EARLY, RING - 1, *own_sems))
+        land, mine, *own_sems = take(5)
+        late = [Reduce(dwo[0], None, land, mine, 0, RING - 1, *own_sems)]
+        land, *own_sems = take(3)
+        late.append(Reduce(dwqkv, None, land, None, 0, RING - 1, *own_sems, None))
+        spreads = [Spread(r, full, *take(3)) for r, full in zip([*reduces, *late], fulls)]
+        early_spreads, late_spreads = spreads[:count], spreads[count:]
+        dp = lax.axis_index("dp")
+        flip = lambda bit: {"dp": dp + bit - 2 * bit * lax.rem(lax.div(dp, bit), 2)}
+        meet(partner(1), partner(2), ring_peer(0), ring_peer(1), flip(1), flip(2), flip(4))
+        for ring in (*reduces, late[0]):
+            ring.start()
+        for ring in (*reduces, late[0]):
+            ring.prefetch()
+    else:
+        meet(partner(1), partner(2))
+    for k in range(2):
+        out_load[k].start()
+        out_from_side[k].start()
 
     @pl.loop(0, CHUNKS)
     def _(k):
-        parts[at(0, k)] = term(3, k).astype(bf16)
+        terms[at(0, k)] = term(3, k).astype(bf16)
         side0(k).start()
         mine = term(2, k)
         side0(k).wait_recv()
-        parts[at(2 * own, k)] = (mine + cr[0, at(0, k)].astype(f32)).astype(bf16)
+        terms[at(2 * own, k)] = (mine + cr[0, at(0, k)].astype(f32)).astype(bf16)
         across(k).start()
 
+    chunk = dwqkv.shape[2]
+
+    def weight_rows(k, size):
+        part = attn_in[:, pl.ds(pl.multiple_of(k * size, size), size)]
+        padded = jnp.concatenate([dot(part, d[...], TN).astype(bf16) for d in (dq, dk, dv)], axis=1)
+        return dot(padded, merge[...], NT).astype(bf16)
+
+    @pl.loop(0, width // 384)
+    def _(k):
+        block = weight_rows(k, 384)
+        for i in range(384 // chunk):
+            number = k * (384 // chunk) + i
+            dwqkv[lax.div(number, RING), lax.rem(number, RING)] = block[i * chunk : (i + 1) * chunk]
+
+    if count:
+        late[1].start()
+    else:
+        stored = pltpu.make_async_copy(dwqkv, dwqkv_out[0], load_sem.at[2])
+        stored.start()
+        stored.wait()
+
     @pl.loop(0, CHUNKS)
     def _(k):
-        parts[at(own, k)] = term(1, k).astype(bf16)
+        terms[at(own, k)] = term(1, k).astype(bf16)
         side1(k).start()
         grad_ref[at(0, k)] = term(0, k)
+
+    out_load[0].wait()
+    out_from_side[0].wait_recv()
+
+    @pl.loop(0, CHUNKS)
+    def _(k):
+        out_mine[0, k] = (out_mine[0, k].astype(f32) + out_side[0, k].astype(f32)).astype(bf16)
+
+    out_from_across.start()
+
+    if count:
+
+        @pl.loop(0, RING - 1 - EARLY)
+        def _(k):
+            for ring in reduces:
+                ring.step(k)
+            for ring in late:
+                ring.step(k)
+
+        for ring in early_spreads:
+            ring.start()
+
+    gain_sum[...] = jnp.zeros_like(gain_sum)
+    gain_sum[1:2] = jnp.sum(gain_two[...], axis=0, keepdims=True)
 
     @pl.loop(0, CHUNKS)
     def _(k):
@@ -734,20 +916,73 @@
         across(k).wait_recv()
         here = at(0, k)
         grad = grad_ref[here] + cr[1, here].astype(f32) + xr[here].astype(f32)
-        inputs = tokens[here].astype(f32)
-        inverse = lax.rsqrt(jnp.mean(inputs * inputs, axis=-1, keepdims=True) + epsilon)
-        unit = inputs * inverse
-        scaled = grad * gain[...]
-        grad_ref[here] = grad_one[here] + inverse * (scaled - unit * jnp.mean(scaled * unit, axis=-1, keepdims=True))
-        sums = jnp.sum((grad * unit).reshape(-1, 8, width), axis=0)
-
-        @pl.when(k == 0)
-        def _():
-            gain_grad[...] = sums
-
-        @pl.when(k > 0)
-        def _():
-            gain_grad[...] += sums
+        back, sums = rows_back(grad, tokens[here].astype(f32), gain[...])
+        grad_ref[here] = grad_one[here] + back
+        gain_sum[0:1] += jnp.sum(sums, axis=0, keepdims=True)
+
+    def gain_copy(stage):
+        to = [partner(1), partner(2)] + ([flip(1), flip(2), flip(4)] if count else [])
+        return pltpu.make_async_remote_copy(
+            src_ref=gain_sum,
+            dst_ref=gain_land.at[stage],
+            send_sem=gain_send.at[stage],
+            recv_sem=gain_recv.at[stage],
+            device_id=to[stage],
+            device_id_type=pl.DeviceIdType.MESH,
+        )
+
+    def gain_add(stage):
+        gain_copy(stage).wait()
+        gain_sum[...] += gain_land[stage]
+
+    gain_copy(0).start()
+    if count:
+
+        @pl.loop(0, EARLY)
+        def _(k):
+            for ring in early_spreads:
+                ring.step(k)
+            for ring in late:
+                ring.step(RING - 1 - EARLY + k)
+
+        for ring in late_spreads:
+            ring.start()
+    gain_add(0)
+    gain_copy(1).start()
+    out_load[1].wait()
+    out_from_side[1].wait_recv()
+    out_from_across.wait_recv()
+
+    @pl.loop(0, CHUNKS)
+    def _(k):
+        total = out_mine[1, k].astype(f32) + out_side[1, k].astype(f32) + out_across[k].astype(f32)
+        out_ref[k] = (hid1[k] + total).astype(bf16)
+
+    gain_add(1)
+    if count:
+        gain_copy(2).start()
+
+        @pl.loop(0, RING - 1 - EARLY)
+        def _(k):
+            for ring in early_spreads:
+                ring.step(EARLY + k)
+            for ring in late_spreads:
+                ring.step(k)
+
+        gain_add(2)
+        gain_copy(3).start()
+        gain_add(3)
+        gain_copy(4).start()
+
+        @pl.loop(RING - 1 - EARLY, RING - 1)
+        def _(k):
+            for ring in late_spreads:
+                ring.step(k)
+
+        gain_add(4)
+        for ring in (*reduces, *late, *spreads):
+            ring.finish()
+    gains_ref[...] = gain_sum[...]
 
     @pl.loop(0, CHUNKS)
     def _(k):
@@ -755,24 +990,58 @@
         side1(k).wait_send()
         across(k).wait_send()
 
-
-def end(dq, dk, dv, wq, wk, wv, tokens, grad_one, gain):
+    for k in range(2):
+        out_from_side[k].wait_send()
+    out_from_across.wait_send()
+
+
+def end(dq, dk, dv, wq, wk, wv, tokens, grad_one, gain, attn_in, merge, gain_two, hid1, parts_in, parts, states, dwo):
     own, width = tokens.shape
-    return pl.pallas_call(
-        end_kernel,
-        in_specs=[VMEM] * 9,
-        out_specs=[VMEM] * 2,
-        out_shape=[jax.ShapeDtypeStruct((own, width), f32), jax.ShapeDtypeStruct((8, width), f32)],
+    heads = merge.shape[0]
+    count = len(parts)
+    sds = jax.ShapeDtypeStruct
+    pieces = hid1.shape
+    qkv_shape = (2, RING, width // (2 * RING), heads)
+    late = [dwo] if count else []
+    ring_shapes = [*[p.shape for p in parts], dwo.shape, qkv_shape] if count else []
+    ring_buffers = []
+    for p in parts:
+        ring_buffers += ring_scratch(p.shape, RING - 1 - EARLY, True)
+    if count:
+        ring_buffers += ring_scratch(dwo.shape, RING - 1, True) + ring_scratch(qkv_shape, RING - 1, False)
+        for _ in ring_shapes:
+            ring_buffers += [pltpu.SemaphoreType.DMA((2, RING - 1))] * 2 + [pltpu.SemaphoreType.DMA((2,))]
+    stages = 5 if count else 2
+    outs = pl.pallas_call(
+        functools.partial(end_kernel, count),
+        in_specs=[VMEM] * 13 + [ANY] * (1 + 2 * count + len(late)),
+        out_specs=[VMEM] * 3 + [ANY] * (len(ring_shapes) or 1),
+        out_shape=[
+            sds((own, width), f32),
+            sds((8, width), f32),
+            sds(pieces, bf16),
+            *[sds(shape, bf16) for shape in (ring_shapes or [qkv_shape])],
+        ],
         scratch_shapes=[
             pltpu.VMEM((3 * own, width), bf16),
             pltpu.VMEM((2, own, width), bf16),
             pltpu.VMEM((own, width), bf16),
-            *dma_sems(3, CHUNKS),
+            pltpu.VMEM((2, *pieces), bf16),
+            pltpu.VMEM((2, *pieces), bf16),
+            pltpu.VMEM(pieces, bf16),
+            pltpu.VMEM((8, width), f32),
+            pltpu.VMEM((stages, 8, width), f32),
+            pltpu.VMEM(qkv_shape, bf16),
+            *dma_sems(4, max(CHUNKS, 3)),
+            pltpu.SemaphoreType.DMA((3,)),
+            *dma_sems(stages),
+            *ring_buffers,
         ],
         compiler_params=comm_params(3),
-        cost_estimate=cost(50e-6 * 1e15, 30e6),
+        cost_estimate=cost(150e-6 * 1e15, 60e6),
         name="end",
-    )(dq, dk, dv, wq, wk, wv, tokens, grad_one, gain)
+    )(dq, dk, dv, wq, wk, wv, tokens, grad_one, gain, attn_in, merge, gain_two, hid1, parts_in, *parts, *states, *late)
+    return outs[:3], outs[3:]
 
 
 def spread(heads):
@@ -818,24 +1087,31 @@
 
     qkv, attn_in = project_qkv(normed_one, wq, wk, wv, cos, sin)
     attended, lse, cots = attend(qkv, start, cotangent, blocks)
-    hid1, grad_attended, parts, grad_one, dwd, dwg, dwu, dwo, gain_two_grad = middle(
+    hid1, grad_attended, parts, grad_one, dwd, dwg, dwu, dwo, gain_two = middle(
         attended, wo, tokens, gain_mlp, cotangent, cots, w_gate, w_up, w_down
     )
     grad_attended = grad_attended.reshape(seq, -1)
-    dq, dk, dv, output = attend_back(
-        qkv, attended, grad_attended, lse, start, cos, sin, parts, hid1, blocks
+    dwo = dot(spread_q, dwo).astype(bf16)
+    ringed = lax.axis_size("dp") == RING
+    chunks = lambda t: t.reshape(2, RING, t.shape[0] // (2 * RING), t.shape[1])
+    early = [chunks(t) for t in (dwd, dwg, dwu)] if ringed else []
+    (dq, dk, dv), states = attend_back(qkv, attended, grad_attended, lse, start, cos, sin, early, blocks)
+    (grad_tokens, gains, output), sums = end(
+        dq, dk, dv, wq, wk, wv, tokens, grad_one.reshape(own, width), gain_attn, attn_in.reshape(seq, width),
+        spread(8), gain_two, hid1, parts, early, states, chunks(dwo) if ringed else None,
     )
     output = output.reshape(own, width)
-    attn_in = attn_in.reshape(seq, width)
-    grad_w_down, grad_w_gate, grad_w_up = dp_sum(dwd), dp_sum(dwg), dp_sum(dwu)
-    grad_w_out = dp_sum(dot(spread_q, dwo).astype(bf16))
-    grad_w_query = dp_sum(dot(attn_in, dot(dq, spread_q, NT).astype(bf16), TN).astype(bf16))
-    grad_w_key = dp_sum(dot(attn_in, dot(dk, spread_k, NT).astype(bf16), TN).astype(bf16))
-    grad_w_value = dp_sum(dot(attn_in, dot(dv, spread_k, NT).astype(bf16), TN).astype(bf16))
-    grad_tokens, gain_one_grad = end(dq, dk, dv, wq, wk, wv, tokens, grad_one.reshape(own, width), gain_attn)
-
-    gains = jnp.stack([jnp.sum(gain_one_grad, 0), jnp.sum(gain_two_grad, 0)])
-    gains = all_sum(gains)
+    if not ringed:
+        gains = lax.psum(gains, "dp")
+        sums = [lax.psum(t, "dp") for t in (dwd, dwg, dwu, dwo, sums[0])]
+    sums = [t.reshape(shape).astype(f32) for t, shape in zip(sums, (
+        w_down.shape, w_gate.shape, w_up.shape, w_out.shape, (width, spread(8).shape[0])
+    ))]
+    grad_w_down, grad_w_gate, grad_w_up, grad_w_out, grad_w_qkv = sums
+    heads_q, heads_k = w_query.shape[1], key_weight.shape[1]
+    grad_w_query = grad_w_qkv[:, :heads_q]
+    grad_w_key = grad_w_qkv[:, heads_q : heads_q + heads_k]
+    grad_w_value = grad_w_qkv[:, heads_q + heads_k :]
     return (
         output, grad_tokens, gains[0], grad_w_query, grad_w_key, grad_w_value, grad_w_out,
         gains[1], grad_w_gate, grad_w_up, grad_w_down,

time: 830 us -> 609 us (0.73)
  waiting for transfers between devices: 343 us -> 0 us
  Pallas kernels: 354 us -> 536 us
  starting transfers between devices: 33 us -> 0 us
  matrix products: 30.4 us -> 12.6 us
  other arithmetic: 42 us -> 32 us
    ppermute x47 -> x0, waiting for transfers between devices: 343 us -> none  [the longest x45 343 us: dp_swap(): return lax.ppermute(values, 'dp', [(i, i ^ bits) for i in range(size)])]
    pallas_call x2, Pallas kernels: 98.7 us -> 293 us  [the longest x1 231 us: end(): pl.pallas_call(functools.partial(end_kernel, count), in_specs=[VMEM] * 13...]
    ppermute x47 -> x0, starting transfers between devices: 33 us -> none  [the longest x45 31.9 us: dp_swap(): return lax.ppermute(values, 'dp', [(i, i ^ bits) for i in range(size)])]
    dot_general x8 -> x5, matrix products: 30.4 us -> 12.6 us  [dot(): return lax.dot_general(left, right, dims, preferred_element_type=f32)]
    pallas_call x1, Pallas kernels: 169 us -> 156 us  [middle(): pl.pallas_call(middle_kernel, in_specs=[VMEM] * 4 + [ANY] * 2 + [VMEM] *...]
    dynamic_slice x21 -> x0, local copies, waits for them, and re-layouts: 8.92 us -> none  [dp_sum(): send = lax.dynamic_slice_in_dim(piece, (1 - mine) * half, half, 0)]
    convert_element_type x28 -> x6, other arithmetic: 23.9 us -> 18.6 us  [the longest x5 16.4 us: body(): t.reshape(shape).astype(f32)]
  transfers between devices with their start and end apart: 47 -> 0, of which waited for: 32 -> 0; matrix products, arithmetic and copies ran while one was open for 7% -> 0% of each run, Pallas kernels for 0% -> 0%
where the time goes in v3:
time: 609 us; the launch traced here: 597 us
  Pallas kernels  536 us (88%)
  other arithmetic  32 us (5%)
  local copies, waits for them, and re-layouts  15.8 us (3%)
  matrix products  12.6 us (2%)
    pallas_call x1, Pallas kernels, end(): pl.pallas_call(functools.partial(end_kernel, count), in_specs=[VMEM] * 13...  231 us
    pallas_call x1, Pallas kernels, middle(): pl.pallas_call(middle_kernel, in_specs=[VMEM] * 4 + [ANY] * 2 + [VMEM] *...  156 us
    pallas_call x1, Pallas kernels, attend_back(): pl.pallas_call(functools.partial(attend_back_kernel, count, blocks=blocks...  61.4 us
    pallas_call x1, Pallas kernels, project_qkv(): pl.pallas_call(qkv_kernel, in_specs=[VMEM] * 6, out_specs=[VMEM, ANY], ou...  44 us
    pallas_call x1, Pallas kernels, attend(): pl.pallas_call(functools.partial(attend_kernel, blocks=blocks, size=seq /...  42.6 us
    convert_element_type x5, other arithmetic, body(): t.reshape(shape).astype(f32)  16.4 us
    dot_general x5, matrix products, dot(): return lax.dot_general(left, right, dims, preferred_element_type=f32)  12.6 us

profile of v3, /device:TPU:24, one launch (start us, length us, event | category | flops | bytes accessed | tf_op | source)
XLA Modules:
  0.0 597.0 jit_solution(400890142301626443)
XLA Ops:
  2.2 1.9 fusion
  6.8 2.6 select_select_fusion
  12.0 2.6 fusion.6.wv.refs_5_
  14.6 1.6 fusion.5.wk.refs_4_
  16.2 2.2 fusion.3.refs_10_
  18.5 1.6 fusion.2.x_ref
  20.0 2.4 fusion.4.wq.refs_3_
  22.4 2.4 convolution_convert_fusion.wo
  24.9 3.7 fusion.7
  28.6 1.9 pad_maximum_fusion
  30.5 44.0 %gather_project_qkv.1 = (bf16[2048,1024]{1,0:T(8,128)(2,1)}, bf16[4,512,1536]{2,1,0:T(8,128)(2,1)}) custom-call(bf16[512,1536]{1,0:T(8,128)(2,1)} %fusion.2.x_ref, bf16[1536,512]{1,0:T(8,128)(2,1)} %fusion.4.wq.refs_3_, bf16[1536,256]{1,0:T(8,128)(2,1)} %fusion.5.wk.refs_4_, bf16[1536,256]{1,0:T(8,128)(2,1)} %fusion.6.wv.refs_5_, ...), custom_call_target="tpu_custom_call" | custom-call | flops 40000000000 | bytes 20000000 | tf_op jit(solution)/shard_map/gather_project_qkv/pallas_call | solution.py:282
  74.5 42.6 %attention.1 = (bf16[2048,512]{1,0:T(8,128)(2,1)}, f32[2,2,2048]{2,1,0:T(2,128)}, bf16[3,4,128,1536]{3,2,1,0:T(8,128)(2,1)}) custom-call(bf16[2048,1024]{1,0:T(8,128)(2,1)} %get-tuple-element.40.q_ref.k_ref.v_ref.refs_0_.refs_1_.refs_2_, bf16[2048,1024]{1,0:T(8,128)(2,1)} %get-tuple-element.40.q_ref.k_ref.v_ref.refs_0_.refs_1_.refs_2_, ...), custom_call_target="tpu_custom_call" | custom-call | flops 8589934592 | bytes 12582912 | tf_op jit(solution)/shard_map/attention/pallas_call | solution.py:353
  117.1 156.2 %middle.1 = (f32[4,128,1536]{2,1,0:T(8,128)}, bf16[4,4,128,512]{3,2,1,0:T(8,128)(2,1)}, bf16[4,4,128,1536]{3,2,1,0:T(8,128)(2,1)}, f32[4,128,1536]{2,1,0:T(8,128...) custom-call(bf16[4,4,128,512]{3,2,1,0:T(8,128)(2,1)} %bitcast.59, ...), custom_call_target="tpu_custom_call" | custom-call | flops 149999992832 | bytes 80000000 | tf_op jit(solution)/shard_map/middle/pallas_call | solution.py:747
  273.3 61.4 %attention_back.1 = (bf16[2048,512]{1,0:T(8,128)(2,1)}, bf16[2048,256]{1,0:T(8,128)(2,1)}, bf16[2048,256]{1,0:T(8,128)(2,1)}, bf16[2,64,1536]{2,1,0:T(8,128)(2,1...) custom-call(bf16[2048,1024]{1,0:T(8,128)(2,1)} %get-tuple-element.40.q_ref.k_ref.v_ref.refs_0_.refs_1_.refs_2_, ...), custom_call_target="tpu_custom_call" | custom-call | flops 21474836480 | bytes 20971520 | tf_op jit(solution)/shard_map/attention_back/pallas_call | solution.py:493
  334.8 3.6 convolution_convert_fusion.2
  338.4 231.3 %end.1 = (f32[512,1536]{1,0:T(8,128)}, f32[8,1536]{1,0:T(8,128)}, bf16[4,128,1536]{2,1,0:T(8,128)(2,1)}, bf16[2,8,64,1536]{3,2,1,0:T(8,128)(2,1)}, bf16[2,8,96,1...) custom-call(bf16[2048,512]{1,0:T(8,128)(2,1)} %get-tuple-element.48., ...), custom_call_target="tpu_custom_call" | custom-call | flops 149999992832 | bytes 60000000 | tf_op jit(solution)/shard_map/end/pallas_call | solution.py:1015
  569.7 1.6 slice_reduce_fusion
  571.3 3.0 bitcast_convert_fusion.4
  574.8 1.6 slice.24
  576.8 1.5 copy.33
  579.8 5.5 bitcast_convert_fusion.2
  585.3 3.7 bitcast_convert_fusion.1
  588.9 3.8 bitcast_convert_fusion
  595.2 1.7 copy.39
  (60 shorter events, 11.7 us)
Async XLA Ops:
  0.6 14.0 %copy-start.6 = (bf16[1536,192]{0,1:T(8,128)(2,1)S(1)}, bf16[1536,192]{0,1:T(8,128)(2,1)}, u32[]{:S(2)}) copy-start(bf16[1536,192]{0,1:T(8,128)(2,1)} %param.20) | copy-start | bytes 1769476
  0.7 21.7 %copy-start.14 = (pred[384]{0:T(512)(128)(4,1)}, pred[384]{0:T(512)(128)(4,1)S(1)}, u32[]{:S(2)}) copy-start(pred[384]{0:T(512)(128)(4,1)S(1)} %get-tuple-element.84) | copy-start | bytes 1156
  0.7 21.7 %copy-start.15 = (pred[384]{0:T(512)(128)(4,1)}, pred[384]{0:T(512)(128)(4,1)S(1)}, u32[]{:S(2)}) copy-start(pred[384]{0:T(512)(128)(4,1)S(1)} %get-tuple-element.85) | copy-start | bytes 1156
  2.2 16.3 %copy-start = (bf16[512,1536]{1,0:T(8,128)(2,1)S(1)}, bf16[512,1536]{1,0:T(8,128)(2,1)}, u32[]{:S(2)}) copy-start(bf16[512,1536]{1,0:T(8,128)(2,1)} %refs_6_.1) | copy-start | bytes 4718596
  2.2 16.3 %copy-start.7 = (f32[1536]{0:T(1024)S(1)}, f32[1536]{0:T(1024)}, u32[]{:S(2)}) copy-start(f32[1536]{0:T(1024)} %param.18) | copy-start | bytes 18436
  4.2 18.2 %copy-start.8 = (s32[384]{0:T(512)}, s32[384]{0:T(512)S(1)}, u32[]{:S(2)}) copy-start(s32[384]{0:T(512)S(1)} %get-tuple-element.82) | copy-start | bytes 4612
  4.2 18.2 %copy-start.9 = (s32[384]{0:T(512)}, s32[384]{0:T(512)S(1)}, u32[]{:S(2)}) copy-start(s32[384]{0:T(512)S(1)} %get-tuple-element.83) | copy-start | bytes 4612
  4.2 18.2 %copy-start.10 = (s32[384]{0:T(512)}, s32[384]{0:T(512)S(1)}, u32[]{:S(2)}) copy-start(s32[384]{0:T(512)S(1)} %get-tuple-element.80) | copy-start | bytes 4612
  4.2 18.2 %copy-start.11 = (s32[384]{0:T(512)}, s32[384]{0:T(512)S(1)}, u32[]{:S(2)}) copy-start(s32[384]{0:T(512)S(1)} %get-tuple-element.81) | copy-start | bytes 4612
  14.6 5.4 copy-start.12
  18.4 4.0 copy-start.13
  569.7 4.6 copy-start.4
  579.8 5.5 copy-start.3
  585.3 3.7 copy-start.2
  588.9 3.8 copy-start.5
  592.7 2.5 copy-start.1

commit v4 on v3

v4 whole, which is shorter than its diff:
```python
import functools
import math

import jax
import jax.numpy as jnp
from jax import lax
from jax.experimental import pallas as pl
from jax.experimental.pallas import tpu as pltpu
from jax.sharding import PartitionSpec as P

HEAD_SIZE = 96
HALF = HEAD_SIZE // 2
LANES = 128
epsilon = 1e-05
rope_base = 100000.0
masked_value = -1e30
score_scale = 1.0 / math.sqrt(HEAD_SIZE)
log2_e = math.log2(math.e)
bf16, f32 = jnp.bfloat16, jnp.float32
NN = (((1,), (0,)), ((), ()))
NT = (((1,), (1,)), ((), ()))
TN = (((0,), (0,)), ((), ()))
VMEM_LIMIT = 67043328
CHUNKS = 4


def dot(left, right, dims=NN):
    return lax.dot_general(left, right, dims, preferred_element_type=f32)


def params():
    return pltpu.CompilerParams(vmem_limit_bytes=VMEM_LIMIT)


def cost(flops, nbytes):
    return pl.CostEstimate(flops=int(flops), bytes_accessed=int(nbytes), transcendentals=0)


def whole(shape):
    return pl.BlockSpec(shape, lambda *_: (0,) * len(shape), pipeline_mode=pl.Buffered(1))


ANY = pl.BlockSpec(memory_space=pl.ANY)
VMEM = pl.BlockSpec(memory_space=pltpu.VMEM)


def peer(bits):
    me = lax.axis_index("tensor")
    low, high = lax.rem(me, 2), lax.div(me, 2)
    if bits % 2:
        low = 1 - low
    if bits // 2:
        high = 1 - high
    return 2 * high + low


def partner(bits):
    return {"tensor": peer(bits)}


def send(source, target, sems, at, bits):
    return pltpu.make_async_remote_copy(
        src_ref=source,
        dst_ref=target,
        send_sem=sems[0].at[at],
        recv_sem=sems[1].at[at],
        device_id=partner(bits),
        device_id_type=pl.DeviceIdType.MESH,
    )


def meet(*others):
    barrier = pltpu.get_barrier_semaphore()
    for other in others:
        pl.semaphore_signal(barrier, inc=1, device_id=other, device_id_type=pl.DeviceIdType.MESH)
    pl.semaphore_wait(barrier, len(others))


RING = 8
IN_MIDDLE = 3
IN_BACK = 6


def ring_place():
    index = lax.axis_index("dp")
    deep, wide = lax.div(index, 2), lax.rem(index, 2)
    return deep + wide * (RING - 1 - 2 * deep)


def ring_peer(way):
    place = lax.rem(ring_place() + (1, RING - 1)[way], RING)
    wide = lax.div(place, RING // 2)
    return {"dp": 2 * (place + wide * (RING - 1 - 2 * place)) + wide}


def ring_chunk(way, step):
    return lax.rem(ring_place() + (2 * RING - step if way == 0 else step), RING)


def ring_send(source, target, sems, at, way):
    return pltpu.make_async_remote_copy(
        src_ref=source,
        dst_ref=target,
        send_sem=sems[0].at[at],
        recv_sem=sems[1].at[at],
        device_id=ring_peer(way),
        device_id_type=pl.DeviceIdType.MESH,
    )


class Reduce:
    def __init__(self, parts, state, land, mine, first, last, send_sem, recv_sem, load_sem=None):
        self.parts, self.state, self.land, self.mine = parts, state, land, mine
        self.first, self.count, self.sems, self.load_sem = first, last - first, (send_sem, recv_sem), load_sem

    def begin(self, way):
        source = self.parts.at[way, ring_chunk(way, 0)] if self.state is None else self.state.at[way]
        return ring_send(source, self.land(way, 0), self.sems, (way, 0), way)

    def copy(self, way, k):
        return ring_send(self.land(way, k - 1), self.land(way, k), self.sems, (way, k), way)

    def load(self, way, k):
        source = self.parts.at[way, ring_chunk(way, self.first + k + 1)]
        return pltpu.make_async_copy(source, self.mine(way, k), self.load_sem.at[way, k])

    def start(self):
        for way in range(2):
            self.begin(way).start()

    def prefetch(self):
        for k in range(self.count):
            for way in range(2):
                self.load(way, k).start()

    def step(self, k):
        for way in range(2):
            (self.copy(way, k) if k else self.begin(way)).wait_recv()
            if self.mine is None:
                own = self.parts[way, ring_chunk(way, self.first + k + 1)]
            else:
                self.load(way, k).wait()
                own = self.mine(way, k)[...]
            here = self.land(way, k)
            here[...] = (here[...].astype(f32) + own.astype(f32)).astype(bf16)
            if k + 1 < self.count:
                self.copy(way, k + 1).start()

    def result(self, way):
        return self.land(way, self.count - 1)

    def finish(self):
        for way in range(2):
            self.begin(way).wait_send()
            for k in range(1, self.count):
                self.copy(way, k).wait_send()


class Spread:
    def __init__(self, reduced, full, send_sem, recv_sem, own_sem):
        self.reduced, self.full, self.sems, self.own_sem = reduced, full, (send_sem, recv_sem), own_sem

    def slot(self, way, step):
        return self.full.at[way, ring_chunk(way, step + RING - 1)]

    def keep(self, way):
        return pltpu.make_async_copy(self.reduced.result(way), self.slot(way, 0), self.own_sem.at[way])

    def copy(self, way, k):
        source = self.slot(way, k) if k else self.reduced.result(way)
        return ring_send(source, self.slot(way, k), self.sems, (way, k), way)

    def start(self):
        for way in range(2):
            self.copy(way, 0).start()
            self.keep(way).start()

    def step(self, k):
        for way in range(2):
            ring_send(self.slot(way, k + 1), self.slot(way, k + 1), self.sems, (way, k), way).wait_recv()
            if k < RING - 2:
                self.copy(way, k + 1).start()

    def finish(self):
        for way in range(2):
            self.keep(way).wait()
            for k in range(RING - 1):
                self.copy(way, k).wait_send()


def slots(ref):
    return lambda way, k: ref.at[way, k]


def ring_scratch(shape, steps, loads):
    rows, cols = shape[2:]
    land = pltpu.VMEM((2, steps, rows, cols), bf16)
    sems = [pltpu.SemaphoreType.DMA((2, steps))] * (3 if loads else 2)
    return [land] * (2 if loads else 1) + sems


def comm_params(number):
    return pltpu.CompilerParams(vmem_limit_bytes=VMEM_LIMIT, collective_id=number, has_side_effects=True)


def dma_sems(*shape):
    return [pltpu.SemaphoreType.DMA(shape)] * 2


def spread(heads, turned=False):
    shape = (heads * HEAD_SIZE, heads * LANES)
    feature = lax.broadcasted_iota(jnp.int32, shape[::-1] if turned else shape, int(turned))
    lane = lax.broadcasted_iota(jnp.int32, shape[::-1] if turned else shape, 1 - int(turned))
    target = feature
    for half in range(1, 2 * heads):
        target += jnp.where(feature >= half * HALF, LANES // 2 - HALF, 0)
    return jnp.where(lane == target, 1.0, 0.0).astype(bf16)


def front_kernel(
    tokens, gains, w_query, key_weight, value_weight, w_out, segments, positions, cot,
    qkv_out, stack_out, att_out, lse_out, cots, wq_out, wk_out, wv_out, wo_out, cos_out, sin_out, start_out,
    x, land, qkv, att, wq, wk, wv, wo, cos_v, sin_v, send_sem, recv_sem, store_sem,
    *, blocks,
):
    sems = (send_sem, recv_sem)
    own, width = tokens.shape
    rows = own // CHUNKS
    seq = qkv.shape[0]
    size = seq // blocks

    def piece(k):
        return pl.ds(pl.multiple_of(k * rows, rows), rows)

    side = send(x, land.at[0], sems, (0, 0), 1)
    across = lambda k: send(x.at[piece(k)], land.at[1, piece(k)], sems, (1, k), 2)
    onward = lambda k: send(land.at[1, piece(k)], land.at[2, piece(k)], sems, (2, k), 1)
    cot_side = send(cot, cots.at[0], sems, (3, 0), 1)
    cot_across = lambda k: send(cot.at[k], cots.at[1, k], sems, (4, k), 2)
    cot_onward = lambda k: send(cots.at[1, k], cots.at[2, k], sems, (5, k), 1)
    stores = []

    def store(source, target):
        copy = pltpu.make_async_copy(source, target, store_sem.at[len(stores)])
        copy.start()
        stores.append(copy)

    meet(partner(1), partner(2))

    @pl.loop(0, CHUNKS)
    def _(k):
        inputs = tokens[piece(k)].astype(f32)
        inverse = lax.rsqrt(jnp.mean(inputs * inputs, axis=-1, keepdims=True) + epsilon)
        x[piece(k)] = (inputs * inverse * gains[0:1, :]).astype(bf16)
        across(k).start()

    side.start()
    store(x, stack_out.at[0])

    spread_q, spread_k = spread(w_query.shape[1] // HEAD_SIZE), spread(key_weight.shape[1] // HEAD_SIZE)
    for source, matrix, target, out in (
        (w_query, spread_q, wq, wq_out),
        (key_weight, spread_k, wk, wk_out),
        (value_weight, spread_k, wv, wv_out),
    ):
        target[...] = dot(source[...], matrix).astype(bf16)
        store(target, out)
    wo[...] = dot(spread(w_query.shape[1] // HEAD_SIZE, True), w_out[...]).astype(bf16)
    store(wo, wo_out)

    lane = lax.broadcasted_iota(jnp.int32, (1, LANES), 1)
    feature = jnp.where(lane < LANES // 2, lane, lane - LANES // 2)
    frequency = jnp.exp(feature.astype(f32) * (-2.0 * math.log(rope_base) / HEAD_SIZE))
    frequency = jnp.where(feature < HALF, frequency, 0.0)
    sign = jnp.where(lane < LANES // 2, -1.0, 1.0)
    for p in range(4):

        @pl.loop(0, CHUNKS)
        def _(k):
            base = pl.multiple_of(peer(p) * own + k * rows, rows)
            angles = positions[pl.ds(base, rows), :].astype(f32) * frequency
            here = pl.ds(pl.multiple_of(p * own + k * rows, rows), rows)
            cos_v[here] = jnp.cos(angles)
            sin_v[here] = jnp.sin(angles) * sign

    store(cos_v, cos_out)
    store(sin_v, sin_out)
    documents = segments[...].astype(f32)
    starts = jnp.zeros_like(documents)
    for document in (1, 2, 3):
        first = jnp.sum(jnp.where(documents < document, 1.0, 0.0), axis=1, keepdims=True)
        starts = jnp.where(documents >= document, first, starts)
    start_out[...] = starts.astype(jnp.int32)

    head_lane = lax.broadcasted_iota(jnp.int32, (rows, LANES), 1)

    def project(ref, base):
        values = ref[...]
        here = pl.ds(pl.multiple_of(base, rows), rows)
        cos, sin = cos_v[here], sin_v[here]
        for w, first, turn in ((wq, 0, True), (wk, 4, True), (wv, 6, False)):
            y = dot(values, w[...])
            for h in range(w.shape[1] // LANES):
                v = y[:, h * LANES : (h + 1) * LANES]
                if turn:
                    v = v * cos + pltpu.roll(v, LANES // 2, 1) * sin
                else:
                    v = jnp.where(head_lane == HALF, 1.0, v)
                at = (first + h) * LANES
                qkv[here, at : at + LANES] = v.astype(bf16)

    @pl.loop(0, CHUNKS)
    def _(k):
        project(x.at[piece(k)], k * rows)

    side.wait_recv()
    store(land.at[0], stack_out.at[1])
    cot_side.start()

    @pl.loop(0, CHUNKS)
    def _(k):
        project(land.at[0, piece(k)], own + k * rows)

    @pl.loop(0, CHUNKS)
    def _(k):
        across(k).wait_recv()
        onward(k).start()
        cot_across(k).start()
        project(land.at[1, piece(k)], 2 * own + k * rows)
        onward(k).wait_recv()
        project(land.at[2, piece(k)], 3 * own + k * rows)

    store(land.at[1], stack_out.at[2])
    store(land.at[2], stack_out.at[3])
    store(qkv, qkv_out)

    @pl.loop(0, 2)
    def _(g):
        for i in range(blocks):
            at = pl.ds(pl.multiple_of(peer(i) * size, size), size)
            cols = [pl.ds(pl.multiple_of((2 * g + r) * LANES, LANES), LANES) for r in range(2)]
            queries = [qkv[at, cols[r]] for r in range(2)]
            start = start_out[:, i * size : (i + 1) * size]
            state = [None, None]
            for j in [i, *range(i)]:
                key_at = pl.ds(pl.multiple_of(peer(j) * size, size), size)
                keys = qkv[key_at, pl.ds(pl.multiple_of((4 + g) * LANES, LANES), LANES)]
                values = qkv[key_at, pl.ds(pl.multiple_of((6 + g) * LANES, LANES), LANES)]
                key_rows = lax.broadcasted_iota(jnp.int32, (size, size), 0)
                allowed = key_rows >= start - j * size
                if j == i:
                    allowed &= key_rows <= lax.broadcasted_iota(jnp.int32, (size, size), 1)
                for r in range(2):
                    scores = jnp.where(allowed, dot(keys, queries[r], NT) * (score_scale * log2_e), masked_value)
                    peak = jnp.max(scores, axis=0, keepdims=True)
                    if state[r] is not None:
                        peak = jnp.maximum(state[r][0], peak)
                    weights = jnp.exp2(scores - peak)
                    mixed = dot(values, weights.astype(bf16), TN)
                    if state[r] is not None:
                        mixed += state[r][1] * jnp.exp2(state[r][0] - peak)
                    state[r] = (peak, mixed)
            for r, (peak, mixed) in enumerate(state):
                total = mixed[HALF : HALF + 1, :]
                att[at, cols[r]] = (mixed / total).T.astype(bf16)
                lse_out[g, r : r + 1, at] = peak + jnp.log2(total)

    store(att, att_out)
    for k in range(CHUNKS):
        cot_across(k).wait_recv()
        cot_onward(k).start()
    side.wait_send()
    cot_side.wait()
    for k in range(CHUNKS):
        across(k).wait_send()
        onward(k).wait_send()
        cot_across(k).wait_send()
        cot_onward(k).wait()
    for copy in stores:
        copy.wait()


def front(tokens, gains, w_query, key_weight, value_weight, w_out, segments, positions, cot, blocks):
    own, width = tokens.shape
    seq = segments.shape[1]
    pieces = (CHUNKS, own // CHUNKS, width)
    sds = jax.ShapeDtypeStruct
    heads = 4 * LANES
    arrays = dict(
        qkv=(seq, 8 * LANES), att=(seq, heads), wq=(width, heads), wk=(width, heads // 2), wv=(width, heads // 2),
        wo=(heads, width),
    )
    low = lambda name: sds(arrays[name], bf16)
    scratch = lambda name: pltpu.VMEM(arrays[name], bf16)
    table = sds((seq, LANES), f32)
    return pl.pallas_call(
        functools.partial(front_kernel, blocks=blocks),
        in_specs=[VMEM] * 8 + [ANY],
        out_specs=[ANY] * 3 + [VMEM] + [ANY] * 7 + [VMEM],
        out_shape=[
            low("qkv"), sds((4, own, width), bf16), low("att"), sds((2, 2, seq), f32), sds((3, *pieces), bf16),
            low("wq"), low("wk"), low("wv"), low("wo"), table, table, sds((1, seq), jnp.int32),
        ],
        scratch_shapes=[
            pltpu.VMEM((own, width), bf16),
            pltpu.VMEM((3, own, width), bf16),
            *[scratch(name) for name in arrays],
            pltpu.VMEM((seq, LANES), f32),
            pltpu.VMEM((seq, LANES), f32),
            *dma_sems(6, CHUNKS),
            pltpu.SemaphoreType.DMA((12,)),
        ],
        compiler_params=comm_params(1),
        cost_estimate=cost(80e-6 * 1e15, 40e6),
        name="front",
    )(tokens, gains, w_query, key_weight, value_weight, w_out, segments, positions, cot.reshape(pieces))


def attend_back_kernel(count, *refs, blocks, size):
    q_ref, k_ref, v_ref, o_ref, do_ref, lse_ref, start_ref, cos_ref, sin_ref, *rest = refs
    parts, befores, rest = rest[:count], rest[count : 2 * count], rest[2 * count :]
    dq_ref, dk_ref, dv_ref, *rest = rest
    states, rest = rest[:count], rest[count:]
    dq_sum, dk_sum, dv_sum, inner, *rest = rest
    rings = []
    for a in range(count):
        land, mine, *own_sems = rest[5 * a : 5 * a + 5]
        rings.append(Reduce(parts[a], befores[a], slots(land), slots(mine), IN_MIDDLE, IN_BACK, *own_sems))
    steps = IN_BACK - IN_MIDDLE
    keep_sem = rest[-1] if count else None

    def keep(a, way):
        return pltpu.make_async_copy(rings[a].result(way), states[a].at[way], keep_sem.at[a, way])

    if count:

        @pl.when(pl.program_id(0) == 0)
        def _():
            meet(ring_peer(0), ring_peer(1))
            for ring in rings:
                ring.start()
            for ring in rings:
                ring.prefetch()

    pairs = blocks * (blocks + 1) // 2
    hooks = {}
    for number in range(count * steps):
        due = min(round((number + 1) * 2.25) + 1, 2 * pairs - 1)
        hooks.setdefault(due, []).append((number % count, number // count))

    def hook(pair):
        for half in range(2):
            todo = hooks.get(half * pairs + pair, [])
            if todo:

                @pl.when(pl.program_id(0) == half)
                def _():
                    for a, k in todo:
                        rings[a].step(k)
                        if k == steps - 1:
                            keep(a, 0).start()
                            keep(a, 1).start()

    for c in range(blocks):
        rows = slice(c * size, (c + 1) * size)
        for r in range(2):
            cols = slice(r * LANES, (r + 1) * LANES)
            product = do_ref[rows, cols].astype(f32) * o_ref[rows, cols].astype(f32)
            inner[r : r + 1, rows] = jnp.sum(product.T, axis=0, keepdims=True)
    for i in reversed(range(blocks)):
        for j in [i, *range(i)]:
            at = pl.multiple_of(peer(i) * size, size)
            key_at = pl.multiple_of(peer(j) * size, size)
            keys = k_ref[pl.ds(key_at, size), :]
            values = v_ref[pl.ds(key_at, size), :]
            start = start_ref[:, i * size : (i + 1) * size]
            key_rows = lax.broadcasted_iota(jnp.int32, (size, size), 0)
            allowed = key_rows >= start - j * size
            if j == i:
                allowed &= key_rows <= lax.broadcasted_iota(jnp.int32, (size, size), 1)
            dk = dv = None
            for r in range(2):
                cols = slice(r * LANES, (r + 1) * LANES)
                queries = q_ref[pl.ds(at, size), cols]
                grads = do_ref[pl.ds(at, size), cols]
                scores = jnp.where(allowed, dot(keys, queries, NT) * (score_scale * log2_e), masked_value)
                weights = jnp.exp2(scores - lse_ref[0, r : r + 1, pl.ds(at, size)])
                grad_weights = dot(values, grads, NT)
                grad_scores = (weights * (grad_weights - inner[r : r + 1, pl.ds(at, size)])).astype(bf16)
                dv_term = dot(weights.astype(bf16), grads)
                dk_term = dot(grad_scores, queries)
                dv = dv_term if dv is None else dv + dv_term
                dk = dk_term if dk is None else dk + dk_term
                dq = dot(grad_scores, keys, TN)
                if j == i:
                    dq_sum[pl.ds(at, size), cols] = dq
                else:
                    dq_sum[pl.ds(at, size), cols] += dq
            if i == blocks - 1:
                dk_sum[pl.ds(key_at, size), :] = dk
                dv_sum[pl.ds(key_at, size), :] = dv
            else:
                dk_sum[pl.ds(key_at, size), :] += dk
                dv_sum[pl.ds(key_at, size), :] += dv
            hook(sum(range(blocks, i + 1, -1)) + (0 if j == i else j + 1))
    for c in range(blocks):
        rows = slice(c * size, (c + 1) * size)
        cos, sin = cos_ref[rows, :], sin_ref[rows, :]

        def back(grads):
            return ((grads * cos - pltpu.roll(grads, LANES // 2, 1) * sin) * score_scale).astype(bf16)

        for r in range(2):
            cols = slice(r * LANES, (r + 1) * LANES)
            dq_ref[rows, cols] = back(dq_sum[rows, cols])
        dk_ref[rows, :] = back(dk_sum[rows, :])
        dv_ref[rows, :] = dv_sum[rows, :].astype(bf16)

    if count:

        @pl.when(pl.program_id(0) == 1)
        def _():
            for a, ring in enumerate(rings):
                ring.finish()
                keep(a, 0).wait()
                keep(a, 1).wait()


def attend_back(qkv, attended, grads, lse, start, cos, sin, parts, befores, blocks):
    seq = qkv.shape[0]
    pair = pl.BlockSpec((seq, 2 * LANES), lambda g: (0, g))
    single = pl.BlockSpec((seq, LANES), lambda g: (0, g))
    table = pl.BlockSpec((seq, LANES), lambda g: (0, 0))
    count = len(parts)
    outs = pl.pallas_call(
        functools.partial(attend_back_kernel, count, blocks=blocks, size=seq // blocks),
        grid=(2,),
        in_specs=[
            pair,
            pl.BlockSpec((seq, LANES), lambda g: (0, 4 + g)),
            pl.BlockSpec((seq, LANES), lambda g: (0, 6 + g)),
            pair,
            pair,
            pl.BlockSpec((1, 2, seq), lambda g: (g, 0, 0)),
            pl.BlockSpec((1, seq), lambda g: (0, 0)),
            table,
            table,
            *[ANY] * (2 * count),
        ],
        out_specs=[pair, single, single, *[ANY] * count],
        scratch_shapes=[
            pltpu.VMEM((seq, 2 * LANES), f32),
            pltpu.VMEM((seq, LANES), f32),
            pltpu.VMEM((seq, LANES), f32),
            pltpu.VMEM((2, seq), f32),
            *[x for p in parts for x in ring_scratch(p.shape, IN_BACK - IN_MIDDLE, True)],
            *[pltpu.SemaphoreType.DMA((count, 2))] * bool(count),
        ],
        out_shape=[
            jax.ShapeDtypeStruct((seq, 4 * LANES), bf16),
            jax.ShapeDtypeStruct((seq, 2 * LANES), bf16),
            jax.ShapeDtypeStruct((seq, 2 * LANES), bf16),
            *[jax.ShapeDtypeStruct((2, *p.shape[2:]), bf16) for p in parts],
        ],
        compiler_params=comm_params(5) if count else params(),
        cost_estimate=cost(5 * 2 * 4 * LANES * seq * seq, 10 * seq * 8 * LANES),
        name="attention_back",
    )(qkv, qkv, qkv, attended, grads, lse, start, cos, sin, *parts, *befores)
    return outs[:3], outs[3:]


def rows_back(grad, inputs, gain):
    inverse = lax.rsqrt(jnp.mean(inputs * inputs, axis=-1, keepdims=True) + epsilon)
    unit = inputs * inverse
    scaled = grad * gain
    back = inverse * (scaled - unit * jnp.mean(scaled * unit, axis=-1, keepdims=True))
    return back, jnp.sum((grad * unit).reshape(-1, 8, grad.shape[-1]), axis=0)

RS1_C0, RS1_C1, RS1_X, AG2_X, AG2_C, AG2_F, RS3_C0, RS3_C1, RS3_X, AG3_X, AG3_C, AG3_F = range(12)


class _Chunks:
    def __init__(self, ref):
        self.ref, self.rows = ref, ref.shape[0] // (2 * RING)

    @property
    def at(self):
        return self

    def __getitem__(self, index):
        way, chunk = index
        return self.ref.at[pl.ds(pl.multiple_of((way * RING + chunk) * self.rows, self.rows), self.rows)]


def middle_kernel(
    ringed, att, wo, tokens, gains, cot_own, cots, wg_in, wu_in, wd_in,
    hid1, datt_out, parts_out, grad_one_out, dwd_out, dwg_out, dwu_out, dwo_out, gain_grad, *refs,
):
    states, refs = (refs[:3], refs[3:]) if ringed else ([], refs)
    (
        xs, cot, hid, gg, gu, g, cr, xr, part_stage, grad_stage, datt_stage, tile_stage, wg, wu, wd,
        send_sem, recv_sem, cot_sem, part_sem, grad_sem, datt_sem, tile_sem, free_sem, *ring_sems,
    ) = refs
    gain = gains.at[1:2]
    pieces, _, n, width = xs.shape
    units = wg.shape[1]
    heads = wo.shape[0]
    sems = (send_sem, recv_sem)
    two = (2 * n, width)

    def copy(kind, k):
        source, target, bits = {
            RS1_C0: (g.at[k, 3], cr.at[k, 0], 1),
            RS1_C1: (g.at[k, 1], cr.at[k, 1], 1),
            RS1_X: (g.at[k, 2], xr.at[k], 2),
            AG2_X: (xs.at[k, 0], xs.at[k, 2], 2),
            AG2_C: (xs.at[k, 0], xs.at[k, 1], 1),
            AG2_F: (xs.at[k, 2], xs.at[k, 3], 1),
            RS3_C0: (g.at[k, 3], cr.at[k, 0], 1),
            RS3_C1: (g.at[k, 1], cr.at[k, 1], 1),
            RS3_X: (g.at[k, 2], xr.at[k], 2),
            AG3_X: (g.at[k, 0], g.at[k, 2], 2),
            AG3_C: (g.at[k, 0], g.at[k, 1], 1),
            AG3_F: (g.at[k, 2], g.at[k, 3], 1),
        }[kind]
        return send(source, target, sems, (kind, k), bits)

    def credit(k, bits):
        pl.semaphore_signal(
            free_sem.at[bits - 1, k], inc=1, device_id=partner(bits), device_id_type=pl.DeviceIdType.MESH
        )

    def cot_copy(p):
        if p >= 4:
            source, target = ((wg_in, wg), (wu_in, wu), (wd_in, wd))[p - 4]
            return pltpu.make_async_copy(source, target, cot_sem.at[p])
        source = cot_own if p == 0 else cots.at[p - 1]
        return pltpu.make_async_copy(source, cot.at[:, p], cot_sem.at[p])

    def part_copy(k, low):
        return pltpu.make_async_copy(part_stage.at[k], parts_out.at[k, pl.ds(low, 2)], part_sem.at[k])

    for p in (4, 5, 6, 0, 1, 2, 3):
        cot_copy(p).start()
    meet(partner(1), partner(2), *([ring_peer(0), ring_peer(1)] if ringed else []))

    @pl.loop(0, pieces)
    def _(k):
        for p, kind in ((3, RS1_C0), (1, RS1_C1)):
            g[k, p] = dot(att[p, k], wo[...]).astype(bf16)
            copy(kind, k).start()

    @pl.loop(0, pieces)
    def _(k):
        term = dot(att[2, k], wo[...])
        copy(RS1_C0, k).wait_recv()
        g[k, 2] = (term + cr[k, 0].astype(f32)).astype(bf16)
        copy(RS1_X, k).start()

    def feed_forward(k, low):
        x = xs[k, pl.ds(low, 2)].reshape(two)
        gate = dot(x, wg[...])
        up = dot(x, wu[...])
        grad_hidden = dot(cot[k, pl.ds(low, 2)].reshape(two), wd[...], NT)
        sig = jax.nn.sigmoid(gate)
        act = gate * sig
        hidden = (act * up).astype(bf16)
        grad_gate = (grad_hidden * up * sig * (1.0 + gate * (1.0 - sig))).astype(bf16)
        grad_up = (grad_hidden * act).astype(bf16)
        hid[k, pl.ds(low, 2)] = hidden.reshape(2, n, units)
        gg[k, pl.ds(low, 2)] = grad_gate.reshape(2, n, units)
        gu[k, pl.ds(low, 2)] = grad_up.reshape(2, n, units)
        back = dot(grad_gate, wg[...], NT) + dot(grad_up, wu[...], NT)
        g[k, pl.ds(low, 2)] = back.astype(bf16).reshape(2, n, width)
        return hidden

    def out_part(k, low, hidden):
        part_stage[k] = dot(hidden, wd[...]).astype(bf16).reshape(2, n, width)
        part_copy(k, low).start()

    for p in range(7):
        cot_copy(p).wait()

    @pl.loop(0, pieces)
    def _(k):
        term = dot(att[0, k], wo[...])
        copy(RS1_C1, k).wait_recv()
        copy(RS1_X, k).wait_recv()
        hidden = tokens[k].astype(f32) + (term + cr[k, 1].astype(f32) + xr[k].astype(f32))
        hid1[k] = hidden
        inverse = lax.rsqrt(jnp.mean(hidden * hidden, axis=-1, keepdims=True) + epsilon)
        xs[k, 0] = (hidden * inverse * gain[...]).astype(bf16)
        copy(AG2_X, k).start()
        copy(AG2_C, k).start()
        copy(AG2_C, k).wait_recv()
        copy(RS1_C1, k).wait_send()
        out_part(k, 0, feed_forward(k, 0))

    @pl.loop(0, pieces)
    def _(k):
        copy(AG2_X, k).wait_recv()
        copy(AG2_F, k).start()
        part_copy(k, 0).wait()
        copy(AG2_F, k).wait_recv()
        copy(RS1_C0, k).wait_send()
        copy(RS1_X, k).wait_send()
        hidden = feed_forward(k, 2)
        copy(RS3_C0, k).start()
        copy(RS3_C1, k).start()
        out_part(k, 2, hidden)
        copy(RS3_C0, k).wait_recv()
        g[k, 2] = (g[k, 2].astype(f32) + cr[k, 0].astype(f32)).astype(bf16)
        copy(RS3_X, k).start()

    tokens_all = 4 * pieces * n

    def tile(slot, left, right, cols, out, at):
        height = out.shape[1]
        target = out.at[pl.ds(pl.multiple_of(at * 256, 256), 256)]
        move = pltpu.make_async_copy(tile_stage.at[slot, :, pl.ds(0, height)], target, tile_sem.at[slot])
        part = left[:, :, :, pl.ds(pl.multiple_of(at * 256, 256), 256)].reshape(tokens_all, 256)
        tile_stage[slot, :, pl.ds(0, height)] = dot(part, right[...].reshape(tokens_all, cols), TN).astype(bf16)
        return move

    def norm_back(k):
        copy(RS3_C1, k).wait_recv()
        copy(RS3_X, k).wait_recv()
        copy(RS3_C0, k).wait_send()
        copy(RS3_C1, k).wait_send()
        credit(k, 1)
        copy(RS3_X, k).wait_send()
        credit(k, 2)
        grad = g[k, 0].astype(f32) + cr[k, 1].astype(f32) + xr[k].astype(f32)
        back, sums = rows_back(grad, hid1[k], gain[...])
        result = cot[k, 0].astype(f32) + back
        g[k, 0] = result.astype(bf16)
        pl.semaphore_wait(free_sem.at[0, k], 1)
        pl.semaphore_wait(free_sem.at[1, k], 1)
        copy(AG3_X, k).start()
        copy(AG3_C, k).start()
        grad_stage[...] = result
        stored = pltpu.make_async_copy(grad_stage, grad_one_out.at[k], grad_sem.at[0])
        stored.start()

        @pl.when(k == 0)
        def _():
            gain_grad[...] = sums

        @pl.when(k > 0)
        def _():
            gain_grad[...] += sums

        return stored

    @pl.loop(0, 2)
    def _(k):
        first = tile(0, hid, cot, width, dwd_out, 2 * k)
        first.start()
        second = tile(1, hid, cot, width, dwd_out, 2 * k + 1)
        second.start()
        stored = norm_back(k)
        first.wait()
        second.wait()
        stored.wait()

    rings = []
    if ringed:
        n_down = dwd_out.shape[0] // (2 * RING)
        n_up = dwg_out.shape[0] // (2 * RING)
        places = (
            (lambda way, k: cot.at[k, 1 + way, pl.ds(0, n_down)], lambda way, k: cot.at[k, 3, pl.ds(way * n_down, n_down)]),
            (lambda way, k: hid.at[k, way, pl.ds(0, n_up)], lambda way, k: gg.at[k, way, pl.ds(0, n_up)]),
            (lambda way, k: hid.at[k, 2 + way, pl.ds(0, n_up)], lambda way, k: gu.at[k, way, pl.ds(0, n_up)]),
        )
        for a, (part, (land, mine)) in enumerate(zip((dwd_out, dwg_out, dwu_out), places)):
            rings.append(Reduce(_Chunks(part), None, land, mine, 0, IN_MIDDLE, *ring_sems[3 * a : 3 * a + 3]))
        for way in range(2):
            pl.semaphore_signal(
                free_sem.at[2, way], inc=1, device_id=ring_peer(1 - way), device_id_type=pl.DeviceIdType.MESH
            )

    @pl.loop(2, 4)
    def _(k):
        stored = norm_back(k)
        for i in range(3):
            at = 3 * (k - 2) + i
            gate = tile(0, xs, gg, units, dwg_out, at)
            gate.start()
            up = tile(1, xs, gu, units, dwu_out, at)
            up.start()
            gate.wait()
            up.wait()
        stored.wait()

    if ringed:
        for way in range(2):
            pl.semaphore_wait(free_sem.at[2, way], 1)
        for ring in rings:
            ring.start()
        for ring in rings:
            ring.prefetch()

    for k in range(pieces):
        copy(AG3_X, k).wait_recv()
        copy(AG3_F, k).start()
        copy(AG3_C, k).wait_recv()
        copy(AG3_F, k).wait_recv()
        datt_stage[...] = dot(g[k].reshape(4 * n, width), wo[...], NT).astype(bf16).reshape(4, n, heads)
        moved = pltpu.make_async_copy(datt_stage, datt_out.at[:, k], datt_sem.at[0])
        moved.start()
        moved.wait()
        if ringed and k > 0:
            for ring in rings:
                if k - 1 < IN_MIDDLE - 1:
                    ring.step(k - 1)

    for u in range(heads // 256):
        total = None
        for p in range(4):
            left = att[p, :, :, u * 256 : (u + 1) * 256].reshape(pieces * n, 256)
            term = dot(left, g[:, p].reshape(pieces * n, width), TN)
            total = term if total is None else total + term
        tile_stage[u] = total.astype(bf16)
        pltpu.make_async_copy(tile_stage.at[u], dwo_out.at[pl.ds(u * 256, 256)], tile_sem.at[u]).start()
    for u in range(heads // 256):
        pltpu.make_async_copy(tile_stage.at[u], dwo_out.at[pl.ds(u * 256, 256)], tile_sem.at[u]).wait()

    if ringed:
        for a, ring in enumerate(rings):
            ring.step(IN_MIDDLE - 1)
            for way in range(2):
                pltpu.make_async_copy(ring.result(way), states[a].at[way], ring_sems[-1].at[a, way]).start()
        for a, ring in enumerate(rings):
            ring.finish()
            for way in range(2):
                pltpu.make_async_copy(ring.result(way), states[a].at[way], ring_sems[-1].at[a, way]).wait()

    @pl.loop(0, pieces)
    def _(k):
        part_copy(k, 2).wait()
        for kind in (AG2_X, AG2_C, AG2_F, AG3_X, AG3_C, AG3_F):
            copy(kind, k).wait_send()


def middle(attended, wo, tokens, gains, cot_own, cots, wg, wu, wd, ringed):
    width, units, heads = wg.shape[0], wg.shape[1], wo.shape[0]
    pieces = CHUNKS
    n = tokens.shape[0] // pieces
    sds = jax.ShapeDtypeStruct
    own = (pieces, n, width)
    all_rows = (pieces, 4, n, width)
    all_units = (pieces, 4, n, units)
    chunk_down, chunk_up = (units // (2 * RING), width), (width // (2 * RING), units)
    states = [sds((2, *chunk), bf16) for chunk in (chunk_down, chunk_up, chunk_up)] if ringed else []
    return pl.pallas_call(
        functools.partial(middle_kernel, ringed),
        in_specs=[VMEM] * 4 + [ANY] * 5,
        out_specs=[VMEM] + [ANY] * 7 + [VMEM] + [ANY] * len(states),
        out_shape=[
            sds(own, f32),
            sds((4, pieces, n, heads), bf16),
            sds(all_rows, bf16),
            sds(own, f32),
            sds((units, width), bf16),
            sds((width, units), bf16),
            sds((width, units), bf16),
            sds((heads, width), bf16),
            sds((8, width), f32),
            *states,
        ],
        scratch_shapes=[
            pltpu.VMEM(all_rows, bf16),
            pltpu.VMEM(all_rows, bf16),
            pltpu.VMEM(all_units, bf16),
            pltpu.VMEM(all_units, bf16),
            pltpu.VMEM(all_units, bf16),
            pltpu.VMEM(all_rows, bf16),
            pltpu.VMEM((pieces, 2, n, width), bf16),
            pltpu.VMEM(own, bf16),
            pltpu.VMEM((pieces, 2, n, width), bf16),
            pltpu.VMEM((n, width), f32),
            pltpu.VMEM((4, n, heads), bf16),
            pltpu.VMEM((2, 256, width), bf16),
            *[pltpu.VMEM(w.shape, bf16) for w in (wg, wu, wd)],
            *dma_sems(12, pieces),
            pltpu.SemaphoreType.DMA((7,)),
            pltpu.SemaphoreType.DMA((pieces,)),
            pltpu.SemaphoreType.DMA((1,)),
            pltpu.SemaphoreType.DMA((1,)),
            pltpu.SemaphoreType.DMA((2,)),
            pltpu.SemaphoreType.REGULAR((3, pieces)),
            *([pltpu.SemaphoreType.DMA((2, IN_MIDDLE))] * 9 + [pltpu.SemaphoreType.DMA((3, 2))]) * ringed,
        ],
        compiler_params=comm_params(2),
        cost_estimate=cost(150e-6 * 1e15, 80e6),
        name="middle",
    )(
        attended.reshape(4, pieces, n, heads), wo, tokens.reshape(own), gains,
        cot_own.reshape(own), cots, wg, wu, wd,
    )


def end_kernel(count, *refs):
    refs = list(refs)
    take = lambda n: [refs.pop(0) for _ in range(n)]
    loaded, gains, gain_two, parts_in = take(10), *take(3)
    parts, states, dwo = take(count), take(count), take(1 if count else 0)
    grad_ref, gains_ref, out_ref = take(3)
    fulls = take(count + 3 if count else 0)
    dw_out = take(0 if count else 2)
    inputs = take(10)
    dq, dk, dv, wq, wk, wv, attn_in, tokens, grad_one, hid1 = inputs
    terms, cr, xr, out_mine, out_side, out_across, gain_sum, gain_land, dwq, dwkv = take(10)
    send_sem, recv_sem, load_sem, gain_send, gain_recv, in_sem = take(6)
    own, width = tokens.shape
    rows = own // CHUNKS
    sems = (send_sem, recv_sem)
    gain = gains.at[0:1]
    fetch = [pltpu.make_async_copy(source, target, in_sem.at[i]) for i, (source, target) in enumerate(zip(loaded, inputs))]

    def at(base, k):
        return pl.ds(pl.multiple_of(base + k * rows, rows), rows)

    def term(p, k):
        here = at(p * own, k)
        return dot(dq[here], wq[...], NT) + dot(dk[here], wk[...], NT) + dot(dv[here], wv[...], NT)

    side0 = lambda k: send(terms.at[at(0, k)], cr.at[0, at(0, k)], sems, (0, k), 1)
    side1 = lambda k: send(terms.at[at(own, k)], cr.at[1, at(0, k)], sems, (1, k), 1)
    across = lambda k: send(terms.at[at(2 * own, k)], xr.at[at(0, k)], sems, (2, k), 2)
    out_load = [pltpu.make_async_copy(parts_in.at[:, 2 - 2 * k], out_mine.at[k], load_sem.at[k]) for k in range(2)]
    out_from_side = [send(parts_in.at[:, 3 - 2 * k], out_side.at[k], sems, (3, k), 1) for k in range(2)]
    out_from_across = send(out_mine.at[0], out_across, sems, (3, 2), 2)

    reduces, late, early_spreads, late_spreads = [], [], [], []
    if count:
        for a in range(count):
            land, mine, *own_sems = take(5)
            reduces.append(Reduce(parts[a], states[a], slots(land), slots(mine), IN_BACK, RING - 1, *own_sems))
        land, mine, *own_sems = take(5)
        late.append(Reduce(dwo[0], None, slots(land), slots(mine), 0, RING - 1, *own_sems))
        for part in (dwq, dwkv):
            land, *own_sems = take(3)
            late.append(Reduce(part, None, slots(land), None, 0, RING - 1, *own_sems))
        spreads = [Spread(r, full, *take(3)) for r, full in zip([*reduces, *late], fulls)]
        early_spreads, late_spreads = spreads[:count], spreads[count:]

    for copy in fetch:
        copy.start()
    if count:
        dp = lax.axis_index("dp")
        flip = lambda bit: {"dp": dp + bit - 2 * bit * lax.rem(lax.div(dp, bit), 2)}
        meet(partner(1), partner(2), ring_peer(0), ring_peer(1), flip(1), flip(2), flip(4))
        for ring in (*reduces, late[0]):
            ring.start()
        for ring in (*reduces, late[0]):
            ring.prefetch()
    else:
        meet(partner(1), partner(2))
    for copy in fetch[:6]:
        copy.wait()

    @pl.loop(0, CHUNKS)
    def _(k):
        terms[at(0, k)] = term(3, k).astype(bf16)
        side0(k).start()

    for k in range(2):
        out_load[k].start()
        out_from_side[k].start()

    @pl.loop(0, CHUNKS)
    def _(k):
        mine = term(2, k)
        side0(k).wait_recv()
        terms[at(2 * own, k)] = (mine + cr[0, at(0, k)].astype(f32)).astype(bf16)
        across(k).start()

    for ring, following in zip(reduces, early_spreads):
        ring.step(0)
        following.start()

    chunk = dwq.shape[2]
    tall = 4 * chunk
    fetch[6].wait()
    merge_q, merge_kv = spread(dwq.shape[3] // HEAD_SIZE), spread(dwkv.shape[3] // HEAD_SIZE)

    @pl.loop(0, width // tall)
    def _(k):
        part = attn_in[:, pl.ds(pl.multiple_of(k * tall, LANES), tall)]
        block_q = dot(dot(part, dq[...], TN).astype(bf16), merge_q, NT).astype(bf16)
        padded = jnp.concatenate([dot(part, d[...], TN).astype(bf16) for d in (dk, dv)], axis=1)
        block_kv = dot(padded, merge_kv, NT).astype(bf16)
        for i in range(4):
            number = k * 4 + i
            here = (lax.div(number, RING), lax.rem(number, RING))
            dwq[here] = block_q[i * chunk : (i + 1) * chunk]
            dwkv[here] = block_kv[i * chunk : (i + 1) * chunk]

    if count:
        late[0].step(0)
        for ring in late[1:]:
            ring.start()
        late[0].step(1)
    else:
        stored = [pltpu.make_async_copy(s, t, load_sem.at[2 + i]) for i, (s, t) in enumerate(zip((dwq, dwkv), dw_out))]
        for copy in stored:
            copy.start()
        for copy in stored:
            copy.wait()

    out_load[0].wait()
    out_from_side[0].wait_recv()

    @pl.loop(0, CHUNKS)
    def _(k):
        out_mine[0, k] = (out_mine[0, k].astype(f32) + out_side[0, k].astype(f32)).astype(bf16)

    out_from_across.start()

    def early(numbers, k):
        for a in numbers:
            if a < count:
                early_spreads[a].step(k)

    def onward(turn):
        for a, ring in enumerate(late):
            ahead = 2 if a == 0 else 0
            if turn < RING - 1:
                if turn + ahead < RING - 1:
                    ring.step(turn + ahead)
                if turn == RING - 2:
                    late_spreads[a].start()
            else:
                late_spreads[a].step(turn - (RING - 1))

    early((0,), 0)

    @pl.loop(0, CHUNKS)
    def _(k):
        terms[at(own, k)] = term(1, k).astype(bf16)
        side1(k).start()
        grad_ref[at(0, k)] = term(0, k)

    onward(0)
    early((1, 2), 0)
    onward(1)

    def tokens_back():
        for copy in fetch[7:9]:
            copy.wait()
        gain_sum[...] = jnp.zeros_like(gain_sum)
        gain_sum[1:2] = jnp.sum(gain_two[...], axis=0, keepdims=True)

        @pl.loop(0, CHUNKS)
        def _(k):
            side1(k).wait_recv()
            across(k).wait_recv()
            here = at(0, k)
            grad = grad_ref[here] + cr[1, here].astype(f32) + xr[here].astype(f32)
            back, sums = rows_back(grad, tokens[here].astype(f32), gain[...])
            grad_ref[here] = grad_one[here] + back
            gain_sum[0:1] += jnp.sum(sums, axis=0, keepdims=True)

        gain_copy(0).start()

    def gain_copy(stage):
        to = [partner(1), partner(2)] + ([flip(1), flip(2), flip(4)] if count else [])
        return pltpu.make_async_remote_copy(
            src_ref=gain_sum,
            dst_ref=gain_land.at[stage],
            send_sem=gain_send.at[stage],
            recv_sem=gain_recv.at[stage],
            device_id=to[stage],
            device_id_type=pl.DeviceIdType.MESH,
        )

    def gain_add(stage):
        gain_copy(stage).wait()
        gain_sum[...] += gain_land[stage]

    def output():
        fetch[9].wait()
        out_load[1].wait()
        out_from_side[1].wait_recv()
        out_from_across.wait_recv()

        @pl.loop(0, CHUNKS)
        def _(k):
            total = out_mine[1, k].astype(f32) + out_side[1, k].astype(f32) + out_across[k].astype(f32)
            out_ref[k] = (hid1[k] + total).astype(bf16)

    for turn in range(1, RING - 1):
        if turn == 2:
            tokens_back()
        if turn == 3:
            gain_add(0)
            gain_copy(1).start()
        if turn == 4:
            gain_add(1)
            if count:
                gain_copy(2).start()
            output()
        if turn == 5 and count:
            gain_add(2)
            gain_copy(3).start()
        if turn == 6 and count:
            gain_add(3)
            gain_copy(4).start()
        early((0,), turn)
        if count:
            onward(2 * turn)
        early((1, 2), turn)
        if count:
            onward(2 * turn + 1)
    if count:
        gain_add(4)
    for ring in (*reduces, *late, *early_spreads, *late_spreads):
        ring.finish()
    gains_ref[...] = gain_sum[...]

    @pl.loop(0, CHUNKS)
    def _(k):
        side0(k).wait_send()
        side1(k).wait_send()
        across(k).wait_send()

    for k in range(2):
        out_from_side[k].wait_send()
    out_from_across.wait_send()


def end(dq, dk, dv, wq, wk, wv, attn_in, tokens, grad_one, hid1, gains, gain_two, parts_in, parts, states, dwo, cuts):
    own, width = tokens.shape
    count = len(parts)
    sds = jax.ShapeDtypeStruct
    pieces = hid1.shape
    loaded = (dq, dk, dv, wq, wk, wv, attn_in, tokens, grad_one, hid1)
    qkv_shapes = [(2, RING, width // (2 * RING), c) for c in cuts]
    late = [dwo] if count else []
    ring_shapes = [*[p.shape for p in parts], dwo.shape, *qkv_shapes] if count else qkv_shapes
    ring_buffers = []
    for p in parts:
        ring_buffers += ring_scratch(p.shape, RING - 1 - IN_BACK, True)
    if count:
        ring_buffers += ring_scratch(dwo.shape, RING - 1, True)
        for shape in qkv_shapes:
            ring_buffers += ring_scratch(shape, RING - 1, False)
        for _ in ring_shapes:
            ring_buffers += [pltpu.SemaphoreType.DMA((2, RING - 1))] * 2 + [pltpu.SemaphoreType.DMA((2,))]
    stages = 5 if count else 2
    outs = pl.pallas_call(
        functools.partial(end_kernel, count),
        in_specs=[ANY] * 10 + [VMEM] * 2 + [ANY] * (1 + 2 * count + len(late)),
        out_specs=[VMEM] * 3 + [ANY] * len(ring_shapes),
        out_shape=[
            sds((own, width), f32),
            sds((8, width), f32),
            sds(pieces, bf16),
            *[sds(shape, bf16) for shape in ring_shapes],
        ],
        scratch_shapes=[
            *[pltpu.VMEM(t.shape, t.dtype) for t in loaded],
            pltpu.VMEM((3 * own, width), bf16),
            pltpu.VMEM((2, own, width), bf16),
            pltpu.VMEM((own, width), bf16),
            pltpu.VMEM((2, *pieces), bf16),
            pltpu.VMEM((2, *pieces), bf16),
            pltpu.VMEM(pieces, bf16),
            pltpu.VMEM((8, width), f32),
            pltpu.VMEM((stages, 8, width), f32),
            *[pltpu.VMEM(shape, bf16) for shape in qkv_shapes],
            *dma_sems(4, max(CHUNKS, 3)),
            pltpu.SemaphoreType.DMA((4,)),
            *dma_sems(stages),
            pltpu.SemaphoreType.DMA((10,)),
            *ring_buffers,
        ],
        compiler_params=comm_params(3),
        cost_estimate=cost(150e-6 * 1e15, 60e6),
        name="end",
    )(*loaded, gains, gain_two, parts_in, *parts, *states, *late)
    return outs[:3], outs[3:]


def body(
    tokens, segments, positions, norm_attn, w_query, key_weight, value_weight, w_out,
    norm_mlp, w_gate, w_up, w_down, cotangent,
):
    seq = segments.shape[0]
    own, width = tokens.shape
    blocks = 4
    heads_q, heads_k = w_query.shape[1], key_weight.shape[1]
    gains = jnp.stack([norm_attn, norm_mlp])

    qkv, attn_in, attended, lse, cots, wq, wk, wv, wo, cos, sin, start = front(
        tokens, gains, w_query, key_weight, value_weight, w_out, segments.reshape(1, seq), positions.reshape(seq, 1),
        cotangent, blocks,
    )
    ringed = lax.axis_size("dp") == RING
    hid1, grad_attended, parts, grad_one, dwd, dwg, dwu, dwo, gain_two, *states = middle(
        attended, wo, tokens, gains, cotangent, cots, w_gate, w_up, w_down, ringed
    )
    grad_attended = grad_attended.reshape(seq, -1)
    dwo = dot(spread(heads_q // HEAD_SIZE), dwo).astype(bf16)
    chunks = lambda t: t.reshape(2, RING, t.shape[0] // (2 * RING), t.shape[1])
    early = [chunks(t) for t in (dwd, dwg, dwu)] if ringed else []
    (dq, dk, dv), states = attend_back(
        qkv, attended, grad_attended, lse, start, cos, sin, early, states, blocks
    )
    (grad_tokens, gain_grads, output), sums = end(
        dq, dk, dv, wq, wk, wv, attn_in.reshape(seq, width), tokens, grad_one.reshape(own, width), hid1, gains,
        gain_two, parts, early, states, chunks(dwo) if ringed else None, (heads_q, 2 * heads_k),
    )
    output = output.reshape(own, width)
    if not ringed:
        gain_grads = lax.psum(gain_grads, "dp")
        sums = [lax.psum(t, "dp") for t in (dwd, dwg, dwu, dwo, *sums)]
    down, gate, up, out, query, both = [t.reshape(-1, t.shape[-1]) for t in sums]
    key, value = both[:, :heads_k], both[:, heads_k:]
    return (
        output, grad_tokens, gain_grads[0],
        *[t.astype(f32) for t in (query, key, value, out)],
        gain_grads[1], *[t.astype(f32) for t in (gate, up, down)],
    )


def solution(mesh):
    rows, cols, both = P("tensor", None), P(None, "tensor"), P(("dp", "tensor"), None)
    in_specs = (both, P("dp"), P("dp"), P(), cols, cols, cols, rows, P(), cols, cols, rows, both)
    out_specs = (both, both, P(), cols, cols, cols, rows, P(), cols, cols, rows)
    return jax.shard_map(body, mesh=mesh, in_specs=in_specs, out_specs=out_specs, check_vma=False)
```

time: 609 us -> 519 us (0.85)
  Pallas kernels: 536 us -> 471 us
  other arithmetic: 32 us -> 17.8 us
  matrix products: 12.6 us -> 3.26 us
    pallas_call x4 -> x3, Pallas kernels: 474 us -> 425 us  [the longest x1 181 us: end(): pl.pallas_call(functools.partial(end_kernel, count), in_specs=[ANY] * 10...]
    pallas_call x1, Pallas kernels: 61.4 us -> 46.4 us  [attend_back(): pl.pallas_call(functools.partial(attend_back_kernel, count, blocks=blocks...]
    dot_general x5 -> x1, matrix products: 12.6 us -> 3.26 us  [dot(): return lax.dot_general(left, right, dims, preferred_element_type=f32)]
    convert_element_type x7 -> x6, other arithmetic: 20.2 us -> 16.6 us  [body(): t.astype(f32)]
where the time goes in v4:
time: 519 us; the launch traced here: 510 us
  Pallas kernels  471 us (91%)
  other arithmetic  17.8 us (3%)
  local copies, waits for them, and re-layouts  16.7 us (3%)
    pallas_call x1, Pallas kernels, end(): pl.pallas_call(functools.partial(end_kernel, count), in_specs=[ANY] * 10...  181 us
    pallas_call x1, Pallas kernels, middle(): pl.pallas_call(functools.partial(middle_kernel, ringed), in_specs=[VMEM]...  168 us
    pallas_call x1, Pallas kernels, front(): pl.pallas_call(functools.partial(front_kernel, blocks=blocks), in_specs=[...  76.3 us
    pallas_call x1, Pallas kernels, attend_back(): pl.pallas_call(functools.partial(attend_back_kernel, count, blocks=blocks...  46.4 us
    convert_element_type x6, other arithmetic, body(): t.astype(f32)  16.6 us
    unnamed x22, local copies, waits for them, and re-layouts  10.7 us

profile of v4, /device:TPU:24, one launch (start us, length us, event | category | flops | bytes accessed | tf_op | source)
XLA Modules:
  0.0 509.8 jit_solution(12165126060366584489)
XLA Ops:
  1.2 0.7 stack.9
  1.9 0.7 stack.10
  2.6 0.6 pad_maximum_fusion.gains.refs_10_
  3.3 2.2 copy.28.key_weight
  5.5 2.2 copy.29.value_weight
  7.7 1.3 copy.30.positions
  9.0 76.3 %front.1 = (bf16[2048,1024]{1,0:T(8,128)(2,1)}, bf16[4,512,1536]{2,1,0:T(8,128)(2,1)}, bf16[2048,512]{1,0:T(8,128)(2,1)}, f32[2,2,2048]{2,1,0:T(2,128)}, bf16[3,...) custom-call(bf16[512,1536]{1,0:T(8,128)(2,1)} %refs_7_.1, ...), custom_call_target="tpu_custom_call" | custom-call | flops 80000000000 | bytes 40000000 | tf_op jit(solution)/shard_map/front/pallas_call | solution.py:396
  85.4 167.8 %middle.1 = (f32[4,128,1536]{2,1,0:T(8,128)}, bf16[4,4,128,512]{3,2,1,0:T(8,128)(2,1)}, bf16[4,4,128,1536]{3,2,1,0:T(8,128)(2,1)}, f32[4,128,1536]{2,1,0:T(8,128...) custom-call(bf16[4,4,128,512]{3,2,1,0:T(8,128)(2,1)} %bitcast.45, ...), custom_call_target="tpu_custom_call" | custom-call | flops 149999992832 | bytes 80000000 | tf_op jit(solution)/shard_map/middle/pallas_call | solution.py:855
  253.1 46.4 %attention_back.1 = (bf16[2048,512]{1,0:T(8,128)(2,1)}, bf16[2048,256]{1,0:T(8,128)(2,1)}, bf16[2048,256]{1,0:T(8,128)(2,1)}, bf16[2,64,1536]{2,1,0:T(8,128)(2,1...) custom-call(bf16[2048,1024]{1,0:T(8,128)(2,1)} %get-tuple-element.50.refs_0_.refs_1_.refs_2_, ...), custom_call_target="tpu_custom_call" | custom-call | flops 21474836480 | bytes 20971520 | tf_op jit(solution)/shard_map/attention_back/pallas_call | solution.py:535
  299.6 3.3 convolution_convert_fusion
  302.8 180.6 %end.1 = (f32[512,1536]{1,0:T(8,128)}, f32[8,1536]{1,0:T(8,128)}, bf16[4,128,1536]{2,1,0:T(8,128)(2,1)}, bf16[2,8,64,1536]{3,2,1,0:T(8,128)(2,1)}, bf16[2,8,96,1...) custom-call(bf16[2048,512]{1,0:T(8,128)(2,1)} %get-tuple-element.65., ...), custom_call_target="tpu_custom_call" | custom-call | flops 149999992832 | bytes 60000000 | tf_op jit(solution)/shard_map/end/pallas_call | solution.py:1152
  483.4 1.5 slice_reduce_fusion
  484.9 1.7 fusion.11
  486.9 1.1 convert_element_type.47
  488.3 1.1 convert_element_type.46
  489.5 1.7 bitcast_convert_fusion.4
  491.1 1.8 bitcast_convert_fusion.3
  492.9 1.0 copy-done.3
  493.9 4.1 bitcast_convert_fusion
  498.0 0.6 copy-done.1
  498.6 6.7 %bitcast_convert_fusion.1 = (f32[1536,1024]{1,0:T(8,128)}, f32[1536,1024]{1,0:T(8,128)}) fusion(bf16[2,8,96,1024]{3,2,1,0:T(8,128)(2,1)S(1)} %copy-done.1, bf16[2,8,96,1024]{3,2,1,0:T(8,128)(2,1)S(1)} %copy-done), kind=kLoop, calls=%fused_computation.1 | loop fusion | flops 3145728 | bytes 18874368 | tf_op jit(solution)/shard_map/convert_element_type | solution.py:1224
  505.4 1.1 copy.37
  506.5 1.3 copy-done.2
  507.8 1.7 copy.38
  (16 shorter events, 1.1 us)
Async XLA Ops:
  0.6 7.0 %copy-start.7 = (s32[2048]{0:T(1024)S(1)}, s32[2048]{0:T(1024)}, u32[]{:S(2)}) copy-start(s32[2048]{0:T(1024)} %param.15) | copy-start | bytes 24580
  486.9 2.6 copy-start.6
  488.3 2.8 copy-start.5
  491.1 2.7 copy-start.3
  493.9 4.1 copy-start
  493.9 4.7 copy-start.1
  498.6 6.7 %copy-start.4 = (bf16[4,128,1536]{2,1,0:T(8,128)(2,1)S(1)}, bf16[4,128,1536]{2,1,0:T(8,128)(2,1)}, u32[]{:S(2)}) copy-start(bf16[4,128,1536]{2,1,0:T(8,128)(2,1)} %get-tuple-element.80) | copy-start | bytes 4718596
  505.4 2.5 copy-start.2

commit v5 on v4

--- a/solution.py
+++ b/solution.py
@@ -77,8 +77,7 @@
 
 
 RING = 8
-IN_MIDDLE = 3
-IN_BACK = 6
+IN_MIDDLE = (6, 3, 3)
 
 
 def ring_place():
@@ -128,22 +127,22 @@
         for way in range(2):
             self.begin(way).start()
 
-    def prefetch(self):
-        for k in range(self.count):
+    def prefetch(self, steps=None):
+        for k in steps or range(self.count):
             for way in range(2):
                 self.load(way, k).start()
 
     def step(self, k):
         for way in range(2):
-            (self.copy(way, k) if k else self.begin(way)).wait_recv()
+            here = self.land(way, k)
+            ring_send(here, here, self.sems, (way, k), way).wait_recv()
             if self.mine is None:
                 own = self.parts[way, ring_chunk(way, self.first + k + 1)]
             else:
                 self.load(way, k).wait()
                 own = self.mine(way, k)[...]
-            here = self.land(way, k)
             here[...] = (here[...].astype(f32) + own.astype(f32)).astype(bf16)
-            if k + 1 < self.count:
+            if not isinstance(k, int) or k + 1 < self.count:
                 self.copy(way, k + 1).start()
 
     def result(self, way):
@@ -188,6 +187,14 @@
                 self.copy(way, k).wait_send()
 
 
+class Reduced:
+    def __init__(self, state):
+        self.state = state
+
+    def result(self, way):
+        return self.state.at[way]
+
+
 def slots(ref):
     return lambda way, k: ref.at[way, k]
 
@@ -197,6 +204,10 @@
     land = pltpu.VMEM((2, steps, rows, cols), bf16)
     sems = [pltpu.SemaphoreType.DMA((2, steps))] * (3 if loads else 2)
     return [land] * (2 if loads else 1) + sems
+
+
+def as_row(ref):
+    return jnp.concatenate([ref[i : i + 1, :] for i in range(ref.shape[0])], axis=1)
 
 
 def comm_params(number):
@@ -218,7 +229,7 @@
 
 
 def front_kernel(
-    tokens, gains, w_query, key_weight, value_weight, w_out, segments, positions, cot,
+    tokens, gain_ref, w_query, key_turned, value_turned, w_out, segments, positions, cot,
     qkv_out, stack_out, att_out, lse_out, cots, wq_out, wk_out, wv_out, wo_out, cos_out, sin_out, start_out,
     x, land, qkv, att, wq, wk, wv, wo, cos_v, sin_v, send_sem, recv_sem, store_sem,
     *, blocks,
@@ -245,25 +256,26 @@
         copy.start()
         stores.append(copy)
 
+    gain = as_row(gain_ref)
     meet(partner(1), partner(2))
 
     @pl.loop(0, CHUNKS)
     def _(k):
         inputs = tokens[piece(k)].astype(f32)
         inverse = lax.rsqrt(jnp.mean(inputs * inputs, axis=-1, keepdims=True) + epsilon)
-        x[piece(k)] = (inputs * inverse * gains[0:1, :]).astype(bf16)
+        x[piece(k)] = (inputs * inverse * gain).astype(bf16)
         across(k).start()
 
     side.start()
     store(x, stack_out.at[0])
 
-    spread_q, spread_k = spread(w_query.shape[1] // HEAD_SIZE), spread(key_weight.shape[1] // HEAD_SIZE)
-    for source, matrix, target, out in (
-        (w_query, spread_q, wq, wq_out),
-        (key_weight, spread_k, wk, wk_out),
-        (value_weight, spread_k, wv, wv_out),
+    spread_q, spread_k = spread(w_query.shape[1] // HEAD_SIZE), spread(key_turned.shape[0] // HEAD_SIZE)
+    for source, matrix, dims, target, out in (
+        (w_query, spread_q, NN, wq, wq_out),
+        (key_turned, spread_k, TN, wk, wk_out),
+        (value_turned, spread_k, TN, wv, wv_out),
     ):
-        target[...] = dot(source[...], matrix).astype(bf16)
+        target[...] = dot(source[...], matrix, dims).astype(bf16)
         store(target, out)
     wo[...] = dot(spread(w_query.shape[1] // HEAD_SIZE, True), w_out[...]).astype(bf16)
     store(wo, wo_out)
@@ -273,13 +285,14 @@
     frequency = jnp.exp(feature.astype(f32) * (-2.0 * math.log(rope_base) / HEAD_SIZE))
     frequency = jnp.where(feature < HALF, frequency, 0.0)
     sign = jnp.where(lane < LANES // 2, -1.0, 1.0)
+    per_own = own // LANES
     for p in range(4):
 
-        @pl.loop(0, CHUNKS)
+        @pl.loop(0, per_own)
         def _(k):
-            base = pl.multiple_of(peer(p) * own + k * rows, rows)
-            angles = positions[pl.ds(base, rows), :].astype(f32) * frequency
-            here = pl.ds(pl.multiple_of(p * own + k * rows, rows), rows)
+            row = positions[pl.ds(peer(p) * per_own + k, 1), :].astype(f32)
+            angles = jnp.broadcast_to(row, (LANES, LANES)).T * frequency
+            here = pl.ds(pl.multiple_of(p * own + k * LANES, LANES), LANES)
             cos_v[here] = jnp.cos(angles)
             sin_v[here] = jnp.sin(angles) * sign
 
@@ -288,9 +301,12 @@
     documents = segments[...].astype(f32)
     starts = jnp.zeros_like(documents)
     for document in (1, 2, 3):
-        first = jnp.sum(jnp.where(documents < document, 1.0, 0.0), axis=1, keepdims=True)
+        first = jnp.where(documents < document, 1.0, 0.0)
+        first = jnp.sum(jnp.sum(first, axis=0, keepdims=True), axis=1, keepdims=True)
         starts = jnp.where(documents >= document, first, starts)
-    start_out[...] = starts.astype(jnp.int32)
+    starts = starts.astype(jnp.int32)
+    for i in range(seq // LANES):
+        start_out[:, i * LANES : (i + 1) * LANES] = starts[i : i + 1, :]
 
     head_lane = lax.broadcasted_iota(jnp.int32, (rows, LANES), 1)
 
@@ -380,9 +396,9 @@
         copy.wait()
 
 
-def front(tokens, gains, w_query, key_weight, value_weight, w_out, segments, positions, cot, blocks):
+def front(tokens, gain, w_query, key_turned, value_turned, w_out, segments, positions, cot, blocks):
     own, width = tokens.shape
-    seq = segments.shape[1]
+    seq = segments.shape[0] * LANES
     pieces = (CHUNKS, own // CHUNKS, width)
     sds = jax.ShapeDtypeStruct
     heads = 4 * LANES
@@ -413,7 +429,7 @@
         compiler_params=comm_params(1),
         cost_estimate=cost(80e-6 * 1e15, 40e6),
         name="front",
-    )(tokens, gains, w_query, key_weight, value_weight, w_out, segments, positions, cot.reshape(pieces))
+    )(tokens, gain, w_query, key_turned, value_turned, w_out, segments, positions, cot.reshape(pieces))
 
 
 def attend_back_kernel(count, *refs, blocks, size):
@@ -425,8 +441,7 @@
     rings = []
     for a in range(count):
         land, mine, *own_sems = rest[5 * a : 5 * a + 5]
-        rings.append(Reduce(parts[a], befores[a], slots(land), slots(mine), IN_MIDDLE, IN_BACK, *own_sems))
-    steps = IN_BACK - IN_MIDDLE
+        rings.append(Reduce(parts[a], befores[a], slots(land), slots(mine), IN_MIDDLE[a], RING - 1, *own_sems))
     keep_sem = rest[-1] if count else None
 
     def keep(a, way):
@@ -437,16 +452,16 @@
         @pl.when(pl.program_id(0) == 0)
         def _():
             meet(ring_peer(0), ring_peer(1))
-            for ring in rings:
+            for ring in sorted(rings, key=lambda ring: -ring.count):
                 ring.start()
             for ring in rings:
                 ring.prefetch()
 
     pairs = blocks * (blocks + 1) // 2
     hooks = {}
-    for number in range(count * steps):
-        due = min(round((number + 1) * 2.25) + 1, 2 * pairs - 1)
-        hooks.setdefault(due, []).append((number % count, number // count))
+    turns = sorted((k, -rings[a].count, a) for a in range(count) for k in range(rings[a].count))
+    for number, (k, _, a) in enumerate(turns):
+        hooks.setdefault(min(round((number + 1) * 2.1) + 1, 2 * pairs - 1), []).append((a, k))
 
     def hook(pair):
         for half in range(2):
@@ -457,7 +472,7 @@
                 def _():
                     for a, k in todo:
                         rings[a].step(k)
-                        if k == steps - 1:
+                        if k == rings[a].count - 1:
                             keep(a, 0).start()
                             keep(a, 1).start()
 
@@ -553,7 +568,7 @@
             pltpu.VMEM((seq, LANES), f32),
             pltpu.VMEM((seq, LANES), f32),
             pltpu.VMEM((2, seq), f32),
-            *[x for p in parts for x in ring_scratch(p.shape, IN_BACK - IN_MIDDLE, True)],
+            *[x for p, n in zip(parts, IN_MIDDLE) for x in ring_scratch(p.shape, RING - 1 - n, True)],
             *[pltpu.SemaphoreType.DMA((count, 2))] * bool(count),
         ],
         out_shape=[
@@ -593,7 +608,7 @@
 
 
 def middle_kernel(
-    ringed, att, wo, tokens, gains, cot_own, cots, wg_in, wu_in, wd_in,
+    ringed, att, wo, gain_ref, tokens, cot_own, cots, wg_in, wu_in, wd_in,
     hid1, datt_out, parts_out, grad_one_out, dwd_out, dwg_out, dwu_out, dwo_out, gain_grad, *refs,
 ):
     states, refs = (refs[:3], refs[3:]) if ringed else ([], refs)
@@ -601,7 +616,7 @@
         xs, cot, hid, gg, gu, g, cr, xr, part_stage, grad_stage, datt_stage, tile_stage, wg, wu, wd,
         send_sem, recv_sem, cot_sem, part_sem, grad_sem, datt_sem, tile_sem, free_sem, *ring_sems,
     ) = refs
-    gain = gains.at[1:2]
+    gain = as_row(gain_ref)
     pieces, _, n, width = xs.shape
     units = wg.shape[1]
     heads = wo.shape[0]
@@ -632,15 +647,15 @@
 
     def cot_copy(p):
         if p >= 4:
-            source, target = ((wg_in, wg), (wu_in, wu), (wd_in, wd))[p - 4]
+            source, target = ((wg_in, wg), (wu_in, wu), (wd_in, wd), (tokens, xs.at[:, 3]))[p - 4]
             return pltpu.make_async_copy(source, target, cot_sem.at[p])
         source = cot_own if p == 0 else cots.at[p - 1]
         return pltpu.make_async_copy(source, cot.at[:, p], cot_sem.at[p])
 
     def part_copy(k, low):
-        return pltpu.make_async_copy(part_stage.at[k], parts_out.at[k, pl.ds(low, 2)], part_sem.at[k])
-
-    for p in (4, 5, 6, 0, 1, 2, 3):
+        return pltpu.make_async_copy(part_stage.at[low // 2], parts_out.at[k, pl.ds(low, 2)], part_sem.at[low // 2])
+
+    for p in (7, 4, 5, 6, 0, 1, 2, 3):
         cot_copy(p).start()
     meet(partner(1), partner(2), *([ring_peer(0), ring_peer(1)] if ringed else []))
 
@@ -650,12 +665,15 @@
             g[k, p] = dot(att[p, k], wo[...]).astype(bf16)
             copy(kind, k).start()
 
-    @pl.loop(0, pieces)
-    def _(k):
+    def send_across(k):
         term = dot(att[2, k], wo[...])
         copy(RS1_C0, k).wait_recv()
         g[k, 2] = (term + cr[k, 0].astype(f32)).astype(bf16)
         copy(RS1_X, k).start()
+
+    @pl.loop(0, 2)
+    def _(k):
+        send_across(k)
 
     def feed_forward(k, low):
         x = xs[k, pl.ds(low, 2)].reshape(two)
@@ -675,32 +693,50 @@
         return hidden
 
     def out_part(k, low, hidden):
-        part_stage[k] = dot(hidden, wd[...]).astype(bf16).reshape(2, n, width)
+        part = dot(hidden, wd[...]).astype(bf16).reshape(2, n, width)
+
+        @pl.when(k > 0)
+        def _():
+            part_copy(k - 1, low).wait()
+
+        part_stage[low // 2] = part
         part_copy(k, low).start()
 
-    for p in range(7):
+    for p in range(8):
         cot_copy(p).wait()
 
-    @pl.loop(0, pieces)
-    def _(k):
+    def low_rows(k):
         term = dot(att[0, k], wo[...])
         copy(RS1_C1, k).wait_recv()
         copy(RS1_X, k).wait_recv()
-        hidden = tokens[k].astype(f32) + (term + cr[k, 1].astype(f32) + xr[k].astype(f32))
+        hidden = xs[k, 3].astype(f32) + (term + cr[k, 1].astype(f32) + xr[k].astype(f32))
         hid1[k] = hidden
         inverse = lax.rsqrt(jnp.mean(hidden * hidden, axis=-1, keepdims=True) + epsilon)
-        xs[k, 0] = (hidden * inverse * gain[...]).astype(bf16)
+        xs[k, 0] = (hidden * inverse * gain).astype(bf16)
         copy(AG2_X, k).start()
         copy(AG2_C, k).start()
+
+        @pl.when(k + 2 < pieces)
+        def _():
+            send_across(k + 2)
+
         copy(AG2_C, k).wait_recv()
         copy(RS1_C1, k).wait_send()
         out_part(k, 0, feed_forward(k, 0))
 
-    @pl.loop(0, pieces)
-    def _(k):
+    def add_side(k):
+        copy(RS3_C0, k).wait_recv()
+        g[k, 2] = (g[k, 2].astype(f32) + cr[k, 0].astype(f32)).astype(bf16)
+        copy(RS3_X, k).start()
+
+    def high_rows(k):
         copy(AG2_X, k).wait_recv()
         copy(AG2_F, k).start()
-        part_copy(k, 0).wait()
+
+        @pl.when(k >= 2)
+        def _():
+            add_side(k - 2)
+
         copy(AG2_F, k).wait_recv()
         copy(RS1_C0, k).wait_send()
         copy(RS1_X, k).wait_send()
@@ -708,9 +744,20 @@
         copy(RS3_C0, k).start()
         copy(RS3_C1, k).start()
         out_part(k, 2, hidden)
-        copy(RS3_C0, k).wait_recv()
-        g[k, 2] = (g[k, 2].astype(f32) + cr[k, 0].astype(f32)).astype(bf16)
-        copy(RS3_X, k).start()
+
+    @pl.loop(0, pieces + 1)
+    def _(k):
+        @pl.when(k < pieces)
+        def _():
+            low_rows(k)
+
+        @pl.when(k > 0)
+        def _():
+            high_rows(k - 1)
+
+    @pl.loop(pieces - 2, pieces)
+    def _(k):
+        add_side(k)
 
     tokens_all = 4 * pieces * n
 
@@ -731,7 +778,7 @@
         copy(RS3_X, k).wait_send()
         credit(k, 2)
         grad = g[k, 0].astype(f32) + cr[k, 1].astype(f32) + xr[k].astype(f32)
-        back, sums = rows_back(grad, hid1[k], gain[...])
+        back, sums = rows_back(grad, hid1[k], gain)
         result = cot[k, 0].astype(f32) + back
         g[k, 0] = result.astype(bf16)
         pl.semaphore_wait(free_sem.at[0, k], 1)
@@ -767,38 +814,53 @@
     if ringed:
         n_down = dwd_out.shape[0] // (2 * RING)
         n_up = dwg_out.shape[0] // (2 * RING)
+
+        def down_own(way, k):
+            if isinstance(k, int) and k >= 4:
+                return cr.at[k - 4, way, pl.ds(0, n_down)]
+            return cot.at[k, 3, pl.ds(way * n_down, n_down)]
+
         places = (
-            (lambda way, k: cot.at[k, 1 + way, pl.ds(0, n_down)], lambda way, k: cot.at[k, 3, pl.ds(way * n_down, n_down)]),
+            (lambda way, k: cot.at[k % 4, 1 + way, pl.ds(k // 4 * n_down, n_down)], down_own),
             (lambda way, k: hid.at[k, way, pl.ds(0, n_up)], lambda way, k: gg.at[k, way, pl.ds(0, n_up)]),
             (lambda way, k: hid.at[k, 2 + way, pl.ds(0, n_up)], lambda way, k: gu.at[k, way, pl.ds(0, n_up)]),
         )
         for a, (part, (land, mine)) in enumerate(zip((dwd_out, dwg_out, dwu_out), places)):
-            rings.append(Reduce(_Chunks(part), None, land, mine, 0, IN_MIDDLE, *ring_sems[3 * a : 3 * a + 3]))
+            rings.append(Reduce(_Chunks(part), None, land, mine, 0, IN_MIDDLE[a], *ring_sems[3 * a : 3 * a + 3]))
         for way in range(2):
             pl.semaphore_signal(
                 free_sem.at[2, way], inc=1, device_id=ring_peer(1 - way), device_id_type=pl.DeviceIdType.MESH
             )
-
-    @pl.loop(2, 4)
-    def _(k):
-        stored = norm_back(k)
-        for i in range(3):
-            at = 3 * (k - 2) + i
-            gate = tile(0, xs, gg, units, dwg_out, at)
+        for way in range(2):
+            pl.semaphore_wait(free_sem.at[2, way], 1)
+        rings[0].start()
+        rings[0].prefetch(range(4))
+
+    @pl.loop(0, 3)
+    def _(j):
+        for i in range(2):
+            gate = tile(0, xs, gg, units, dwg_out, 2 * j + i)
             gate.start()
-            up = tile(1, xs, gu, units, dwu_out, at)
+            up = tile(1, xs, gu, units, dwu_out, 2 * j + i)
             up.start()
             gate.wait()
             up.wait()
-        stored.wait()
+
+        @pl.when(j == 0)
+        def _():
+            norm_back(2).wait()
+
+        if ringed:
+            rings[0].step(j)
 
     if ringed:
-        for way in range(2):
-            pl.semaphore_wait(free_sem.at[2, way], 1)
-        for ring in rings:
+        for ring in rings[1:]:
             ring.start()
-        for ring in rings:
+        for ring in rings[1:]:
             ring.prefetch()
+    norm_back(3).wait()
+    if ringed:
+        rings[0].prefetch(range(4, IN_MIDDLE[0]))
 
     for k in range(pieces):
         copy(AG3_X, k).wait_recv()
@@ -809,10 +871,21 @@
         moved = pltpu.make_async_copy(datt_stage, datt_out.at[:, k], datt_sem.at[0])
         moved.start()
         moved.wait()
-        if ringed and k > 0:
-            for ring in rings:
-                if k - 1 < IN_MIDDLE - 1:
-                    ring.step(k - 1)
+        if ringed and k < 3:
+            rings[1].step(k)
+            rings[2].step(k)
+            rings[0].step(3 + k)
+
+    if ringed:
+        for a, ring in enumerate(rings):
+            for way in range(2):
+                pltpu.make_async_copy(ring.result(way), states[a].at[way], ring_sems[-1].at[a, way]).start()
+    merge = spread(2)
+    tall = merge.shape[0]
+
+    def out_tile(u):
+        target = dwo_out.at[pl.ds(u * tall, tall)]
+        return pltpu.make_async_copy(tile_stage.at[u, pl.ds(0, tall)], target, tile_sem.at[u])
 
     for u in range(heads // 256):
         total = None
@@ -820,29 +893,27 @@
             left = att[p, :, :, u * 256 : (u + 1) * 256].reshape(pieces * n, 256)
             term = dot(left, g[:, p].reshape(pieces * n, width), TN)
             total = term if total is None else total + term
-        tile_stage[u] = total.astype(bf16)
-        pltpu.make_async_copy(tile_stage.at[u], dwo_out.at[pl.ds(u * 256, 256)], tile_sem.at[u]).start()
+        tile_stage[u, 0:tall] = dot(merge, total.astype(bf16)).astype(bf16)
+        out_tile(u).start()
     for u in range(heads // 256):
-        pltpu.make_async_copy(tile_stage.at[u], dwo_out.at[pl.ds(u * 256, 256)], tile_sem.at[u]).wait()
+        out_tile(u).wait()
 
     if ringed:
-        for a, ring in enumerate(rings):
-            ring.step(IN_MIDDLE - 1)
-            for way in range(2):
-                pltpu.make_async_copy(ring.result(way), states[a].at[way], ring_sems[-1].at[a, way]).start()
         for a, ring in enumerate(rings):
             ring.finish()
             for way in range(2):
                 pltpu.make_async_copy(ring.result(way), states[a].at[way], ring_sems[-1].at[a, way]).wait()
 
+    for low in (0, 2):
+        part_copy(pieces - 1, low).wait()
+
     @pl.loop(0, pieces)
     def _(k):
-        part_copy(k, 2).wait()
         for kind in (AG2_X, AG2_C, AG2_F, AG3_X, AG3_C, AG3_F):
             copy(kind, k).wait_send()
 
 
-def middle(attended, wo, tokens, gains, cot_own, cots, wg, wu, wd, ringed):
+def middle(attended, wo, tokens, gain, cot_own, cots, wg, wu, wd, ringed):
     width, units, heads = wg.shape[0], wg.shape[1], wo.shape[0]
     pieces = CHUNKS
     n = tokens.shape[0] // pieces
@@ -854,7 +925,7 @@
     states = [sds((2, *chunk), bf16) for chunk in (chunk_down, chunk_up, chunk_up)] if ringed else []
     return pl.pallas_call(
         functools.partial(middle_kernel, ringed),
-        in_specs=[VMEM] * 4 + [ANY] * 5,
+        in_specs=[VMEM] * 3 + [ANY] * 6,
         out_specs=[VMEM] + [ANY] * 7 + [VMEM] + [ANY] * len(states),
         out_shape=[
             sds(own, f32),
@@ -864,7 +935,7 @@
             sds((units, width), bf16),
             sds((width, units), bf16),
             sds((width, units), bf16),
-            sds((heads, width), bf16),
+            sds((heads * HEAD_SIZE // LANES, width), bf16),
             sds((8, width), f32),
             *states,
         ],
@@ -877,25 +948,25 @@
             pltpu.VMEM(all_rows, bf16),
             pltpu.VMEM((pieces, 2, n, width), bf16),
             pltpu.VMEM(own, bf16),
-            pltpu.VMEM((pieces, 2, n, width), bf16),
+            pltpu.VMEM((2, 2, n, width), bf16),
             pltpu.VMEM((n, width), f32),
             pltpu.VMEM((4, n, heads), bf16),
             pltpu.VMEM((2, 256, width), bf16),
             *[pltpu.VMEM(w.shape, bf16) for w in (wg, wu, wd)],
             *dma_sems(12, pieces),
-            pltpu.SemaphoreType.DMA((7,)),
-            pltpu.SemaphoreType.DMA((pieces,)),
+            pltpu.SemaphoreType.DMA((8,)),
+            pltpu.SemaphoreType.DMA((2,)),
             pltpu.SemaphoreType.DMA((1,)),
             pltpu.SemaphoreType.DMA((1,)),
             pltpu.SemaphoreType.DMA((2,)),
             pltpu.SemaphoreType.REGULAR((3, pieces)),
-            *([pltpu.SemaphoreType.DMA((2, IN_MIDDLE))] * 9 + [pltpu.SemaphoreType.DMA((3, 2))]) * ringed,
+            *([pltpu.SemaphoreType.DMA((2, n)) for n in IN_MIDDLE for _ in range(3)] + [pltpu.SemaphoreType.DMA((3, 2))]) * ringed,
         ],
         compiler_params=comm_params(2),
         cost_estimate=cost(150e-6 * 1e15, 80e6),
         name="middle",
     )(
-        attended.reshape(4, pieces, n, heads), wo, tokens.reshape(own), gains,
+        attended.reshape(4, pieces, n, heads), wo, gain, tokens.reshape(own),
         cot_own.reshape(own), cots, wg, wu, wd,
     )
 
@@ -903,9 +974,9 @@
 def end_kernel(count, *refs):
     refs = list(refs)
     take = lambda n: [refs.pop(0) for _ in range(n)]
-    loaded, gains, gain_two, parts_in = take(10), *take(3)
-    parts, states, dwo = take(count), take(count), take(1 if count else 0)
-    grad_ref, gains_ref, out_ref = take(3)
+    loaded, gain_ref, gain_two, parts_in = take(10), *take(3)
+    states, dwo = take(count), take(1 if count else 0)
+    grad_ref, gain_one_ref, gain_two_ref, out_ref = take(4)
     fulls = take(count + 3 if count else 0)
     dw_out = take(0 if count else 2)
     inputs = take(10)
@@ -915,7 +986,7 @@
     own, width = tokens.shape
     rows = own // CHUNKS
     sems = (send_sem, recv_sem)
-    gain = gains.at[0:1]
+    gain = as_row(gain_ref)
     fetch = [pltpu.make_async_copy(source, target, in_sem.at[i]) for i, (source, target) in enumerate(zip(loaded, inputs))]
 
     def at(base, k):
@@ -932,17 +1003,15 @@
     out_from_side = [send(parts_in.at[:, 3 - 2 * k], out_side.at[k], sems, (3, k), 1) for k in range(2)]
     out_from_across = send(out_mine.at[0], out_across, sems, (3, 2), 2)
 
-    reduces, late, early_spreads, late_spreads = [], [], [], []
+    late, early_spreads, late_spreads = [], [], []
     if count:
-        for a in range(count):
-            land, mine, *own_sems = take(5)
-            reduces.append(Reduce(parts[a], states[a], slots(land), slots(mine), IN_BACK, RING - 1, *own_sems))
         land, mine, *own_sems = take(5)
         late.append(Reduce(dwo[0], None, slots(land), slots(mine), 0, RING - 1, *own_sems))
         for part in (dwq, dwkv):
             land, *own_sems = take(3)
             late.append(Reduce(part, None, slots(land), None, 0, RING - 1, *own_sems))
-        spreads = [Spread(r, full, *take(3)) for r, full in zip([*reduces, *late], fulls)]
+        reduced = [Reduced(state) for state in states]
+        spreads = [Spread(r, full, *take(3)) for r, full in zip([*reduced, *late], fulls)]
         early_spreads, late_spreads = spreads[:count], spreads[count:]
 
     for copy in fetch:
@@ -951,10 +1020,9 @@
         dp = lax.axis_index("dp")
         flip = lambda bit: {"dp": dp + bit - 2 * bit * lax.rem(lax.div(dp, bit), 2)}
         meet(partner(1), partner(2), ring_peer(0), ring_peer(1), flip(1), flip(2), flip(4))
-        for ring in (*reduces, late[0]):
+        for ring in (late[0], *early_spreads):
             ring.start()
-        for ring in (*reduces, late[0]):
-            ring.prefetch()
+        late[0].prefetch()
     else:
         meet(partner(1), partner(2))
     for copy in fetch[:6]:
@@ -976,32 +1044,35 @@
         terms[at(2 * own, k)] = (mine + cr[0, at(0, k)].astype(f32)).astype(bf16)
         across(k).start()
 
-    for ring, following in zip(reduces, early_spreads):
-        ring.step(0)
-        following.start()
+    if count:
+        late[0].step(0)
+        early_spreads[0].step(0)
+        early_spreads[1].step(0)
 
     chunk = dwq.shape[2]
     tall = 4 * chunk
     fetch[6].wait()
-    merge_q, merge_kv = spread(dwq.shape[3] // HEAD_SIZE), spread(dwkv.shape[3] // HEAD_SIZE)
+    merge_q, merge_k = spread(dwq.shape[3] // HEAD_SIZE), spread(dwkv.shape[1] * dwkv.shape[2] // HEAD_SIZE)
 
     @pl.loop(0, width // tall)
     def _(k):
         part = attn_in[:, pl.ds(pl.multiple_of(k * tall, LANES), tall)]
-        block_q = dot(dot(part, dq[...], TN).astype(bf16), merge_q, NT).astype(bf16)
-        padded = jnp.concatenate([dot(part, d[...], TN).astype(bf16) for d in (dk, dv)], axis=1)
-        block_kv = dot(padded, merge_kv, NT).astype(bf16)
+        block = dot(dot(part, dq[...], TN).astype(bf16), merge_q, NT).astype(bf16)
         for i in range(4):
             number = k * 4 + i
-            here = (lax.div(number, RING), lax.rem(number, RING))
-            dwq[here] = block_q[i * chunk : (i + 1) * chunk]
-            dwkv[here] = block_kv[i * chunk : (i + 1) * chunk]
+            dwq[lax.div(number, RING), lax.rem(number, RING)] = block[i * chunk : (i + 1) * chunk]
+
+    short = dwkv.shape[2]
+    for half, grads in enumerate((dk, dv)):
+        block = dot(merge_k, dot(grads[...], attn_in[...], TN).astype(bf16)).astype(bf16)
+        for i in range(RING):
+            dwkv[half, i] = block[i * short : (i + 1) * short]
 
     if count:
-        late[0].step(0)
         for ring in late[1:]:
             ring.start()
         late[0].step(1)
+        early_spreads[2].step(0)
     else:
         stored = [pltpu.make_async_copy(s, t, load_sem.at[2 + i]) for i, (s, t) in enumerate(zip((dwq, dwkv), dw_out))]
         for copy in stored:
@@ -1034,8 +1105,6 @@
             else:
                 late_spreads[a].step(turn - (RING - 1))
 
-    early((0,), 0)
-
     @pl.loop(0, CHUNKS)
     def _(k):
         terms[at(own, k)] = term(1, k).astype(bf16)
@@ -1043,7 +1112,6 @@
         grad_ref[at(0, k)] = term(0, k)
 
     onward(0)
-    early((1, 2), 0)
     onward(1)
 
     def tokens_back():
@@ -1058,7 +1126,7 @@
             across(k).wait_recv()
             here = at(0, k)
             grad = grad_ref[here] + cr[1, here].astype(f32) + xr[here].astype(f32)
-            back, sums = rows_back(grad, tokens[here].astype(f32), gain[...])
+            back, sums = rows_back(grad, tokens[here].astype(f32), gain)
             grad_ref[here] = grad_one[here] + back
             gain_sum[0:1] += jnp.sum(sums, axis=0, keepdims=True)
 
@@ -1115,9 +1183,11 @@
             onward(2 * turn + 1)
     if count:
         gain_add(4)
-    for ring in (*reduces, *late, *early_spreads, *late_spreads):
+    for ring in (*late, *early_spreads, *late_spreads):
         ring.finish()
-    gains_ref[...] = gain_sum[...]
+    for row, ref in enumerate((gain_one_ref, gain_two_ref)):
+        for i in range(ref.shape[0]):
+            ref[i : i + 1, :] = gain_sum[row : row + 1, i * LANES : (i + 1) * LANES]
 
     @pl.loop(0, CHUNKS)
     def _(k):
@@ -1130,18 +1200,16 @@
     out_from_across.wait_send()
 
 
-def end(dq, dk, dv, wq, wk, wv, attn_in, tokens, grad_one, hid1, gains, gain_two, parts_in, parts, states, dwo, cuts):
+def end(dq, dk, dv, wq, wk, wv, attn_in, tokens, grad_one, hid1, gain, gain_two, parts_in, states, dwo, heads):
     own, width = tokens.shape
-    count = len(parts)
+    count = len(states)
     sds = jax.ShapeDtypeStruct
     pieces = hid1.shape
     loaded = (dq, dk, dv, wq, wk, wv, attn_in, tokens, grad_one, hid1)
-    qkv_shapes = [(2, RING, width // (2 * RING), c) for c in cuts]
+    qkv_shapes = [(2, RING, width // (2 * RING), heads), (2, RING, heads // (2 * RING), width)]
     late = [dwo] if count else []
-    ring_shapes = [*[p.shape for p in parts], dwo.shape, *qkv_shapes] if count else qkv_shapes
+    ring_shapes = [*[(2, RING, *t.shape[1:]) for t in states], dwo.shape, *qkv_shapes] if count else qkv_shapes
     ring_buffers = []
-    for p in parts:
-        ring_buffers += ring_scratch(p.shape, RING - 1 - IN_BACK, True)
     if count:
         ring_buffers += ring_scratch(dwo.shape, RING - 1, True)
         for shape in qkv_shapes:
@@ -1151,11 +1219,12 @@
     stages = 5 if count else 2
     outs = pl.pallas_call(
         functools.partial(end_kernel, count),
-        in_specs=[ANY] * 10 + [VMEM] * 2 + [ANY] * (1 + 2 * count + len(late)),
-        out_specs=[VMEM] * 3 + [ANY] * len(ring_shapes),
+        in_specs=[ANY] * 10 + [VMEM] * 2 + [ANY] * (1 + count + len(late)),
+        out_specs=[VMEM] * 4 + [ANY] * len(ring_shapes),
         out_shape=[
             sds((own, width), f32),
-            sds((8, width), f32),
+            sds(gain.shape, f32),
+            sds(gain.shape, f32),
             sds(pieces, bf16),
             *[sds(shape, bf16) for shape in ring_shapes],
         ],
@@ -1179,8 +1248,8 @@
         compiler_params=comm_params(3),
         cost_estimate=cost(150e-6 * 1e15, 60e6),
         name="end",
-    )(*loaded, gains, gain_two, parts_in, *parts, *states, *late)
-    return outs[:3], outs[3:]
+    )(*loaded, gain, gain_two, parts_in, *states, *late)
+    return outs[:4], outs[4:]
 
 
 def body(
@@ -1191,37 +1260,36 @@
     own, width = tokens.shape
     blocks = 4
     heads_q, heads_k = w_query.shape[1], key_weight.shape[1]
-    gains = jnp.stack([norm_attn, norm_mlp])
+    rows_of = lambda t: t.reshape(-1, LANES)
+    gain_attn, gain_mlp = rows_of(norm_attn), rows_of(norm_mlp)
 
     qkv, attn_in, attended, lse, cots, wq, wk, wv, wo, cos, sin, start = front(
-        tokens, gains, w_query, key_weight, value_weight, w_out, segments.reshape(1, seq), positions.reshape(seq, 1),
+        tokens, gain_attn, w_query, key_weight.T, value_weight.T, w_out, rows_of(segments), rows_of(positions),
         cotangent, blocks,
     )
     ringed = lax.axis_size("dp") == RING
     hid1, grad_attended, parts, grad_one, dwd, dwg, dwu, dwo, gain_two, *states = middle(
-        attended, wo, tokens, gains, cotangent, cots, w_gate, w_up, w_down, ringed
+        attended, wo, tokens, gain_mlp, cotangent, cots, w_gate, w_up, w_down, ringed
     )
     grad_attended = grad_attended.reshape(seq, -1)
-    dwo = dot(spread(heads_q // HEAD_SIZE), dwo).astype(bf16)
     chunks = lambda t: t.reshape(2, RING, t.shape[0] // (2 * RING), t.shape[1])
     early = [chunks(t) for t in (dwd, dwg, dwu)] if ringed else []
     (dq, dk, dv), states = attend_back(
         qkv, attended, grad_attended, lse, start, cos, sin, early, states, blocks
     )
-    (grad_tokens, gain_grads, output), sums = end(
-        dq, dk, dv, wq, wk, wv, attn_in.reshape(seq, width), tokens, grad_one.reshape(own, width), hid1, gains,
-        gain_two, parts, early, states, chunks(dwo) if ringed else None, (heads_q, 2 * heads_k),
+    (grad_tokens, gain_one, gain_two, output), sums = end(
+        dq, dk, dv, wq, wk, wv, attn_in.reshape(seq, width), tokens, grad_one.reshape(own, width), hid1, gain_attn,
+        gain_two, parts, states, chunks(dwo) if ringed else None, heads_q,
     )
-    output = output.reshape(own, width)
     if not ringed:
-        gain_grads = lax.psum(gain_grads, "dp")
+        gain_one, gain_two = lax.psum((gain_one, gain_two), "dp")
         sums = [lax.psum(t, "dp") for t in (dwd, dwg, dwu, dwo, *sums)]
     down, gate, up, out, query, both = [t.reshape(-1, t.shape[-1]) for t in sums]
-    key, value = both[:, :heads_k], both[:, heads_k:]
+    key, value = both[:heads_k].astype(f32).T, both[heads_k:].astype(f32).T
+    query, out, gate, up, down = [t.astype(f32) for t in (query, out, gate, up, down)]
     return (
-        output, grad_tokens, gain_grads[0],
-        *[t.astype(f32) for t in (query, key, value, out)],
-        gain_grads[1], *[t.astype(f32) for t in (gate, up, down)],
+        output.reshape(own, width), grad_tokens, gain_one.reshape(width), query, key, value, out,
+        gain_two.reshape(width), gate, up, down,
     )
 
 

time: 519 us -> 491 us (0.946)
  Pallas kernels: 471 us -> 459 us
  local copies, waits for them, and re-layouts: 16.7 us -> 7.4 us
    pallas_call x1, Pallas kernels: 181 us -> 167 us  [end(): pl.pallas_call(functools.partial(end_kernel, count), in_specs=[ANY] * 10...]
    convert_element_type x6 -> x4, other arithmetic: 16.6 us -> 14.3 us  [body(): t.astype(f32)]
where the time goes in v5:
time: 491 us; the launch traced here: 483 us
  Pallas kernels  459 us (93%)
  other arithmetic  16 us (3%)
  local copies, waits for them, and re-layouts  7.4 us (2%)
    pallas_call x1, Pallas kernels, middle(): pl.pallas_call(functools.partial(middle_kernel, ringed), in_specs=[VMEM]...  168 us
    pallas_call x1, Pallas kernels, end(): pl.pallas_call(functools.partial(end_kernel, count), in_specs=[ANY] * 10...  167 us
    pallas_call x1, Pallas kernels, front(): pl.pallas_call(functools.partial(front_kernel, blocks=blocks), in_specs=[...  75.9 us
    pallas_call x1, Pallas kernels, attend_back(): pl.pallas_call(functools.partial(attend_back_kernel, count, blocks=blocks...  48 us
    convert_element_type x4, other arithmetic, body(): t.astype(f32)  14.3 us

profile of v5, /device:TPU:24, one launch (start us, length us, event | category | flops | bytes accessed | tf_op | source)
XLA Modules:
  0.0 483.2 jit_solution(6672471184175304438)
XLA Ops:
  0.6 75.9 %front.1 = (bf16[2048,1024]{1,0:T(8,128)(2,1)}, bf16[4,512,1536]{2,1,0:T(8,128)(2,1)}, bf16[2048,512]{1,0:T(8,128)(2,1)}, f32[2,2,2048]{2,1,0:T(2,128)}, bf16[3,...) custom-call(bf16[512,1536]{1,0:T(8,128)(2,1)} %refs_7_.1, ...), custom_call_target="tpu_custom_call" | custom-call | flops 80000000000 | bytes 40000000 | tf_op jit(solution)/shard_map/front/pallas_call | solution.py:412
  76.6 168.0 %middle.1 = (f32[4,128,1536]{2,1,0:T(8,128)}, bf16[4,4,128,512]{3,2,1,0:T(8,128)(2,1)}, bf16[4,4,128,1536]{3,2,1,0:T(8,128)(2,1)}, f32[4,128,1536]{2,1,0:T(8,128...) custom-call(bf16[4,4,128,512]{3,2,1,0:T(8,128)(2,1)} %bitcast.62, ...), custom_call_target="tpu_custom_call" | custom-call | flops 149999992832 | bytes 80000000 | tf_op jit(solution)/shard_map/middle/pallas_call | solution.py:926
  244.6 48.0 %attention_back.1 = (bf16[2048,512]{1,0:T(8,128)(2,1)}, bf16[2048,256]{1,0:T(8,128)(2,1)}, bf16[2048,256]{1,0:T(8,128)(2,1)}, bf16[2,64,1536]{2,1,0:T(8,128)(2,1...) custom-call(bf16[2048,1024]{1,0:T(8,128)(2,1)} %get-tuple-element.51.refs_0_.refs_1_.refs_2_, ...), custom_call_target="tpu_custom_call" | custom-call | flops 21474836480 | bytes 20971520 | tf_op jit(solution)/shard_map/attention_back/pallas_call | solution.py:550
  292.5 166.9 %end.1 = (f32[512,1536]{1,0:T(8,128)}, f32[12,128]{1,0:T(8,128)}, f32[12,128]{1,0:T(8,128)}, bf16[4,128,1536]{2,1,0:T(8,128)(2,1)}, bf16[2,8,64,1536]{3,2,1,0:T(...) custom-call(bf16[2048,512]{1,0:T(8,128)(2,1)} %get-tuple-element.66., ...), custom_call_target="tpu_custom_call" | custom-call | flops 149999992832 | bytes 60000000 | tf_op jit(solution)/shard_map/end/pallas_call | solution.py:1220
  459.5 0.0 copy-start.6
  459.5 1.4 fusion
  460.9 0.0 copy-start.5
  460.9 1.8 convert_bitcast_fusion
  462.7 0.0 copy-done.6
  462.7 1.7 bitcast_convert_fusion.4
  464.4 0.0 copy-done.5
  464.4 1.8 bitcast_convert_fusion.3
  466.2 0.0 copy-done.3
  466.2 4.1 bitcast_convert_fusion
  470.3 0.0 copy-done
  470.3 0.6 copy-done.1
  470.9 6.7 %bitcast_convert_fusion.1 = (f32[1536,1024]{1,0:T(8,128)}, f32[1536,1024]{1,0:T(8,128)}) fusion(bf16[2,8,96,1024]{3,2,1,0:T(8,128)(2,1)S(1)} %copy-done.1, bf16[2,8,96,1024]{3,2,1,0:T(8,128)(2,1)S(1)} %copy-done), kind=kLoop, calls=%fused_computation.1 | loop fusion | flops 3145728 | bytes 18874368 | tf_op jit(solution)/shard_map/convert_element_type | solution.py:1289
  477.6 0.0 copy-done.4
  477.6 1.1 copy.28
  478.8 1.3 copy-done.2
  480.1 1.7 copy.29
  481.8 0.0 copy-done.8
  481.8 0.6 copy.30
  482.4 0.6 copy.31
  (8 shorter events, 0.0 us)
Async XLA Ops:
  459.5 3.2 copy-start.6
  460.9 3.5 copy-start.5
  462.7 3.5 copy-start.3
  466.2 4.1 copy-start
  466.2 4.7 copy-start.1
  470.9 6.7 %copy-start.4 = (bf16[4,128,1536]{2,1,0:T(8,128)(2,1)S(1)}, bf16[4,128,1536]{2,1,0:T(8,128)(2,1)}, u32[]{:S(2)}) copy-start(bf16[4,128,1536]{2,1,0:T(8,128)(2,1)} %get-tuple-element.81) | copy-start | bytes 4718596
  477.6 2.5 copy-start.2
  480.1 1.7 copy-start.8
  480.1 2.3 copy-start.7
